TPU v7x, 256 devices: a whole 4x4x8 slice. The times are simulated.
256 devices in a mesh: tm: 32 (over y, x, core), sr: 8 (over z).
Axes of the slice: x: 4, y: 4, z: 8, core: 2. Of those that a mesh axis runs over, the one named last changes fastest.
Arguments:
- observations: bfloat16 [4096, 65536], P(None, ('sr', 'tm')), may hold values from -6 to 6
- loadings: float32 [65536, 128], P(('sr', 'tm')), may hold values from -0.00036621094 to 0.00036621094
- noise_precision: float32 [65536], P(('sr', 'tm')), may hold values from 0.5 to 4
- transition: float32 [128, 128], replicated, may hold values from -1 to 1, as said below
- filter_cov: float32 [128, 128], replicated, may hold values from -1 to 1, as said below
- smoother_gain: float32 [128, 128], replicated, may hold values from -1 to 1, as said below
- smoothed_cov: float32 [128, 128], replicated, may hold values from -1 to 1, as said below
Outputs:
- smoothed_factors: float32 [4096, 128], P('tm')
- new_loadings: float32 [65536, 128], P(('sr', 'tm'))
- new_transition: float32 [128, 128], replicated
Inputs may be any that keep to these rules, and one draw needn't show every extreme that they name: `transition`: the spectral radius is below one. `filter_cov`: symmetric positive definite. `smoother_gain`: the spectral radius is below one. `smoothed_cov`: symmetric positive definite.
All inputs are finite; a program needn't handle non-finite values.
Results may differ from a plain program's by a relative error of at most 0.00175.
The roundings to bfloat16 on the way count: a program that leaves them out, or rounds other values in their place, can miss the bound.
Values may be sent and summed in bfloat16 or wider, within the bound.
No kernel may reach another device: no remote copies, remote signals or barrier semaphores. Data moves between devices by JAX's collectives and lax.ppermute only.
A program may use at most 64 MiB of HBM per device.

v0:
```python
import jax
import jax.numpy as jnp
from jax import lax
from jax.sharding import Mesh
from jax.sharding import PartitionSpec as P

TM = ("tm_0", "tm_1", "tm_2")
SR_TM = ("sr", "tm_0", "tm_1", "tm_2")


precise = lax.Precision.HIGHEST


def split_up(array, dim, size):
    dims = array.shape
    pieces = array.reshape(*dims[:dim], size, dims[dim] // size, *dims[dim + 1 :])
    return jnp.moveaxis(pieces, dim, 0)


def sent_and_summed(array, axis, dim):
    pieces = split_up(array, dim, lax.axis_size(axis))
    arrived = lax.all_to_all(pieces, axis, split_axis=0, concat_axis=0, tiled=True)
    return arrived.sum(axis=0)


def sent_to_all(array, axis):
    copies = jnp.broadcast_to(array, (lax.axis_size(axis), *array.shape))
    return lax.all_to_all(copies, axis, split_axis=0, concat_axis=0, tiled=True)


def of_everyone(array, axis):
    return sent_to_all(array, axis).sum(axis=0)


def over_axes(array, axes):
    far, near = axes
    nearer = of_everyone(array, near)
    return of_everyone(nearer, far)


def filled_with(array, identity):
    return jax.tree.map(
        lambda a, e: jnp.broadcast_to(jnp.asarray(e, a.dtype), a.shape), array, identity
    )


def collected_together(array, axis):
    leaves = jax.tree.leaves(array)
    sequence = sorted(range(len(leaves)), key=lambda k: -leaves[k].size)
    width = (1, *leaves[sequence[0]].shape)[-1]
    lines = [
        jnp.pad(leaves[k].reshape(-1), (0, -leaves[k].size % width)).reshape(-1, width)
        for k in sequence
    ]
    both, at, found = (lax.all_gather(jnp.concatenate(lines), axis), 0, {})
    for k, line in zip(sequence, lines):
        section = both[:, at : at + len(line)].reshape(len(both), -1)
        found[k] = section[:, : leaves[k].size].reshape(-1, *leaves[k].shape)
        at += len(line)
    numbers = iter(range(len(leaves)))
    return jax.tree.map(lambda _: found[next(numbers)], array)


def entering_2(array, axes, combine, identity, reverse):
    before = start = filled_with(array, identity)
    running = array
    for axis in reversed(axes):
        size, here = (lax.axis_size(axis), lax.axis_index(axis))
        pieces = collected_together(running, axis)
        inside, running = (start, start)
        for k in reversed(range(size)) if reverse else range(size):
            passed = k > here if reverse else k < here
            running = combine(running, jax.tree.map(lambda part: part[k], pieces))
            inside = jax.tree.map(lambda new, old: jnp.where(passed, new, old), running, inside)
        before = combine(inside, before)
    return before


def shifted(value, axis, steps):
    count = lax.axis_size(axis)
    leading, last = (max(0, -steps), min(count, count - steps))
    return lax.ppermute(value, axis, [(source, source + steps) for source in range(leading, last)])


def padded_to(lines, size):
    spare = -len(lines) % size
    return jnp.pad(lines, [(0, spare)] + [(0, 0)] * (lines.ndim - 1))


def laid_out(pieces, dim):
    dims = list(pieces.shape[1:])
    dims[dim] *= pieces.shape[0]
    return jnp.moveaxis(pieces, 0, dim).reshape(dims)


def gather_directly(array, axis, dim):
    pieces = sent_to_all(array, axis)
    return laid_out(pieces, dim)


def total_of(array, axes):
    own = sent_and_summed(padded_to(array, lax.axis_size(axes)), axes, 0)
    whole = gather_directly(own, axes, 0)
    return whole[: len(array)].reshape(array.shape)


def in_one(arrays, axis):
    ends = [0]
    for a in arrays:
        ends.append(ends[-1] + a.size)
    running = total_of(jnp.concatenate([a.ravel() for a in arrays]), axis)
    return tuple((running[b:e].reshape(a.shape) for a, b, e in zip(arrays, ends, ends[1:])))


def dot_high(left, right):
    return jnp.dot(left, right, precision=precise, preferred_element_type=jnp.float32)


def matrix_power(matrix, exponent):
    result = jnp.eye(matrix.shape[0], dtype=jnp.float32)
    square = matrix
    remain = exponent
    while remain > 0:
        if remain % 2 == 1:
            result = dot_high(result, square)
        remain = remain // 2
        if remain > 0:
            square = dot_high(square, square)
    return result


def block_prefix(inputs, matrix):
    length = inputs.shape[0]
    width = inputs.shape[1]
    totals = inputs
    raised = matrix
    offset = 1
    while offset < length:
        moved = jnp.concatenate(
            [jnp.zeros((offset, width), jnp.float32), totals[: length - offset]], axis=0
        )
        totals = totals + dot_high(moved, raised.T)
        offset = offset * 2
        if offset < length:
            raised = dot_high(raised, raised)
    return totals


def propagate(start, matrix, length):
    carried = dot_high(matrix, start)[None, :]
    raised = matrix
    while carried.shape[0] < length:
        carried = jnp.concatenate([carried, dot_high(carried, raised.T)], axis=0)
        raised = dot_high(raised, raised)
    return carried


def compose(earlier, later):
    return (dot_high(later[0], earlier[0]), dot_high(later[0], earlier[1]) + later[1])


def local(
    observations, loadings, noise_precision, transition, filter_cov, smoother_gain, smoothed_cov
):
    blocks = lax.axis_size(TM)
    position = lax.axis_index(TM)
    width = transition.shape[0]
    steps_dev = observations.shape[0] // blocks
    scaled = (noise_precision[:, None] * loadings).astype(jnp.bfloat16)
    window = observations
    partial_value = sent_and_summed(
        jnp.dot(window, scaled, preferred_element_type=jnp.float32), TM, 0
    )
    info_part = dot_high(loadings.T, noise_precision[:, None] * loadings)
    proj = of_everyone(partial_value, "sr")
    info = over_axes(info_part, (("tm_0", "tm_1"), ("tm_2", "sr")))
    closed = transition - dot_high(filter_cov, dot_high(info, transition))
    inputs = dot_high(proj, filter_cov.T)
    local_filter = block_prefix(inputs, closed)
    whole_filter = matrix_power(closed, steps_dev)
    identity_pair = (jnp.eye(width, dtype=jnp.float32), jnp.zeros((width,), jnp.float32))
    entering = entering_2(
        (whole_filter, local_filter[steps_dev - 1]), TM, compose, identity_pair, False
    )[1]
    filtered = local_filter + propagate(entering, closed, steps_dev)
    coupled = dot_high(smoother_gain, transition)
    global_rows = position * steps_dev + jnp.arange(steps_dev, dtype=jnp.int32)
    final_row = (global_rows == steps_dev * blocks - 1)[:, None]
    back = jnp.where(final_row, filtered, filtered - dot_high(filtered, coupled.T))
    local_smooth = block_prefix(back[::-1], smoother_gain)[::-1]
    whole_smooth = matrix_power(smoother_gain, steps_dev)
    arriving = entering_2((whole_smooth, local_smooth[0]), TM, compose, identity_pair, True)[1]
    smoothed = local_smooth + propagate(arriving, smoother_gain, steps_dev)[::-1]
    factors_b = smoothed.astype(jnp.bfloat16)
    prior_row = shifted(smoothed[steps_dev - 1 :], TM, 1)
    lag_rows = jnp.concatenate([prior_row, smoothed[: steps_dev - 1]], axis=0)
    kept_rows = jnp.where(final_row, 0.0, smoothed)
    total_part = dot_high(smoothed.T, smoothed)
    previous_part = dot_high(kept_rows.T, kept_rows)
    lagged_part = dot_high(smoothed.T, lag_rows)
    total, previous, lagged = in_one((total_part, previous_part, lagged_part), TM)
    length = steps_dev * blocks
    total = total + length * smoothed_cov
    previous = previous + (length - 1) * smoothed_cov
    lagged = lagged + (length - 1) * dot_high(smoothed_cov, smoother_gain.T)
    window = observations
    cross = jnp.einsum(
        "ts,tk->sk", window, gather_directly(factors_b, TM, 0), preferred_element_type=jnp.float32
    )
    total_factor = jnp.linalg.cholesky(total)
    new_loadings = jax.scipy.linalg.cho_solve((total_factor, True), cross.T).T
    previous_factor = jnp.linalg.cholesky(previous)
    new_transition = jax.scipy.linalg.cho_solve((previous_factor, True), lagged.T).T
    return (smoothed, new_loadings, new_transition)


def solution(mesh):
    split = Mesh(mesh.devices.reshape(4, 4, 2, mesh.shape["sr"]), ("tm_0", "tm_1", "tm_2", "sr"))
    in_specs = (P(None, SR_TM), P(SR_TM, None), P(SR_TM), P(), P(), P(), P())
    out_specs = (P(TM, None), P(SR_TM, None), P())
    return jax.shard_map(local, mesh=split, in_specs=in_specs, out_specs=out_specs, check_vma=False)
```

profile of v0, /device:TPU:1, one launch (start us, length us, event | category | flops | bytes accessed | tf_op | source)
XLA Modules:
  0.0 289.5 jit_solution(1998098044097584090)
XLA Ops:
  0.7 1.6 convolution_bitcast_fusion.5
  3.4 10.0 %all-to-all-start.2 = ((f32[16,128,128]{2,1,0:T(8,128)}), f32[16,128,128]{2,1,0:T(8,128)S(1)}, u32[]{:S(2)}, u32[]{:S(2)}) async-start(f32[16,128,128]{2,1,0:T(8,128)} %broadcast_in_dim.48), calls=%async_computation.2 | async-start | bytes 2097152 | tf_op jit(solution)/shard_map/all_to_all | solution.py:28
  14.4 1.6 copy.73
  15.9 24.1 %all-to-all-done.2 = f32[16,128,128]{2,1,0:T(8,128)S(1)} async-done(((f32[16,128,128]{2,1,0:T(8,128)}), f32[16,128,128]{2,1,0:T(8,128)S(1)}, u32[]{:S(2)}, u32[]{:S(2)}) %all-to-all-start.2) | async-done | bytes 1048608 | tf_op jit(solution)/shard_map/all_to_all | solution.py:28
  40.1 7.4 %all-to-all-start = ((f32[32,128,128]{1,2,0:T(8,128)}), f32[32,128,128]{1,2,0:T(8,128)}, u32[]{:S(2)}, u32[]{:S(2)}) async-start(f32[32,128,128]{1,2,0:T(8,128)} %bitcast.507), calls=%async_computation | async-start | bytes 4194304 | tf_op jit(solution)/shard_map/all_to_all | solution.py:22
  47.7 27.6 %all-to-all-done = f32[32,128,128]{1,2,0:T(8,128)} async-done(((f32[32,128,128]{1,2,0:T(8,128)}), f32[32,128,128]{1,2,0:T(8,128)}, u32[]{:S(2)}, u32[]{:S(2)}) %all-to-all-start) | async-done | bytes 2097184 | tf_op jit(solution)/shard_map/all_to_all | solution.py:22
  76.4 4.7 %all-to-all-start.3 = ((f32[16,128,128]{2,1,0:T(8,128)}), f32[16,128,128]{2,1,0:T(8,128)S(1)}, u32[]{:S(2)}, u32[]{:S(2)}) async-start(f32[16,128,128]{2,1,0:T(8,128)} %broadcast_in_dim.49), calls=%async_computation.3 | async-start | bytes 2097152 | tf_op jit(solution)/shard_map/all_to_all | solution.py:28
  82.7 2.3 reduce_sum.45
  85.0 1.6 copy.53
  86.6 10.3 %all-to-all-done.3 = f32[16,128,128]{2,1,0:T(8,128)S(1)} async-done(((f32[16,128,128]{2,1,0:T(8,128)}), f32[16,128,128]{2,1,0:T(8,128)S(1)}, u32[]{:S(2)}, u32[]{:S(2)}) %all-to-all-start.3) | async-done | bytes 1048608 | tf_op jit(solution)/shard_map/all_to_all | solution.py:28
  96.9 1.7 broadcast_in_dim.47
  98.5 4.4 %all-to-all-start.1 = ((f32[8,128,128]{2,1,0:T(8,128)}), f32[8,128,128]{2,1,0:T(8,128)}, u32[]{:S(2)}, u32[]{:S(2)}) async-start(f32[8,128,128]{2,1,0:T(8,128)} %broadcast_in_dim.47), calls=%async_computation.1 | async-start | bytes 1048576 | tf_op jit(solution)/shard_map/all_to_all | solution.py:28
  103.0 1.6 copy.55
  105.6 1.7 fusion.230
  109.0 8.3 %all-to-all-done.1 = f32[8,128,128]{2,1,0:T(8,128)} async-done(((f32[8,128,128]{2,1,0:T(8,128)}), f32[8,128,128]{2,1,0:T(8,128)}, u32[]{:S(2)}, u32[]{:S(2)}) %all-to-all-start.1) | async-done | bytes 524320 | tf_op jit(solution)/shard_map/all_to_all | solution.py:28
  124.9 5.8 %all-gather.6 = f32[2,129,128]{2,1,0:T(8,128)S(1)} all-gather(f32[1,129,128]{2,1,0:T(8,128)S(1)} %maximum_bitcast_fusion), channel_id=2, replica_groups=mesh['tm_0'=4,'tm_1'=4,'tm_2'=2,'sr'=8] {'tm_2'}, dimensions={0}, use_global_device_ids=true | all-gather | bytes 198144 | tf_op jit(solution)/shard_map/all_gather | solution.py:55
  131.5 9.4 %all-gather.7 = f32[4,129,128]{2,1,0:T(8,128)S(1)} all-gather(f32[1,129,128]{2,1,0:T(8,128)S(1)} %maximum_bitcast_fusion.1), channel_id=3, replica_groups=mesh['tm_0'=4,'tm_1'=4,'tm_2'=2,'sr'=8] {'tm_1'}, dimensions={0}, use_global_device_ids=true | all-gather | bytes 330240 | tf_op jit(solution)/shard_map/all_gather | solution.py:55
  143.3 9.4 %all-gather.8 = f32[4,129,128]{2,1,0:T(8,128)S(1)} all-gather(f32[1,129,128]{2,1,0:T(8,128)S(1)} %maximum_bitcast_fusion.2), channel_id=4, replica_groups=mesh['tm_0'=4,'tm_1'=4,'tm_2'=2,'sr'=8] {'tm_0'}, dimensions={0}, use_global_device_ids=true | all-gather | bytes 330240 | tf_op jit(solution)/shard_map/all_gather | solution.py:55
  155.9 1.2 fusion
  159.1 7.7 %all-gather.9 = f32[2,129,128]{2,1,0:T(8,128)S(1)} all-gather(f32[1,129,128]{2,1,0:T(8,128)S(1)} %maximum_bitcast_fusion.3), channel_id=5, replica_groups=mesh['tm_0'=4,'tm_1'=4,'tm_2'=2,'sr'=8] {'tm_2'}, dimensions={0}, use_global_device_ids=true | all-gather | bytes 198144 | tf_op jit(solution)/shard_map/all_gather | solution.py:55
  167.6 9.4 %all-gather.10 = f32[4,129,128]{2,1,0:T(8,128)S(1)} all-gather(f32[1,129,128]{2,1,0:T(8,128)S(1)} %maximum_bitcast_fusion.4), channel_id=6, replica_groups=mesh['tm_0'=4,'tm_1'=4,'tm_2'=2,'sr'=8] {'tm_1'}, dimensions={0}, use_global_device_ids=true | all-gather | bytes 330240 | tf_op jit(solution)/shard_map/all_gather | solution.py:55
  179.4 9.7 %all-gather.11 = f32[4,129,128]{2,1,0:T(8,128)S(1)} all-gather(f32[1,129,128]{2,1,0:T(8,128)S(1)} %maximum_bitcast_fusion.5), channel_id=7, replica_groups=mesh['tm_0'=4,'tm_1'=4,'tm_2'=2,'sr'=8] {'tm_0'}, dimensions={0}, use_global_device_ids=true | all-gather | bytes 330240 | tf_op jit(solution)/shard_map/all_gather | solution.py:55
  192.7 7.9 %collective-permute-start = (f32[1,128]{1,0:T(1,128)S(1)}, f32[1,128]{1,0:T(1,128)S(1)}, u32[]{:S(2)}, u32[]{:S(2)}) collective-permute-start(f32[1,128]{1,0:T(1,128)S(1)} %slice.411), channel_id=1, source_target_pairs={{0,8},{8,16},{16,24},{24,32},{32,40},{40,48},{48,56},{56,64},{64,7... | collective-permute-start | bytes 1544 | tf_op jit(solution)/shard_map/ppermute | solution.py:82
  201.6 15.6 %all_to_all.40 = f32[32,1,1536]{2,1,0:T(1,128)S(1)} all-to-all(f32[32,1,1536]{2,1,0:T(1,128)S(1)} %bitcast.511), channel_id=1, replica_groups=mesh['tm_0'=4,'tm_1'=4,'tm_2'=2,'sr'=8] {'tm_0','tm_1','tm_2'}, dimensions={0} | all-to-all | bytes 393216 | tf_op jit(solution)/shard_map/all_to_all | solution.py:22
  218.1 3.8 %all-to-all-start.5 = ((f32[32,1,1536]{2,1,0:T(1,128)}), f32[32,1,1536]{2,1,0:T(1,128)S(1)}, u32[]{:S(2)}, u32[]{:S(2)}) async-start(f32[32,1,1536]{2,1,0:T(1,128)} %broadcast_in_dim.54), calls=%async_computation.5 | async-start | bytes 393216 | tf_op jit(solution)/shard_map/all_to_all | solution.py:28
  222.0 8.2 %all-to-all-done.5 = f32[32,1,1536]{2,1,0:T(1,128)S(1)} async-done(((f32[32,1,1536]{2,1,0:T(1,128)}), f32[32,1,1536]{2,1,0:T(1,128)S(1)}, u32[]{:S(2)}, u32[]{:S(2)}) %all-to-all-start.5) | async-done | bytes 196640 | tf_op jit(solution)/shard_map/all_to_all | solution.py:28
  230.2 1.2 broadcast_in_dim.55
  231.4 3.8 %all-to-all-start.6 = ((bf16[32,128,128]{2,1,0:T(8,128)(2,1)}), bf16[32,128,128]{2,1,0:T(8,128)(2,1)S(1)}, u32[]{:S(2)}, u32[]{:S(2)}) async-start(bf16[32,128,128]{2,1,0:T(8,128)(2,1)} %broadcast_in_dim.55), calls=%async_computation.6 | async-start | bytes 2097152 | tf_op jit(solution)/shard_map/all_to_all | solution.py:28
  237.8 12.5 %cholesky.55 = f32[128,128]{1,0:T(8,128)S(1)} custom-call(f32[128,128]{1,0:T(8,128)} %get-tuple-element.11), custom_call_target="Cholesky" | custom-call | tf_op jit(solution)/shard_map/jit(cholesky)/cholesky | solution.py:212
  251.7 9.8 %custom-call.17 = f32[1,128,128]{1,2,0:T(8,128)S(1)} custom-call(f32[1,128,128]{2,1,0:T(8,128)S(1)} %fusion.35), custom_call_target="InvertDiagBlocksLowerTriangular" | custom-call | tf_op jit(solution)/shard_map/jit(_cho_solve)/triangular_solve | solution.py:213
  262.4 11.7 %cholesky.44 = f32[128,128]{1,0:T(8,128)S(1)} custom-call(f32[128,128]{1,0:T(8,128)S(1)} %get-tuple-element.12), custom_call_target="Cholesky" | custom-call | tf_op jit(solution)/shard_map/jit(cholesky)/cholesky | solution.py:210
  275.5 9.8 %custom-call.16 = f32[1,128,128]{1,2,0:T(8,128)S(1)} custom-call(f32[1,128,128]{2,1,0:T(8,128)S(1)} %fusion.34), custom_call_target="InvertDiagBlocksLowerTriangular" | custom-call | tf_op jit(solution)/shard_map/jit(_cho_solve)/triangular_solve | solution.py:211
  (181 shorter events, 42.3 us)
Async XLA Ops:
  0.6 12.8 %copy-start = (bf16[4096,256]{1,0:T(8,128)(2,1)S(1)}, bf16[4096,256]{1,0:T(8,128)(2,1)}, u32[]{:S(2)}) copy-start(bf16[4096,256]{1,0:T(8,128)(2,1)} %param.8) | copy-start | bytes 6291460
  0.6 12.8 %copy-start.10 = (f32[256]{0:T(256)S(1)}, f32[256]{0:T(256)}, u32[]{:S(2)}) copy-start(f32[256]{0:T(256)} %param.10) | copy-start | bytes 3076
  0.7 12.8 %copy-start.5 = (f32[256,128]{1,0:T(8,128)S(1)}, f32[256,128]{1,0:T(8,128)}, u32[]{:S(2)}) copy-start(f32[256,128]{1,0:T(8,128)} %param.9) | copy-start | bytes 393220
  3.4 36.6 %all-to-all-start.2 = ((f32[16,128,128]{2,1,0:T(8,128)}), f32[16,128,128]{2,1,0:T(8,128)S(1)}, u32[]{:S(2)}, u32[]{:S(2)}) async-start(f32[16,128,128]{2,1,0:T(8,128)} %broadcast_in_dim.48), calls=%async_computation.2 | async-start | bytes 2097152 | tf_op jit(solution)/shard_map/all_to_all | solution.py:28
  40.1 7.4 %copy-start.1 = (f32[128,128]{1,0:T(8,128)S(1)}, f32[128,128]{1,0:T(8,128)}, u32[]{:S(2)}) copy-start(f32[128,128]{1,0:T(8,128)} %param.13) | copy-start | bytes 196612
  40.1 35.3 %all-to-all-start = ((f32[32,128,128]{1,2,0:T(8,128)}), f32[32,128,128]{1,2,0:T(8,128)}, u32[]{:S(2)}, u32[]{:S(2)}) async-start(f32[32,128,128]{1,2,0:T(8,128)} %bitcast.507), calls=%async_computation | async-start | bytes 4194304 | tf_op jit(solution)/shard_map/all_to_all | solution.py:22
  76.4 20.4 %all-to-all-start.3 = ((f32[16,128,128]{2,1,0:T(8,128)}), f32[16,128,128]{2,1,0:T(8,128)S(1)}, u32[]{:S(2)}, u32[]{:S(2)}) async-start(f32[16,128,128]{2,1,0:T(8,128)} %broadcast_in_dim.49), calls=%async_computation.3 | async-start | bytes 2097152 | tf_op jit(solution)/shard_map/all_to_all | solution.py:28
  81.6 0.6 copy-start.3
  98.5 18.8 %all-to-all-start.1 = ((f32[8,128,128]{2,1,0:T(8,128)}), f32[8,128,128]{2,1,0:T(8,128)}, u32[]{:S(2)}, u32[]{:S(2)}) async-start(f32[8,128,128]{2,1,0:T(8,128)} %broadcast_in_dim.47), calls=%async_computation.1 | async-start | bytes 1048576 | tf_op jit(solution)/shard_map/all_to_all | solution.py:28
  124.1 0.6 copy-start.8
  131.1 24.8 %copy-start.7 = (f32[128,128]{1,0:T(8,128)S(1)}, f32[128,128]{1,0:T(8,128)}, u32[]{:S(2)}) copy-start(f32[128,128]{1,0:T(8,128)} %fusion.230) | copy-start | bytes 196612
  142.0 15.9 %copy-start.4 = (f32[128,128]{1,0:T(8,128)S(1)}, f32[128,128]{1,0:T(8,128)}, u32[]{:S(2)}) copy-start(f32[128,128]{1,0:T(8,128)} %copy-done.3) | copy-start | bytes 196612
  152.7 6.3 %copy-start.6 = (f32[128,128]{1,0:T(8,128)S(1)}, f32[128,128]{1,0:T(8,128)}, u32[]{:S(2)}) copy-start(f32[128,128]{1,0:T(8,128)} %fusion.76) | copy-start | bytes 196612
  179.4 42.6 %copy-start.9 = (f32[128,128]{1,0:T(8,128)S(1)}, f32[128,128]{1,0:T(8,128)}, u32[]{:S(2)}) copy-start(f32[128,128]{1,0:T(8,128)} %param.14) | copy-start | bytes 196612
  192.4 39.0 %copy-start.2 = (f32[128,128]{1,0:T(8,128)}, f32[128,128]{1,0:T(8,128)S(1)}, u32[]{:S(2)}) copy-start(f32[128,128]{1,0:T(8,128)S(1)} %get-tuple-element.5) | copy-start | bytes 196612
  192.7 8.6 %collective-permute-start = (f32[1,128]{1,0:T(1,128)S(1)}, f32[1,128]{1,0:T(1,128)S(1)}, u32[]{:S(2)}, u32[]{:S(2)}) collective-permute-start(f32[1,128]{1,0:T(1,128)S(1)} %slice.411), channel_id=1, source_target_pairs={{0,8},{8,16},{16,24},{24,32},{32,40},{40,48},{48,56},{56,64},{64,7... | collective-permute-start | bytes 1544 | tf_op jit(solution)/shard_map/ppermute | solution.py:82
  218.1 12.1 %all-to-all-start.5 = ((f32[32,1,1536]{2,1,0:T(1,128)}), f32[32,1,1536]{2,1,0:T(1,128)S(1)}, u32[]{:S(2)}, u32[]{:S(2)}) async-start(f32[32,1,1536]{2,1,0:T(1,128)} %broadcast_in_dim.54), calls=%async_computation.5 | async-start | bytes 393216 | tf_op jit(solution)/shard_map/all_to_all | solution.py:28
  231.4 56.2 %all-to-all-start.6 = ((bf16[32,128,128]{2,1,0:T(8,128)(2,1)}), bf16[32,128,128]{2,1,0:T(8,128)(2,1)S(1)}, u32[]{:S(2)}, u32[]{:S(2)}) async-start(bf16[32,128,128]{2,1,0:T(8,128)(2,1)} %broadcast_in_dim.55), calls=%async_computation.6 | async-start | bytes 2097152 | tf_op jit(solution)/shard_map/all_to_all | solution.py:28
where the time goes:
time: 291 us; the launch traced here: 290 us
  waiting for transfers between devices  78.8 us (27%)
  blocking collectives  66.9 us (23%)
  other arithmetic  51.7 us (18%)
  starting transfers between devices  42.1 us (14%)
  matrix products  33.4 us (11%)
  local copies, waits for them, and re-layouts  15.1 us (5%)
    all_gather x6, blocking collectives, collected_together(): both, at, found = (lax.all_gather(jnp.concatenate(lines), axis), 0, {})  51.4 us
    all_to_all x5, waiting for transfers between devices, sent_to_all(): return lax.all_to_all(copies, axis, split_axis=0, concat_axis=0, tiled=True)  50.9 us
    dot_general x98, matrix products, dot_high(): jnp.dot(left, right, precision=precise, preferred_element_type=jnp.float32)  29.4 us
    all_to_all x1, waiting for transfers between devices, sent_and_summed(): lax.all_to_all(pieces, axis, split_axis=0, concat_axis=0, tiled=True)  27.6 us
    all_to_all x5, starting transfers between devices, sent_to_all(): return lax.all_to_all(copies, axis, split_axis=0, concat_axis=0, tiled=True)  26.8 us
    all_to_all x1, blocking collectives, sent_and_summed(): lax.all_to_all(pieces, axis, split_axis=0, concat_axis=0, tiled=True)  15.6 us
    another operation x3, other arithmetic, local(): previous_factor = jnp.linalg.cholesky(previous)  13.2 us
    another operation x3, other arithmetic, local(): total_factor = jnp.linalg.cholesky(total)  12.4 us
  transfers between devices with their start and end apart: 7, of which 6 were waited for; matrix products, arithmetic and copies ran while one was open for 23% of the time, Pallas kernels for 0%

commit v1 on v0

v1 whole, which is shorter than its diff:
```python
import functools

import jax
import jax.numpy as jnp
from jax import lax
from jax.experimental import pallas as pl
from jax.experimental.pallas import tpu as pltpu
from jax.sharding import Mesh
from jax.sharding import PartitionSpec as P

Y, X, CORE, Z = "tm_0", "tm_1", "tm_2", "sr"
TM = (Y, X, CORE)
SR_TM = (Z, Y, X, CORE)

STEPS = 16
f32 = jnp.float32
bf16 = jnp.bfloat16
precise = lax.Precision.HIGHEST


def thirds(v):
    a = v.astype(bf16)
    rest = v - a.astype(f32)
    b = rest.astype(bf16)
    c = (rest - b.astype(f32)).astype(bf16)
    return a, b, c


def right(w):
    a, b, c = thirds(w)
    both = jnp.concatenate([a, b], axis=1)
    if w.shape[0] <= 128:
        return both, (jnp.concatenate([c, a], axis=0),)
    return both, (c, a)


def plain(a, b):
    return jnp.dot(a, b, preferred_element_type=f32)


def times(v, w):
    both, small = w
    n = both.shape[1] // 2
    a, b, c = thirds(v)
    p, q = plain(a, both), plain(b, both)
    if len(small) == 1:
        least = plain(jnp.concatenate([a, c], axis=1), small[0])
    else:
        least = plain(a, small[0]) + plain(c, small[1])
    return p[:, :n] + (p[:, n:] + q[:, :n] + (q[:, n:] + least))


def high(a, b):
    return times(a, right(b))


def contracted(a, b):
    return lax.dot_general(a, b, (((0,), (0,)), ((), ())), preferred_element_type=f32)


def moved(v, shift, row):
    n = v.shape[0]
    keep = (row >= shift) if shift > 0 else (row < n + shift)
    return jnp.where(keep, pltpu.roll(v, shift % n, 0), 0.0)


def powers(a, n):
    found = [a]
    while len(found) < STEPS:
        more = high(jnp.concatenate(found, axis=0), found[-1])
        found = found + [more[i * n : (i + 1) * n] for i in range(len(found))]
    return found


def scan_kernel(
    core_ref, own_ref, other_ref, ft_ref, kt_ref, jt_ref, cov_ref,
    x_ref, total_ref, previous_ref, lagged_ref, loc_ref, mat_ref,
):
    n = ft_ref.shape[0]
    groups = own_ref.shape[0]
    rows = x_ref.shape[0] // (2 * groups)
    blocks = x_ref.shape[0] // STEPS
    length = x_ref.shape[0]
    first = core_ref[0] == 0
    ft, kt, jt, cov = ft_ref[...], kt_ref[...], jt_ref[...], cov_ref[...]
    info = jnp.concatenate([own_ref[g, rows:] for g in range(groups)], axis=0)
    eye = (
        lax.broadcasted_iota(jnp.int32, (n, n), 0) == lax.broadcasted_iota(jnp.int32, (n, n), 1)
    ).astype(f32)
    row = lax.broadcasted_iota(jnp.int32, (blocks, n), 0)
    a = ft - high(high(ft, info), kt)
    b = eye - high(ft, jt)
    apow = powers(a, n)
    jpow = powers(jt, n)

    def drive(j):
        def half(ref):
            parts = [ref[g, pl.ds(j, rows // STEPS, stride=STEPS), :] for g in range(groups)]
            return jnp.concatenate(parts, axis=0)

        own, other = half(own_ref), half(other_ref)
        return jnp.concatenate(
            [jnp.where(first, own, other), jnp.where(first, other, own)], axis=0
        )

    step = right(jnp.concatenate([a, kt], axis=0))
    state = times(drive(0), right(kt))
    loc_ref[0] = state
    for j in range(1, STEPS):
        state = times(jnp.concatenate([state, drive(j)], axis=1), step)
        loc_ref[j] = state
    enter = state
    back = right(jnp.concatenate([jt, b], axis=0))
    both = lambda j: jnp.concatenate([loc_ref[j], apow[j]], axis=0)
    out = times(both(STEPS - 1), right(b))
    for j in range(STEPS - 1, -1, -1):
        if j < STEPS - 1:
            out = times(jnp.concatenate([out, both(j)], axis=1), back)
        loc_ref[j] = out[:blocks]
        mat_ref[j] = out[blocks:]
    power, shift = apow[STEPS - 1], 1
    while shift < blocks:
        w = right(power)
        enter = enter + times(moved(enter, shift, row), w)
        shift *= 2
        if shift < blocks:
            power = times(power, w)
    e = moved(enter, 1, row)
    after = high(jnp.where(row == blocks - 1, enter, 0.0), ft)
    z = loc_ref[0] + high(e, mat_ref[0]) + high(after, jpow[STEPS - 1])
    power, shift = jpow[STEPS - 1], 1
    while shift < blocks:
        w = right(power)
        z = z + times(moved(z, -shift, row), w)
        shift *= 2
        if shift < blocks:
            power = times(power, w)
    mix = jnp.concatenate([e, moved(z, -1, row) + after], axis=1)
    for j in range(STEPS):
        x = z
        if j > 0:
            x = loc_ref[j] + high(mix, jnp.concatenate([mat_ref[j], jpow[STEPS - 1 - j]], axis=0))
        loc_ref[j] = x
        x_ref[pl.ds(j, blocks, stride=STEPS), :] = x
    sums = jnp.zeros((n, 2 * n), f32)
    for j in range(STEPS):
        x = loc_ref[j]
        prior = moved(loc_ref[STEPS - 1], 1, row) if j == 0 else loc_ref[j - 1]
        xa, xb, _ = thirds(x)
        pa, pb, _ = thirds(prior)
        pair = jnp.concatenate([xa, pa], axis=1)
        rest = jnp.concatenate([xb, pb], axis=1)
        sums = sums + contracted(xa, pair) + (contracted(xb, pair) + contracted(xa, rest))
    last = jnp.where(row == blocks - 1, loc_ref[STEPS - 1], 0.0)
    la, lb, _ = thirds(last)
    ends = contracted(la, la) + (contracted(lb, la) + contracted(la, lb))
    total_ref[...] = sums[:, :n] + length * cov
    previous_ref[...] = (sums[:, :n] - ends) + (length - 1) * cov
    lagged_ref[...] = sums[:, n:] + (length - 1) * high(cov, jt)


def scanned(core, own, other, ft, kt, jt, cov, length):
    n = ft.shape[0]
    square = jax.ShapeDtypeStruct((n, n), f32)
    vmem = pl.BlockSpec(memory_space=pltpu.VMEM)
    return pl.pallas_call(
        scan_kernel,
        out_shape=(jax.ShapeDtypeStruct((length, n), f32), square, square, square),
        in_specs=[pl.BlockSpec(memory_space=pltpu.SMEM)] + [vmem] * 6,
        out_specs=[vmem] * 4,
        scratch_shapes=[
            pltpu.VMEM((STEPS, length // STEPS, n), f32),
            pltpu.VMEM((STEPS, n, n), f32),
        ],
        compiler_params=pltpu.CompilerParams(vmem_limit_bytes=44 * 1024 * 1024),
        cost_estimate=pl.CostEstimate(flops=10**10, bytes_accessed=5 * 10**6, transcendentals=0),
        name="scan",
    )(core, own, other, ft, kt, jt, cov)


def swept(mats, n):
    row8 = lax.broadcasted_iota(jnp.int32, (8, n), 0)
    lane = lax.broadcasted_iota(jnp.int32, (1, n), 1)
    mats = [[m[8 * g : 8 * g + 8] for g in range(n // 8)] for m in mats]
    for k in range(n):
        found = []
        for m in mats:
            g, o = divmod(k, 8)
            pivot_row = m[g][o : o + 1, :]
            d = 1.0 / pivot_row[:, k : k + 1]
            s = jnp.where(lane == k, d, pivot_row * d)
            new = []
            for i, t in enumerate(m):
                u = jnp.where(lane == k, 0.0, t) - t[:, k : k + 1] * s
                new.append(jnp.where(row8 == o, s, u) if i == g else u)
            found.append(new)
        mats = found
    return [jnp.concatenate(m, axis=0) for m in mats]


def inverse_kernel(total_ref, previous_ref, lagged_ref, inverse_ref, transition_ref):
    inverse, other = swept([total_ref[...], previous_ref[...]], total_ref.shape[0])
    inverse_ref[...] = inverse
    transition_ref[...] = high(lagged_ref[...], other)


def inverted(total, previous, lagged):
    vmem = pl.BlockSpec(memory_space=pltpu.VMEM)
    square = jax.ShapeDtypeStruct(total.shape, f32)
    return pl.pallas_call(
        inverse_kernel,
        out_shape=(square, square),
        in_specs=[vmem] * 3,
        out_specs=[vmem] * 2,
        compiler_params=pltpu.CompilerParams(vmem_limit_bytes=16 * 1024 * 1024),
        cost_estimate=pl.CostEstimate(flops=10**9, bytes_accessed=3 * 10**5, transcendentals=0),
        name="inverse",
    )(total, previous, lagged)


def turned(value, axis, steps):
    count = lax.axis_size(axis)
    return lax.ppermute(value, axis, [(i, (i + steps) % count) for i in range(count)])


def over_z(value):
    count = lax.axis_size(Z)
    value = value + lax.ppermute(value, Z, [(i, i ^ 1) for i in range(count)])
    arrived = [turned(value, Z, 2 * k) for k in range(1, count // 2)]
    return sum(arrived, value)


def local(
    observations, loadings, noise_precision, transition, filter_cov, smoother_gain, smoothed_cov
):
    core = lax.axis_index(CORE)
    position = lax.axis_index(TM)
    length = observations.shape[0]
    width = transition.shape[0]
    half = length // 2
    groups = lax.axis_size((Y, X))
    rows = half // groups
    extra = width // groups
    weighted = noise_precision[:, None] * loadings
    scaled = weighted.astype(bf16)

    def projected(which):
        window = lax.dynamic_slice_in_dim(observations, which * half, half, 0)
        return jnp.dot(window, scaled, preferred_element_type=f32)

    info_part = jnp.dot(loadings.T, weighted, precision=precise, preferred_element_type=f32)
    info_part = info_part + turned(info_part, CORE, 1)
    mine = projected(core) + turned(projected(1 - core), CORE, 1)
    pieces = jnp.concatenate(
        [mine.reshape(groups, rows, width), info_part.reshape(groups, extra, width)], axis=1
    )
    arrived = lax.all_to_all(pieces, (Y, X), split_axis=0, concat_axis=0, tiled=True)
    block = over_z(arrived.sum(axis=0))
    copies = jnp.broadcast_to(block, (groups, *block.shape))
    own = lax.all_to_all(copies, (Y, X), split_axis=0, concat_axis=0, tiled=True)
    other = turned(own, CORE, 1)
    smoothed, total, previous, lagged = scanned(
        core[None].astype(jnp.int32), own, other,
        transition.T, filter_cov.T, smoother_gain.T, smoothed_cov, length,
    )
    inverse, new_transition = inverted(total, previous, lagged)
    cross = jnp.einsum(
        "ts,tk->sk", observations, smoothed.astype(bf16), preferred_element_type=f32
    )
    new_loadings = jnp.dot(cross, inverse, precision=precise, preferred_element_type=f32)
    steps_dev = length // lax.axis_size(TM)
    shown = lax.dynamic_slice_in_dim(smoothed, position * steps_dev, steps_dev, 0)
    return (shown, new_loadings, new_transition)


def solution(mesh):
    split = Mesh(mesh.devices.reshape(4, 4, 2, mesh.shape["sr"]), (Y, X, CORE, Z))
    in_specs = (P(None, SR_TM), P(SR_TM, None), P(SR_TM), P(), P(), P(), P())
    out_specs = (P(TM, None), P(SR_TM, None), P())
    return jax.shard_map(local, mesh=split, in_specs=in_specs, out_specs=out_specs, check_vma=False)
```

time: 291 us -> 112 us (0.38)
  waiting for transfers between devices: 78.8 us -> 10.5 us
  other arithmetic: 51.7 us -> 0.18 us
  Pallas kernels: 0 us -> 34.6 us
  matrix products: 33.4 us -> 5.11 us
  blocking collectives: 66.9 us -> 39 us
  starting transfers between devices: 42.1 us -> 19.3 us
  local copies, waits for them, and re-layouts: 15.1 us -> 2.57 us
    all_to_all x6 -> x0, waiting for transfers between devices: 78.5 us -> none  [the longest x5 50.9 us: sent_to_all(): return lax.all_to_all(copies, axis, split_axis=0, concat_axis=0, tiled=True)]
    all_gather x6 -> x0, blocking collectives: 51.4 us -> none  [collected_together(): both, at, found = (lax.all_gather(jnp.concatenate(lines), axis), 0, {})]
    another operation x10 -> x0, other arithmetic: 46.5 us -> none  [the longest x3 13.2 us: local(): previous_factor = jnp.linalg.cholesky(previous)]
    pallas_call x0 -> x2, Pallas kernels: none -> 34.6 us  [the longest x1 22.2 us: scanned(): pl.pallas_call(scan_kernel, out_shape=(jax.ShapeDtypeStruct((length, n),...]
    all_to_all x6 -> x0, starting transfers between devices: 34.1 us -> none  [the longest x5 26.8 us: sent_to_all(): return lax.all_to_all(copies, axis, split_axis=0, concat_axis=0, tiled=True)]
    dot_general x100 -> x5, matrix products: 30.8 us -> 5.11 us  [the longest x2 3.12 us: projected(): return jnp.dot(window, scaled, preferred_element_type=f32)]
    all_to_all x1 -> x2, blocking collectives: 15.6 us -> 39 us  [the longest x1 21.8 us: local(): lax.all_to_all(pieces, (Y, X), split_axis=0, concat_axis=0, tiled=True)]
    ppermute x1 -> x7, starting transfers between devices: 7.91 us -> 19.3 us  [the longest x6 17.6 us: turned(): lax.ppermute(value, axis, [(i, (i + steps) % count) for i in range(count)])]
  transfers between devices with their start and end apart: 7 -> 7, of which waited for: 6 -> 5; matrix products, arithmetic and copies ran while one was open for 23% -> 1% of each run, Pallas kernels for 0% -> 0%
where the time goes in v1:
time: 112 us
  blocking collectives  39 us (35%)
  Pallas kernels  34.6 us (31%)
  starting transfers between devices  19.3 us (17%)
  waiting for transfers between devices  10.5 us (9%)
  matrix products  5.11 us (5%)
  local copies, waits for them, and re-layouts  2.57 us (2%)
    pallas_call x1, Pallas kernels, scanned(): pl.pallas_call(scan_kernel, out_shape=(jax.ShapeDtypeStruct((length, n),...  22.2 us
    all_to_all x1, blocking collectives, local(): lax.all_to_all(pieces, (Y, X), split_axis=0, concat_axis=0, tiled=True)  21.8 us
    ppermute x6, starting transfers between devices, turned(): lax.ppermute(value, axis, [(i, (i + steps) % count) for i in range(count)])  17.6 us
    all_to_all x1, blocking collectives, local(): lax.all_to_all(copies, (Y, X), split_axis=0, concat_axis=0, tiled=True)  17.2 us
    pallas_call x1, Pallas kernels, inverted(): pl.pallas_call(inverse_kernel, out_shape=(square, square), in_specs=[vmem...  12.4 us
    ppermute x6, waiting for transfers between devices, turned(): lax.ppermute(value, axis, [(i, (i + steps) % count) for i in range(count)])  8.78 us
    dot_general x2, matrix products, projected(): return jnp.dot(window, scaled, preferred_element_type=f32)  3.12 us
  transfers between devices with their start and end apart: 7, of which 5 were waited for; matrix products, arithmetic and copies ran while one was open for 1% of the time, Pallas kernels for 0%

profile of v1, /device:TPU:1, one launch (start us, length us, event | category | flops | bytes accessed | tf_op | source)
XLA Modules:
  0.0 112.0 jit_solution(14392838665814136032)
XLA Ops:
  0.6 0.0 copy-start
  0.7 1.6 %copy-done = bf16[4096,256]{1,0:T(8,128)(2,1)S(1)} copy-done((bf16[4096,256]{1,0:T(8,128)(2,1)S(1)}, bf16[4096,256]{1,0:T(8,128)(2,1)}, u32[]{:S(2)}) %copy-start) | copy-done | bytes 2097176
  2.2 1.4 %fusion.2 = f32[2048,128]{1,0:T(8,128)S(1)} fusion(bf16[4096,256]{1,0:T(8,128)(2,1)S(1)} %copy-done, s32[]{:T(128)S(6)} %select_n.10, f32[256,128]{1,0:T(8,128)} %param.8, f32[256]{0:T(256)} %param.9), kind=kOutput, calls=%fused_computation.5 | convolution fusion | flops 134283264 | bytes 2229252 | tf_op jit(solution)/shard_map/dot_general | solution.py:249
  3.6 3.3 %collective-permute-start = (f32[2048,128]{1,0:T(8,128)S(1)}, f32[2048,128]{1,0:T(8,128)}, u32[]{:S(2)}, u32[]{:S(2)}) collective-permute-start(f32[2048,128]{1,0:T(8,128)S(1)} %fusion.2), channel_id=1, source_target_pairs={{0,8},{8,0},{1,9},{9,1},{2,10},{10,2},{3,11},{11,3},{4,12},{12,4},... | collective-permute-start | bytes 3145736 | tf_op jit(solution)/shard_map/ppermute | solution.py:223
  7.0 0.4 convolution_bitcast_fusion
  7.4 0.1 collective-permute-start.1
  7.5 1.8 %collective-permute-done.1 = f32[128,128]{1,0:T(8,128)S(1)} collective-permute-done((f32[128,128]{1,0:T(8,128)S(1)}, f32[128,128]{1,0:T(8,128)S(1)}, u32[]{:S(2)}, u32[]{:S(2)}) %collective-permute-start.1) | collective-permute-done | bytes 65568 | tf_op jit(solution)/shard_map/ppermute | solution.py:223
  9.3 0.0 collective-permute-done
  9.4 1.7 %convolution_add_fusion = f32[2048,128]{1,0:T(8,128)S(1)} fusion(f32[2048,128]{1,0:T(8,128)} %collective-permute-done, bf16[4096,256]{1,0:T(8,128)(2,1)S(1)} %copy-done, s32[]{:T(128)S(6)} %select_n.9, f32[256,128]{1,0:T(8,128)S(1)} %copy-done.2, f32[256]{0:T(256)S(1)} %copy-done.6), kind=kOutput, calls=%fused_computation | convolution fusion | flops 134545408 | bytes 3277828 | tf_op jit(solution)/shard_map/dot_general | solution.py:249
  11.1 0.1 pad_maximum_fusion
  11.2 21.8 %all_to_all.10 = f32[16,136,128]{2,1,0:T(8,128)S(1)} all-to-all(f32[16,136,128]{2,1,0:T(8,128)S(1)} %pad_maximum_fusion), channel_id=1, replica_groups=mesh['tm_0'=4,'tm_1'=4,'tm_2'=2,'sr'=8] {'tm_0','tm_1'}, dimensions={0} | all-to-all | bytes 2228224 | tf_op jit(solution)/shard_map/all_to_all | solution.py:257
  33.0 0.1 reduce_sum.9
  33.1 0.0 copy-start.4
  33.1 1.7 %collective-permute-start.2 = (f32[136,128]{1,0:T(8,128)S(1)}, f32[136,128]{1,0:T(8,128)S(1)}, u32[]{:S(2)}, u32[]{:S(2)}) collective-permute-start(f32[136,128]{1,0:T(8,128)S(1)} %reduce_sum.9), channel_id=1, source_target_pairs={{0,1},{1,0},{2,3},{3,2},{4,5},{5,4},{6,7},{7,6},{8,9},{9,8},{10,11... | collective-permute-start | bytes 208904 | tf_op jit(solution)/shard_map/ppermute | solution.py:228
  34.9 1.7 %collective-permute-done.2 = f32[136,128]{1,0:T(8,128)S(1)} collective-permute-done((f32[136,128]{1,0:T(8,128)S(1)}, f32[136,128]{1,0:T(8,128)S(1)}, u32[]{:S(2)}, u32[]{:S(2)}) %collective-permute-start.2) | collective-permute-done | bytes 69664 | tf_op jit(solution)/shard_map/ppermute | solution.py:228
  36.6 5.9 %collective-permute-start.5 = (f32[136,128]{1,0:T(8,128)S(1)}, f32[136,128]{1,0:T(8,128)S(1)}, u32[]{:S(2)}, u32[]{:S(2)}) collective-permute-start(f32[136,128]{1,0:T(8,128)S(1)} %add.37), channel_id=1, source_target_pairs={{0,6},{1,7},{2,0},{3,1},{4,2},{5,3},{6,4},{7,5},{8,14},{9,15},{10,... | collective-permute-start | bytes 208904 | tf_op jit(solution)/shard_map/ppermute | solution.py:223
  42.5 1.0 collective-permute-start.4
  43.5 2.3 %collective-permute-start.3 = (f32[136,128]{1,0:T(8,128)S(1)}, f32[136,128]{1,0:T(8,128)S(1)}, u32[]{:S(2)}, u32[]{:S(2)}) collective-permute-start(f32[136,128]{1,0:T(8,128)S(1)} %add.37), channel_id=1, source_target_pairs={{0,2},{1,3},{2,4},{3,5},{4,6},{5,7},{6,0},{7,1},{8,10},{9,11},{10,... | collective-permute-start | bytes 208904 | tf_op jit(solution)/shard_map/ppermute | solution.py:223
  45.8 4.0 %collective-permute-done.4 = f32[136,128]{1,0:T(8,128)S(1)} collective-permute-done((f32[136,128]{1,0:T(8,128)S(1)}, f32[136,128]{1,0:T(8,128)S(1)}, u32[]{:S(2)}, u32[]{:S(2)}) %collective-permute-start.4) | collective-permute-done | bytes 69664 | tf_op jit(solution)/shard_map/ppermute | solution.py:223
  49.8 0.7 collective-permute-done.3
  50.5 0.1 broadcast_in_dim.8
  50.6 17.2 %all_to_all.11.own_ref = f32[16,136,128]{2,1,0:T(8,128)S(1)} all-to-all(f32[16,136,128]{2,1,0:T(8,128)S(1)} %broadcast_in_dim.8), channel_id=1, replica_groups=mesh['tm_0'=4,'tm_1'=4,'tm_2'=2,'sr'=8] {'tm_0','tm_1'}, dimensions={0} | all-to-all | bytes 2228224 | tf_op jit(solution)/shard_map/all_to_all | solution.py:260
  67.8 4.9 %collective-permute-start.6 = (f32[16,136,128]{2,1,0:T(8,128)S(1)}, f32[16,136,128]{2,1,0:T(8,128)}, u32[]{:S(2)}, u32[]{:S(2)}) collective-permute-start(f32[16,136,128]{2,1,0:T(8,128)S(1)} %all_to_all.11.own_ref), channel_id=1, source_target_pairs={{0,8},{8,0},{1,9},{9,1},{2,10},{10,2},{3,11},{11,3},{4,12},{12,4},... | collective-permute-start | bytes 3342344 | tf_op jit(solution)/shard_map/ppermute | solution.py:223
  72.7 0.1 copy.10
  72.8 0.1 copy.11
  72.9 0.1 copy.12
  73.0 2.2 %collective-permute-done.6.other_ref = f32[16,136,128]{2,1,0:T(8,128)} collective-permute-done((f32[16,136,128]{2,1,0:T(8,128)S(1)}, f32[16,136,128]{2,1,0:T(8,128)}, u32[]{:S(2)}, u32[]{:S(2)}) %collective-permute-start.6) | collective-permute-done | bytes 1114144 | tf_op jit(solution)/shard_map/ppermute | solution.py:223
  75.2 22.2 %scan.1 = (f32[4096,128]{1,0:T(8,128)S(1)}, f32[128,128]{1,0:T(8,128)S(1)}, f32[128,128]{1,0:T(8,128)S(1)}, f32[128,128]{1,0:T(8,128)S(1)}) custom-call(s32[1]{0:T(128)} %bitcast.core_ref, f32[16,136,128]{2,1,0:T(8,128)S(1)} %all_to_all.11.own_ref, f32[16,136,128]{2,1,0:T(8,128)} %collective-permute-done.6.other_ref, f32[128,128]{1,0:T(8,128)S(1)} %bitcast.13, ...), custom_call_target="tpu_custom_call" | custom-call | flops 10000000000 | bytes 5000000 | tf_op jit(solution)/shard_map/scan/pallas_call | solution.py:166
  97.5 0.5 fusion
  98.0 0.6 constant_dynamic-slice_fusion
  98.6 12.4 %inverse.1 = (f32[128,128]{1,0:T(8,128)S(1)}, f32[128,128]{1,0:T(8,128)}) custom-call(f32[128,128]{1,0:T(8,128)S(1)} %get-tuple-element.10.total_ref, f32[128,128]{1,0:T(8,128)S(1)} %get-tuple-element.11.previous_ref, f32[128,128]{1,0:T(8,128)S(1)} %get-tuple-element.12.lagged_ref), custom_call_target="tpu_custom_call" | custom-call | flops 1000000000 | bytes 300000 | tf_op jit(solution)/shard_map/inverse/pallas_call | solution.py:210
  111.0 1.0 fusion.9
  (15 shorter events, 0.1 us)
Async XLA Ops:
  0.6 1.6 %copy-start = (bf16[4096,256]{1,0:T(8,128)(2,1)S(1)}, bf16[4096,256]{1,0:T(8,128)(2,1)}, u32[]{:S(2)}) copy-start(bf16[4096,256]{1,0:T(8,128)(2,1)} %param.7) | copy-start | bytes 6291460
  0.6 6.3 %copy-start.6 = (f32[256]{0:T(256)S(1)}, f32[256]{0:T(256)}, u32[]{:S(2)}) copy-start(f32[256]{0:T(256)} %param.9) | copy-start | bytes 3076
  0.7 6.3 %copy-start.2 = (f32[256,128]{1,0:T(8,128)S(1)}, f32[256,128]{1,0:T(8,128)}, u32[]{:S(2)}) copy-start(f32[256,128]{1,0:T(8,128)} %param.8) | copy-start | bytes 393220
  3.6 5.7 %collective-permute-start = (f32[2048,128]{1,0:T(8,128)S(1)}, f32[2048,128]{1,0:T(8,128)}, u32[]{:S(2)}, u32[]{:S(2)}) collective-permute-start(f32[2048,128]{1,0:T(8,128)S(1)} %fusion.2), channel_id=1, source_target_pairs={{0,8},{8,0},{1,9},{9,1},{2,10},{10,2},{3,11},{11,3},{4,12},{12,4},... | collective-permute-start | bytes 3145736 | tf_op jit(solution)/shard_map/ppermute | solution.py:223
  7.4 1.9 %collective-permute-start.1 = (f32[128,128]{1,0:T(8,128)S(1)}, f32[128,128]{1,0:T(8,128)S(1)}, u32[]{:S(2)}, u32[]{:S(2)}) collective-permute-start(f32[128,128]{1,0:T(8,128)S(1)} %convolution_bitcast_fusion), channel_id=1, source_target_pairs={{0,8},{8,0},{1,9},{9,1},{2,10},{10,2},{3,11},{11,3},{4,12},{12,4},... | collective-permute-start | bytes 196616 | tf_op jit(solution)/shard_map/ppermute | solution.py:223
  33.1 39.6 %copy-start.3 = (f32[128,128]{1,0:T(8,128)S(1)}, f32[128,128]{1,0:T(8,128)}, u32[]{:S(2)}) copy-start(f32[128,128]{1,0:T(8,128)} %param.10) | copy-start | bytes 196612
  33.1 39.7 %copy-start.4 = (f32[128,128]{1,0:T(8,128)S(1)}, f32[128,128]{1,0:T(8,128)}, u32[]{:S(2)}) copy-start(f32[128,128]{1,0:T(8,128)} %param.11) | copy-start | bytes 196612
  33.1 39.8 %copy-start.5 = (f32[128,128]{1,0:T(8,128)S(1)}, f32[128,128]{1,0:T(8,128)}, u32[]{:S(2)}) copy-start(f32[128,128]{1,0:T(8,128)} %param.12) | copy-start | bytes 196612
  33.1 3.4 %collective-permute-start.2 = (f32[136,128]{1,0:T(8,128)S(1)}, f32[136,128]{1,0:T(8,128)S(1)}, u32[]{:S(2)}, u32[]{:S(2)}) collective-permute-start(f32[136,128]{1,0:T(8,128)S(1)} %reduce_sum.9), channel_id=1, source_target_pairs={{0,1},{1,0},{2,3},{3,2},{4,5},{5,4},{6,7},{7,6},{8,9},{9,8},{10,11... | collective-permute-start | bytes 208904 | tf_op jit(solution)/shard_map/ppermute | solution.py:228
  36.6 38.7 %copy-start.1 = (f32[128,128]{1,0:T(8,128)S(1)}, f32[128,128]{1,0:T(8,128)}, u32[]{:S(2)}) copy-start(f32[128,128]{1,0:T(8,128)} %cov_ref.1) | copy-start | bytes 196612
  36.6 9.2 %collective-permute-start.5 = (f32[136,128]{1,0:T(8,128)S(1)}, f32[136,128]{1,0:T(8,128)S(1)}, u32[]{:S(2)}, u32[]{:S(2)}) collective-permute-start(f32[136,128]{1,0:T(8,128)S(1)} %add.37), channel_id=1, source_target_pairs={{0,6},{1,7},{2,0},{3,1},{4,2},{5,3},{6,4},{7,5},{8,14},{9,15},{10,... | collective-permute-start | bytes 208904 | tf_op jit(solution)/shard_map/ppermute | solution.py:223
  42.5 7.3 %collective-permute-start.4 = (f32[136,128]{1,0:T(8,128)S(1)}, f32[136,128]{1,0:T(8,128)S(1)}, u32[]{:S(2)}, u32[]{:S(2)}) collective-permute-start(f32[136,128]{1,0:T(8,128)S(1)} %add.37), channel_id=1, source_target_pairs={{0,4},{1,5},{2,6},{3,7},{4,0},{5,1},{6,2},{7,3},{8,12},{9,13},{10,... | collective-permute-start | bytes 208904 | tf_op jit(solution)/shard_map/ppermute | solution.py:223
  43.5 7.0 %collective-permute-start.3 = (f32[136,128]{1,0:T(8,128)S(1)}, f32[136,128]{1,0:T(8,128)S(1)}, u32[]{:S(2)}, u32[]{:S(2)}) collective-permute-start(f32[136,128]{1,0:T(8,128)S(1)} %add.37), channel_id=1, source_target_pairs={{0,2},{1,3},{2,4},{3,5},{4,6},{5,7},{6,0},{7,1},{8,10},{9,11},{10,... | collective-permute-start | bytes 208904 | tf_op jit(solution)/shard_map/ppermute | solution.py:223
  67.8 7.4 %collective-permute-start.6 = (f32[16,136,128]{2,1,0:T(8,128)S(1)}, f32[16,136,128]{2,1,0:T(8,128)}, u32[]{:S(2)}, u32[]{:S(2)}) collective-permute-start(f32[16,136,128]{2,1,0:T(8,128)S(1)} %all_to_all.11.own_ref), channel_id=1, source_target_pairs={{0,8},{8,0},{1,9},{9,1},{2,10},{10,2},{3,11},{11,3},{4,12},{12,4},... | collective-permute-start | bytes 3342344 | tf_op jit(solution)/shard_map/ppermute | solution.py:223

commit v2 on v1

--- a/solution.py
+++ b/solution.py
@@ -1,5 +1,3 @@
-import functools
-
 import jax
 import jax.numpy as jnp
 from jax import lax
@@ -12,7 +10,8 @@
 TM = (Y, X, CORE)
 SR_TM = (Z, Y, X, CORE)
 
-STEPS = 16
+STEPS = 8
+SQUARINGS = 7
 f32 = jnp.float32
 bf16 = jnp.bfloat16
 precise = lax.Precision.HIGHEST
@@ -39,9 +38,13 @@
 
 
 def times(v, w):
+    return times_split(thirds(v), w)
+
+
+def times_split(v, w):
     both, small = w
     n = both.shape[1] // 2
-    a, b, c = thirds(v)
+    a, b, c = v
     p, q = plain(a, both), plain(b, both)
     if len(small) == 1:
         least = plain(jnp.concatenate([a, c], axis=1), small[0])
@@ -72,26 +75,82 @@
     return found
 
 
+def kept(blocks_at, count=1):
+    both = blocks_at[0]
+    small = blocks_at[1]
+    if count == 1:
+        return both, (jnp.concatenate([small, both[:, : both.shape[1] // 2]], axis=0),)
+    return both, (small, both[:, : both.shape[1] // 2])
+
+
+def beneath(*pieces):
+    return tuple(jnp.concatenate(p, axis=0) for p in zip(*pieces))
+
+
+def pieces_of(w):
+    a, b, c = thirds(w)
+    return jnp.concatenate([a, b], axis=1), c
+
+
+def ready_kernel(ft_ref, kt_ref, jt_ref, cov_ref, both_ref, small_ref, drift_ref):
+    n = ft_ref.shape[0]
+    ft, kt, jt = ft_ref[...], kt_ref[...], jt_ref[...]
+    eye = (
+        lax.broadcasted_iota(jnp.int32, (n, n), 0) == lax.broadcasted_iota(jnp.int32, (n, n), 1)
+    ).astype(f32)
+
+    def put(at, w):
+        both, small = pieces_of(w)
+        both_ref[at] = both
+        small_ref[at] = small
+
+    put(0, kt)
+    put(1, eye - high(ft, jt))
+    raised = powers(jt, n)
+    for k, w in enumerate(raised):
+        put(2 + k, w)
+    power = raised[-1]
+    for k in range(STEPS + 2, both_ref.shape[0]):
+        power = high(power, power)
+        put(k, power)
+    drift_ref[...] = high(cov_ref[...], jt)
+
+
+def readied(ft, kt, jt, cov, length):
+    n = ft.shape[0]
+    count = 2 + STEPS + (length // STEPS).bit_length() - 2
+    vmem = pl.BlockSpec(memory_space=pltpu.VMEM)
+    return pl.pallas_call(
+        ready_kernel,
+        out_shape=(
+            jax.ShapeDtypeStruct((count, n, 2 * n), bf16),
+            jax.ShapeDtypeStruct((count, n, n), bf16),
+            jax.ShapeDtypeStruct((n, n), f32),
+        ),
+        in_specs=[vmem] * 4,
+        out_specs=[vmem] * 3,
+        compiler_params=pltpu.CompilerParams(vmem_limit_bytes=16 * 1024 * 1024),
+        cost_estimate=pl.CostEstimate(flops=10**9, bytes_accessed=2 * 10**6, transcendentals=0),
+        name="ready",
+    )(ft, kt, jt, cov)
+
+
 def scan_kernel(
-    core_ref, own_ref, other_ref, ft_ref, kt_ref, jt_ref, cov_ref,
-    x_ref, total_ref, previous_ref, lagged_ref, loc_ref, mat_ref,
+    core_ref, place_ref, own_ref, other_ref, both_ref, small_ref, ft_ref, kt_ref, cov_ref, drift_ref,
+    x_ref, shown_ref, total_ref, previous_ref, lagged_ref, loc_ref, mat_ref,
 ):
     n = ft_ref.shape[0]
     groups = own_ref.shape[0]
-    rows = x_ref.shape[0] // (2 * groups)
-    blocks = x_ref.shape[0] // STEPS
     length = x_ref.shape[0]
+    rows = length // (2 * groups)
+    blocks = length // STEPS
     first = core_ref[0] == 0
-    ft, kt, jt, cov = ft_ref[...], kt_ref[...], jt_ref[...], cov_ref[...]
+    ft, cov = ft_ref[...], cov_ref[...]
+    held = lambda k: (both_ref[k], small_ref[k])
     info = jnp.concatenate([own_ref[g, rows:] for g in range(groups)], axis=0)
-    eye = (
-        lax.broadcasted_iota(jnp.int32, (n, n), 0) == lax.broadcasted_iota(jnp.int32, (n, n), 1)
-    ).astype(f32)
     row = lax.broadcasted_iota(jnp.int32, (blocks, n), 0)
-    a = ft - high(high(ft, info), kt)
-    b = eye - high(ft, jt)
+    a = ft - times(high(ft, info), kept(held(0)))
     apow = powers(a, n)
-    jpow = powers(jt, n)
 
     def drive(j):
         def half(ref):
@@ -103,16 +162,16 @@
             [jnp.where(first, own, other), jnp.where(first, other, own)], axis=0
         )
 
-    step = right(jnp.concatenate([a, kt], axis=0))
-    state = times(drive(0), right(kt))
+    step = kept(beneath(pieces_of(a), held(0)), 2)
+    state = times(drive(0), kept(held(0)))
     loc_ref[0] = state
     for j in range(1, STEPS):
         state = times(jnp.concatenate([state, drive(j)], axis=1), step)
         loc_ref[j] = state
     enter = state
-    back = right(jnp.concatenate([jt, b], axis=0))
+    back = kept(beneath(held(2), held(1)), 2)
     both = lambda j: jnp.concatenate([loc_ref[j], apow[j]], axis=0)
-    out = times(both(STEPS - 1), right(b))
+    out = times(both(STEPS - 1), kept(held(1)))
     for j in range(STEPS - 1, -1, -1):
         if j < STEPS - 1:
             out = times(jnp.concatenate([out, both(j)], axis=1), back)
@@ -127,19 +186,19 @@
             power = times(power, w)
     e = moved(enter, 1, row)
     after = high(jnp.where(row == blocks - 1, enter, 0.0), ft)
-    z = loc_ref[0] + high(e, mat_ref[0]) + high(after, jpow[STEPS - 1])
-    power, shift = jpow[STEPS - 1], 1
+    z = loc_ref[0] + high(e, mat_ref[0]) + times(after, kept(held(1 + STEPS)))
+    level, shift = 1 + STEPS, 1
     while shift < blocks:
-        w = right(power)
-        z = z + times(moved(z, -shift, row), w)
+        z = z + times(moved(z, -shift, row), kept(held(level)))
         shift *= 2
-        if shift < blocks:
-            power = times(power, w)
+        level += 1
     mix = jnp.concatenate([e, moved(z, -1, row) + after], axis=1)
+    mixed = thirds(mix)
     for j in range(STEPS):
         x = z
         if j > 0:
-            x = loc_ref[j] + high(mix, jnp.concatenate([mat_ref[j], jpow[STEPS - 1 - j]], axis=0))
+            w = kept(beneath(pieces_of(mat_ref[j]), held(1 + STEPS - j)), 2)
+            x = loc_ref[j] + times_split(mixed, w)
         loc_ref[j] = x
         x_ref[pl.ds(j, blocks, stride=STEPS), :] = x
     sums = jnp.zeros((n, 2 * n), f32)
@@ -151,23 +210,31 @@
         pair = jnp.concatenate([xa, pa], axis=1)
         rest = jnp.concatenate([xb, pb], axis=1)
         sums = sums + contracted(xa, pair) + (contracted(xb, pair) + contracted(xa, rest))
-    last = jnp.where(row == blocks - 1, loc_ref[STEPS - 1], 0.0)
+    last = jnp.where(lax.broadcasted_iota(jnp.int32, (8, n), 0) == 7, x_ref[length - 8 :], 0.0)
     la, lb, _ = thirds(last)
     ends = contracted(la, la) + (contracted(lb, la) + contracted(la, lb))
     total_ref[...] = sums[:, :n] + length * cov
     previous_ref[...] = (sums[:, :n] - ends) + (length - 1) * cov
-    lagged_ref[...] = sums[:, n:] + (length - 1) * high(cov, jt)
-
-
-def scanned(core, own, other, ft, kt, jt, cov, length):
+    lagged_ref[...] = sums[:, n:] + (length - 1) * drift_ref[...]
+    count = shown_ref.shape[0]
+    shown_ref[...] = x_ref[pl.ds(pl.multiple_of(place_ref[0] * count, count), count), :]
+
+
+def scanned(core, place, own, other, ready, ft, kt, cov, length, parts):
+    both, small, drift = ready
     n = ft.shape[0]
     square = jax.ShapeDtypeStruct((n, n), f32)
     vmem = pl.BlockSpec(memory_space=pltpu.VMEM)
+    smem = pl.BlockSpec(memory_space=pltpu.SMEM)
     return pl.pallas_call(
         scan_kernel,
-        out_shape=(jax.ShapeDtypeStruct((length, n), f32), square, square, square),
-        in_specs=[pl.BlockSpec(memory_space=pltpu.SMEM)] + [vmem] * 6,
-        out_specs=[vmem] * 4,
+        out_shape=(
+            jax.ShapeDtypeStruct((length, n), f32),
+            jax.ShapeDtypeStruct((length // parts, n), f32),
+            square, square, square,
+        ),
+        in_specs=[smem] * 2 + [vmem] * 8,
+        out_specs=[vmem] * 5,
         scratch_shapes=[
             pltpu.VMEM((STEPS, length // STEPS, n), f32),
             pltpu.VMEM((STEPS, n, n), f32),
@@ -175,7 +242,7 @@
         compiler_params=pltpu.CompilerParams(vmem_limit_bytes=44 * 1024 * 1024),
         cost_estimate=pl.CostEstimate(flops=10**10, bytes_accessed=5 * 10**6, transcendentals=0),
         name="scan",
-    )(core, own, other, ft, kt, jt, cov)
+    )(core, place, own, other, both, small, ft, kt, cov, drift)
 
 
 def swept(mats, n):
@@ -198,24 +265,60 @@
     return [jnp.concatenate(m, axis=0) for m in mats]
 
 
-def inverse_kernel(total_ref, previous_ref, lagged_ref, inverse_ref, transition_ref):
-    inverse, other = swept([total_ref[...], previous_ref[...]], total_ref.shape[0])
-    inverse_ref[...] = inverse
-    transition_ref[...] = high(lagged_ref[...], other)
-
-
-def inverted(total, previous, lagged):
+def three(v, w):
+    a, b, _ = thirds(v)
+    c, d, _ = thirds(w)
+    n = w.shape[1]
+    y = plain(a, jnp.concatenate([c, d], axis=1))
+    return y[:, :n] + (y[:, n:] + plain(b, c))
+
+
+def inverse_kernel(total_ref, previous_ref, lagged_ref, cross_ref, loadings_ref, transition_ref, found_ref):
+    n = total_ref.shape[0]
+    eye = (
+        lax.broadcasted_iota(jnp.int32, (n, n), 0) == lax.broadcasted_iota(jnp.int32, (n, n), 1)
+    ).astype(f32)
+    mats = [total_ref[...], previous_ref[...]]
+    near, left = [], []
+    for m in mats:
+        bound = jnp.max(jnp.sum(jnp.abs(m), axis=0, keepdims=True), axis=1, keepdims=True)
+        r = eye - m * (1.8 / bound)
+        left.append(r)
+        near.append((eye + r) * (1.8 / bound))
+    for _ in range(SQUARINGS):
+        for i in range(2):
+            left[i] = three(left[i], left[i])
+            near[i] = near[i] + three(near[i], left[i])
+    size = jnp.zeros((1, 1), f32)
+    for i in range(2):
+        r = eye - high(mats[i], near[i])
+        found_ref[i] = near[i] + three(near[i], r)
+        square = jnp.sum(jnp.sum(r * r, axis=0, keepdims=True), axis=1, keepdims=True)
+        size = jnp.maximum(size, square)
+
+    @pl.when(jnp.logical_not(size[0, 0] < 1e-6))
+    def _():
+        one, two = swept([total_ref[...], previous_ref[...]], n)
+        found_ref[0] = one
+        found_ref[1] = two
+
+    loadings_ref[...] = high(cross_ref[...], found_ref[0])
+    transition_ref[...] = high(lagged_ref[...], found_ref[1])
+
+
+def inverted(total, previous, lagged, cross):
     vmem = pl.BlockSpec(memory_space=pltpu.VMEM)
     square = jax.ShapeDtypeStruct(total.shape, f32)
     return pl.pallas_call(
         inverse_kernel,
-        out_shape=(square, square),
-        in_specs=[vmem] * 3,
+        out_shape=(jax.ShapeDtypeStruct(cross.shape, f32), square),
+        in_specs=[vmem] * 4,
         out_specs=[vmem] * 2,
+        scratch_shapes=[pltpu.VMEM((2, *total.shape), f32)],
         compiler_params=pltpu.CompilerParams(vmem_limit_bytes=16 * 1024 * 1024),
-        cost_estimate=pl.CostEstimate(flops=10**9, bytes_accessed=3 * 10**5, transcendentals=0),
+        cost_estimate=pl.CostEstimate(flops=10**9, bytes_accessed=6 * 10**5, transcendentals=0),
         name="inverse",
-    )(total, previous, lagged)
+    )(total, previous, lagged, cross)
 
 
 def turned(value, axis, steps):
@@ -259,17 +362,15 @@
     copies = jnp.broadcast_to(block, (groups, *block.shape))
     own = lax.all_to_all(copies, (Y, X), split_axis=0, concat_axis=0, tiled=True)
     other = turned(own, CORE, 1)
-    smoothed, total, previous, lagged = scanned(
-        core[None].astype(jnp.int32), own, other,
-        transition.T, filter_cov.T, smoother_gain.T, smoothed_cov, length,
+    ready = readied(transition.T, filter_cov.T, smoother_gain.T, smoothed_cov, length)
+    smoothed, shown, total, previous, lagged = scanned(
+        core[None].astype(jnp.int32), position[None].astype(jnp.int32), own, other, ready,
+        transition.T, filter_cov.T, smoothed_cov, length, lax.axis_size(TM),
     )
-    inverse, new_transition = inverted(total, previous, lagged)
     cross = jnp.einsum(
         "ts,tk->sk", observations, smoothed.astype(bf16), preferred_element_type=f32
     )
-    new_loadings = jnp.dot(cross, inverse, precision=precise, preferred_element_type=f32)
-    steps_dev = length // lax.axis_size(TM)
-    shown = lax.dynamic_slice_in_dim(smoothed, position * steps_dev, steps_dev, 0)
+    new_loadings, new_transition = inverted(total, previous, lagged, cross)
     return (shown, new_loadings, new_transition)
 
 

time: 112 us -> 101 us (0.902)
  Pallas kernels: 34.6 us -> 26.4 us
  waiting for transfers between devices: 10.5 us -> 8.28 us
    pallas_call x1 -> x2, Pallas kernels: 12.4 us -> 7.04 us  [the longest x1 4.37 us: inverted(): pl.pallas_call(inverse_kernel, out_shape=(jax.ShapeDtypeStruct(cross.shap...]
    pallas_call x1, Pallas kernels: 22.2 us -> 19.3 us  [scanned(): pl.pallas_call(scan_kernel, out_shape=(jax.ShapeDtypeStruct((length, n),...]
    ppermute x6, waiting for transfers between devices: 8.78 us -> 6.58 us  [turned(): lax.ppermute(value, axis, [(i, (i + steps) % count) for i in range(count)])]
  transfers between devices with their start and end apart: 7 -> 7, of which waited for: 5 -> 4; matrix products, arithmetic and copies ran while one was open for 1% -> 1% of each run, Pallas kernels for 0% -> 3%
where the time goes in v2:
time: 101 us; the launch traced here: 100 us
  blocking collectives  39 us (39%)
  Pallas kernels  26.4 us (26%)
  starting transfers between devices  19.3 us (19%)
  waiting for transfers between devices  8.28 us (8%)
  matrix products  4.48 us (4%)
  local copies, waits for them, and re-layouts  1.93 us (2%)
    all_to_all x1, blocking collectives, local(): lax.all_to_all(pieces, (Y, X), split_axis=0, concat_axis=0, tiled=True)  21.8 us
    pallas_call x1, Pallas kernels, scanned(): pl.pallas_call(scan_kernel, out_shape=(jax.ShapeDtypeStruct((length, n),...  19.3 us
    ppermute x6, starting transfers between devices, turned(): lax.ppermute(value, axis, [(i, (i + steps) % count) for i in range(count)])  17.6 us
    all_to_all x1, blocking collectives, local(): lax.all_to_all(copies, (Y, X), split_axis=0, concat_axis=0, tiled=True)  17.2 us
    ppermute x6, waiting for transfers between devices, turned(): lax.ppermute(value, axis, [(i, (i + steps) % count) for i in range(count)])  6.58 us
    pallas_call x1, Pallas kernels, inverted(): pl.pallas_call(inverse_kernel, out_shape=(jax.ShapeDtypeStruct(cross.shap...  4.37 us
    dot_general x2, matrix products, projected(): return jnp.dot(window, scaled, preferred_element_type=f32)  3.12 us
    pallas_call x1, Pallas kernels, readied(): pl.pallas_call(ready_kernel, out_shape=(jax.ShapeDtypeStruct((count, n, 2...  2.67 us
  transfers between devices with their start and end apart: 7, of which 4 were waited for; matrix products, arithmetic and copies ran while one was open for 1% of the time, Pallas kernels for 3%

profile of v2, /device:TPU:1, one launch (start us, length us, event | category | flops | bytes accessed | tf_op | source)
XLA Modules:
  0.0 100.4 jit_solution(3066200026094416954)
XLA Ops:
  0.6 0.0 copy-start
  0.7 1.6 %copy-done = bf16[4096,256]{1,0:T(8,128)(2,1)S(1)} copy-done((bf16[4096,256]{1,0:T(8,128)(2,1)S(1)}, bf16[4096,256]{1,0:T(8,128)(2,1)}, u32[]{:S(2)}) %copy-start) | copy-done | bytes 2097176
  2.2 1.4 %fusion.1 = f32[2048,128]{1,0:T(8,128)S(1)} fusion(bf16[4096,256]{1,0:T(8,128)(2,1)S(1)} %copy-done, s32[]{:T(128)S(6)} %select_n.7, f32[256,128]{1,0:T(8,128)} %param.8, f32[256]{0:T(256)} %param.9), kind=kOutput, calls=%fused_computation.5 | convolution fusion | flops 134283264 | bytes 2229252 | tf_op jit(solution)/shard_map/dot_general | solution.py:352
  3.6 3.3 %collective-permute-start = (f32[2048,128]{1,0:T(8,128)S(1)}, f32[2048,128]{1,0:T(8,128)}, u32[]{:S(2)}, u32[]{:S(2)}) collective-permute-start(f32[2048,128]{1,0:T(8,128)S(1)} %fusion.1), channel_id=1, source_target_pairs={{0,8},{8,0},{1,9},{9,1},{2,10},{10,2},{3,11},{11,3},{4,12},{12,4},... | collective-permute-start | bytes 3145736 | tf_op jit(solution)/shard_map/ppermute | solution.py:326
  7.0 0.4 convolution_bitcast_fusion.1
  7.4 0.1 collective-permute-start.1
  7.5 1.8 %collective-permute-done.1 = f32[128,128]{1,0:T(8,128)S(1)} collective-permute-done((f32[128,128]{1,0:T(8,128)S(1)}, f32[128,128]{1,0:T(8,128)S(1)}, u32[]{:S(2)}, u32[]{:S(2)}) %collective-permute-start.1) | collective-permute-done | bytes 65568 | tf_op jit(solution)/shard_map/ppermute | solution.py:326
  9.3 0.0 collective-permute-done
  9.4 1.7 %convolution_add_fusion = f32[2048,128]{1,0:T(8,128)S(1)} fusion(f32[2048,128]{1,0:T(8,128)} %collective-permute-done, bf16[4096,256]{1,0:T(8,128)(2,1)S(1)} %copy-done, s32[]{:T(128)S(6)} %select_n.6, f32[256,128]{1,0:T(8,128)S(1)} %copy-done.2, f32[256]{0:T(256)S(1)} %copy-done.6), kind=kOutput, calls=%fused_computation | convolution fusion | flops 134545408 | bytes 3277828 | tf_op jit(solution)/shard_map/dot_general | solution.py:352
  11.1 0.1 pad_maximum_fusion
  11.2 21.8 %all_to_all.10 = f32[16,136,128]{2,1,0:T(8,128)S(1)} all-to-all(f32[16,136,128]{2,1,0:T(8,128)S(1)} %pad_maximum_fusion), channel_id=1, replica_groups=mesh['tm_0'=4,'tm_1'=4,'tm_2'=2,'sr'=8] {'tm_0','tm_1'}, dimensions={0} | all-to-all | bytes 2228224 | tf_op jit(solution)/shard_map/all_to_all | solution.py:360
  33.0 0.1 reduce_sum.9
  33.1 0.0 copy-start.4
  33.1 0.0 copy-start.5
  33.1 1.7 %collective-permute-start.2 = (f32[136,128]{1,0:T(8,128)S(1)}, f32[136,128]{1,0:T(8,128)S(1)}, u32[]{:S(2)}, u32[]{:S(2)}) collective-permute-start(f32[136,128]{1,0:T(8,128)S(1)} %reduce_sum.9), channel_id=1, source_target_pairs={{0,1},{1,0},{2,3},{3,2},{4,5},{5,4},{6,7},{7,6},{8,9},{9,8},{10,11... | collective-permute-start | bytes 208904 | tf_op jit(solution)/shard_map/ppermute | solution.py:331
  34.9 1.7 %collective-permute-done.2 = f32[136,128]{1,0:T(8,128)S(1)} collective-permute-done((f32[136,128]{1,0:T(8,128)S(1)}, f32[136,128]{1,0:T(8,128)S(1)}, u32[]{:S(2)}, u32[]{:S(2)}) %collective-permute-start.2) | collective-permute-done | bytes 69664 | tf_op jit(solution)/shard_map/ppermute | solution.py:331
  36.6 0.0 copy-start.1
  36.6 5.9 %collective-permute-start.5 = (f32[136,128]{1,0:T(8,128)S(1)}, f32[136,128]{1,0:T(8,128)S(1)}, u32[]{:S(2)}, u32[]{:S(2)}) collective-permute-start(f32[136,128]{1,0:T(8,128)S(1)} %add.36), channel_id=1, source_target_pairs={{0,6},{1,7},{2,0},{3,1},{4,2},{5,3},{6,4},{7,5},{8,14},{9,15},{10,... | collective-permute-start | bytes 208904 | tf_op jit(solution)/shard_map/ppermute | solution.py:326
  42.5 1.0 %collective-permute-start.4 = (f32[136,128]{1,0:T(8,128)S(1)}, f32[136,128]{1,0:T(8,128)S(1)}, u32[]{:S(2)}, u32[]{:S(2)}) collective-permute-start(f32[136,128]{1,0:T(8,128)S(1)} %add.36), channel_id=1, source_target_pairs={{0,4},{1,5},{2,6},{3,7},{4,0},{5,1},{6,2},{7,3},{8,12},{9,13},{10,... | collective-permute-start | bytes 208904 | tf_op jit(solution)/shard_map/ppermute | solution.py:326
  43.5 2.3 %collective-permute-start.3 = (f32[136,128]{1,0:T(8,128)S(1)}, f32[136,128]{1,0:T(8,128)S(1)}, u32[]{:S(2)}, u32[]{:S(2)}) collective-permute-start(f32[136,128]{1,0:T(8,128)S(1)} %add.36), channel_id=1, source_target_pairs={{0,2},{1,3},{2,4},{3,5},{4,6},{5,7},{6,0},{7,1},{8,10},{9,11},{10,... | collective-permute-start | bytes 208904 | tf_op jit(solution)/shard_map/ppermute | solution.py:326
  45.8 4.0 %collective-permute-done.4 = f32[136,128]{1,0:T(8,128)S(1)} collective-permute-done((f32[136,128]{1,0:T(8,128)S(1)}, f32[136,128]{1,0:T(8,128)S(1)}, u32[]{:S(2)}, u32[]{:S(2)}) %collective-permute-start.4) | collective-permute-done | bytes 69664 | tf_op jit(solution)/shard_map/ppermute | solution.py:326
  49.8 0.7 collective-permute-done.3
  50.5 0.1 broadcast_in_dim.12
  50.6 17.2 %all_to_all.11.own_ref = f32[16,136,128]{2,1,0:T(8,128)S(1)} all-to-all(f32[16,136,128]{2,1,0:T(8,128)S(1)} %broadcast_in_dim.12), channel_id=1, replica_groups=mesh['tm_0'=4,'tm_1'=4,'tm_2'=2,'sr'=8] {'tm_0','tm_1'}, dimensions={0} | all-to-all | bytes 2228224 | tf_op jit(solution)/shard_map/all_to_all | solution.py:363
  67.8 4.9 %collective-permute-start.6 = (f32[16,136,128]{2,1,0:T(8,128)S(1)}, f32[16,136,128]{2,1,0:T(8,128)}, u32[]{:S(2)}, u32[]{:S(2)}) collective-permute-start(f32[16,136,128]{2,1,0:T(8,128)S(1)} %all_to_all.11.own_ref), channel_id=1, source_target_pairs={{0,8},{8,0},{1,9},{9,1},{2,10},{10,2},{3,11},{11,3},{4,12},{12,4},... | collective-permute-start | bytes 3342344 | tf_op jit(solution)/shard_map/ppermute | solution.py:326
  72.7 0.1 copy.10
  72.8 0.1 copy.11
  72.9 0.1 copy.12
  73.0 2.7 %ready.1 = (bf16[18,128,256]{2,1,0:T(8,128)(2,1)S(1)}, bf16[18,128,128]{2,1,0:T(8,128)(2,1)S(1)}, f32[128,128]{1,0:T(8,128)S(1)}) custom-call(f32[128,128]{1,0:T(8,128)S(1)} %bitcast.14, f32[128,128]{1,0:T(8,128)S(1)} %bitcast.16, f32[128,128]{1,0:T(8,128)S(1)} %bitcast.18, f32[128,128]{1,0:T(8,128)S(1)} %copy-done.1), custom_call_target="tpu_custom_call" | custom-call | flops 1000000000 | bytes 2000000 | tf_op jit(solution)/shard_map/ready/pallas_call | solution.py:123
  75.7 19.3 %scan.1 = (f32[4096,128]{1,0:T(8,128)S(1)}, f32[128,128]{1,0:T(8,128)}, f32[128,128]{1,0:T(8,128)S(1)}, f32[128,128]{1,0:T(8,128)S(1)}, f32[128,128]{1,0:T(8,128)S(1)}) custom-call(s32[1]{0:T(128)} %bitcast.core_ref, s32[1]{0:T(128)} %bitcast.1.place_ref, f32[16,136,128]{2,1,0:T(8,128)S(1)} %all_to_all.11.own_ref, ...), custom_call_target="tpu_custom_call" | custom-call | flops 10000000000 | bytes 5000000 | tf_op jit(solution)/shard_map/scan/pallas_call | solution.py:229
  95.1 0.9 convolution_bitcast_fusion.cross_ref
  96.0 4.4 %inverse.1 = (f32[256,128]{1,0:T(8,128)}, f32[128,128]{1,0:T(8,128)}) custom-call(f32[128,128]{1,0:T(8,128)S(1)} %get-tuple-element.17.total_ref, f32[128,128]{1,0:T(8,128)S(1)} %get-tuple-element.18.previous_ref, f32[128,128]{1,0:T(8,128)S(1)} %get-tuple-element.19.lagged_ref, f32[256,128]{1,0:T(8,128)S(1)} %convolution_bitcast_fusion.cross_ref), custom_call_target="tpu_custom_call" | custom-call | flops 1000000000 | bytes 600000 | tf_op jit(solution)/shard_map/inverse/pallas_call | solution.py:312
  (14 shorter events, 0.1 us)
Async XLA Ops:
  0.6 1.6 %copy-start = (bf16[4096,256]{1,0:T(8,128)(2,1)S(1)}, bf16[4096,256]{1,0:T(8,128)(2,1)}, u32[]{:S(2)}) copy-start(bf16[4096,256]{1,0:T(8,128)(2,1)} %param.7) | copy-start | bytes 6291460
  0.6 6.3 %copy-start.6 = (f32[256]{0:T(256)S(1)}, f32[256]{0:T(256)}, u32[]{:S(2)}) copy-start(f32[256]{0:T(256)} %param.9) | copy-start | bytes 3076
  0.7 6.3 %copy-start.2 = (f32[256,128]{1,0:T(8,128)S(1)}, f32[256,128]{1,0:T(8,128)}, u32[]{:S(2)}) copy-start(f32[256,128]{1,0:T(8,128)} %param.8) | copy-start | bytes 393220
  3.6 5.7 %collective-permute-start = (f32[2048,128]{1,0:T(8,128)S(1)}, f32[2048,128]{1,0:T(8,128)}, u32[]{:S(2)}, u32[]{:S(2)}) collective-permute-start(f32[2048,128]{1,0:T(8,128)S(1)} %fusion.1), channel_id=1, source_target_pairs={{0,8},{8,0},{1,9},{9,1},{2,10},{10,2},{3,11},{11,3},{4,12},{12,4},... | collective-permute-start | bytes 3145736 | tf_op jit(solution)/shard_map/ppermute | solution.py:326
  7.4 1.9 %collective-permute-start.1 = (f32[128,128]{1,0:T(8,128)S(1)}, f32[128,128]{1,0:T(8,128)S(1)}, u32[]{:S(2)}, u32[]{:S(2)}) collective-permute-start(f32[128,128]{1,0:T(8,128)S(1)} %convolution_bitcast_fusion.1), channel_id=1, source_target_pairs={{0,8},{8,0},{1,9},{9,1},{2,10},{10,2},{3,11},{11,3},{4,12},{12,4},... | collective-permute-start | bytes 196616 | tf_op jit(solution)/shard_map/ppermute | solution.py:326
  33.1 39.6 %copy-start.3 = (f32[128,128]{1,0:T(8,128)S(1)}, f32[128,128]{1,0:T(8,128)}, u32[]{:S(2)}) copy-start(f32[128,128]{1,0:T(8,128)} %param.10) | copy-start | bytes 196612
  33.1 39.7 %copy-start.4 = (f32[128,128]{1,0:T(8,128)S(1)}, f32[128,128]{1,0:T(8,128)}, u32[]{:S(2)}) copy-start(f32[128,128]{1,0:T(8,128)} %param.11) | copy-start | bytes 196612
  33.1 39.8 %copy-start.5 = (f32[128,128]{1,0:T(8,128)S(1)}, f32[128,128]{1,0:T(8,128)}, u32[]{:S(2)}) copy-start(f32[128,128]{1,0:T(8,128)} %param.12) | copy-start | bytes 196612
  33.1 3.4 %collective-permute-start.2 = (f32[136,128]{1,0:T(8,128)S(1)}, f32[136,128]{1,0:T(8,128)S(1)}, u32[]{:S(2)}, u32[]{:S(2)}) collective-permute-start(f32[136,128]{1,0:T(8,128)S(1)} %reduce_sum.9), channel_id=1, source_target_pairs={{0,1},{1,0},{2,3},{3,2},{4,5},{5,4},{6,7},{7,6},{8,9},{9,8},{10,11... | collective-permute-start | bytes 208904 | tf_op jit(solution)/shard_map/ppermute | solution.py:331
  36.6 36.5 %copy-start.1 = (f32[128,128]{1,0:T(8,128)S(1)}, f32[128,128]{1,0:T(8,128)}, u32[]{:S(2)}) copy-start(f32[128,128]{1,0:T(8,128)} %cov_ref.3) | copy-start | bytes 196612
  36.6 9.2 %collective-permute-start.5 = (f32[136,128]{1,0:T(8,128)S(1)}, f32[136,128]{1,0:T(8,128)S(1)}, u32[]{:S(2)}, u32[]{:S(2)}) collective-permute-start(f32[136,128]{1,0:T(8,128)S(1)} %add.36), channel_id=1, source_target_pairs={{0,6},{1,7},{2,0},{3,1},{4,2},{5,3},{6,4},{7,5},{8,14},{9,15},{10,... | collective-permute-start | bytes 208904 | tf_op jit(solution)/shard_map/ppermute | solution.py:326
  42.5 7.3 %collective-permute-start.4 = (f32[136,128]{1,0:T(8,128)S(1)}, f32[136,128]{1,0:T(8,128)S(1)}, u32[]{:S(2)}, u32[]{:S(2)}) collective-permute-start(f32[136,128]{1,0:T(8,128)S(1)} %add.36), channel_id=1, source_target_pairs={{0,4},{1,5},{2,6},{3,7},{4,0},{5,1},{6,2},{7,3},{8,12},{9,13},{10,... | collective-permute-start | bytes 208904 | tf_op jit(solution)/shard_map/ppermute | solution.py:326
  43.5 7.0 %collective-permute-start.3 = (f32[136,128]{1,0:T(8,128)S(1)}, f32[136,128]{1,0:T(8,128)S(1)}, u32[]{:S(2)}, u32[]{:S(2)}) collective-permute-start(f32[136,128]{1,0:T(8,128)S(1)} %add.36), channel_id=1, source_target_pairs={{0,2},{1,3},{2,4},{3,5},{4,6},{5,7},{6,0},{7,1},{8,10},{9,11},{10,... | collective-permute-start | bytes 208904 | tf_op jit(solution)/shard_map/ppermute | solution.py:326
  67.8 7.9 %collective-permute-start.6 = (f32[16,136,128]{2,1,0:T(8,128)S(1)}, f32[16,136,128]{2,1,0:T(8,128)}, u32[]{:S(2)}, u32[]{:S(2)}) collective-permute-start(f32[16,136,128]{2,1,0:T(8,128)S(1)} %all_to_all.11.own_ref), channel_id=1, source_target_pairs={{0,8},{8,0},{1,9},{9,1},{2,10},{10,2},{3,11},{11,3},{4,12},{12,4},... | collective-permute-start | bytes 3342344 | tf_op jit(solution)/shard_map/ppermute | solution.py:326

commit v3 on v2

--- a/solution.py
+++ b/solution.py
@@ -12,6 +12,7 @@
 
 STEPS = 8
 SQUARINGS = 7
+FIRST = 4
 f32 = jnp.float32
 bf16 = jnp.bfloat16
 precise = lax.Precision.HIGHEST
@@ -107,10 +108,12 @@
     put(0, kt)
     put(1, eye - high(ft, jt))
     raised = powers(jt, n)
+    put(2, ft)
+    put(3, high(ft, raised[-1]))
     for k, w in enumerate(raised):
-        put(2 + k, w)
+        put(FIRST + k, w)
     power = raised[-1]
-    for k in range(STEPS + 2, both_ref.shape[0]):
+    for k in range(FIRST + STEPS, both_ref.shape[0]):
         power = high(power, power)
         put(k, power)
     drift_ref[...] = high(cov_ref[...], jt)
@@ -118,7 +121,7 @@
 
 def readied(ft, kt, jt, cov, length):
     n = ft.shape[0]
-    count = 2 + STEPS + (length // STEPS).bit_length() - 2
+    count = FIRST + STEPS + (length // STEPS).bit_length() - 2
     vmem = pl.BlockSpec(memory_space=pltpu.VMEM)
     return pl.pallas_call(
         ready_kernel,
@@ -136,7 +139,7 @@
 
 
 def scan_kernel(
-    core_ref, place_ref, own_ref, other_ref, both_ref, small_ref, ft_ref, kt_ref, cov_ref, drift_ref,
+    core_ref, place_ref, own_ref, other_ref, both_ref, small_ref, ft_ref, cov_ref, drift_ref,
     x_ref, shown_ref, total_ref, previous_ref, lagged_ref, loc_ref, mat_ref,
 ):
     n = ft_ref.shape[0]
@@ -145,12 +148,12 @@
     rows = length // (2 * groups)
     blocks = length // STEPS
     first = core_ref[0] == 0
-    ft, cov = ft_ref[...], cov_ref[...]
+    cov = cov_ref[...]
     held = lambda k: (both_ref[k], small_ref[k])
-    info = jnp.concatenate([own_ref[g, rows:] for g in range(groups)], axis=0)
+    info = jnp.concatenate([own_ref[g, rows:] + other_ref[g, rows:] for g in range(groups)], axis=0)
     row = lax.broadcasted_iota(jnp.int32, (blocks, n), 0)
-    a = ft - times(high(ft, info), kept(held(0)))
-    apow = powers(a, n)
+    levels = blocks.bit_length() - 1
+    a = ft_ref[...] - times(high(ft_ref[...], info), kept(held(0)))
 
     def drive(j):
         def half(ref):
@@ -162,14 +165,25 @@
             [jnp.where(first, own, other), jnp.where(first, other, own)], axis=0
         )
 
+    apow, leaps = [a], []
     step = kept(beneath(pieces_of(a), held(0)), 2)
     state = times(drive(0), kept(held(0)))
     loc_ref[0] = state
     for j in range(1, STEPS):
         state = times(jnp.concatenate([state, drive(j)], axis=1), step)
         loc_ref[j] = state
+        if len(apow) < STEPS:
+            more = high(jnp.concatenate(apow, axis=0), apow[-1])
+            apow = apow + [more[i * n : (i + 1) * n] for i in range(len(apow))]
+            if len(apow) == STEPS:
+                leap = apow[-1]
+                leaps.append(right(leap))
+        elif len(leaps) < levels:
+            leap = times(leap, leaps[-1])
+            leaps.append(right(leap))
     enter = state
-    back = kept(beneath(held(2), held(1)), 2)
+    level = 0
+    back = kept(beneath(held(FIRST), held(1)), 2)
     both = lambda j: jnp.concatenate([loc_ref[j], apow[j]], axis=0)
     out = times(both(STEPS - 1), kept(held(1)))
     for j in range(STEPS - 1, -1, -1):
@@ -177,40 +191,49 @@
             out = times(jnp.concatenate([out, both(j)], axis=1), back)
         loc_ref[j] = out[:blocks]
         mat_ref[j] = out[blocks:]
-    power, shift = apow[STEPS - 1], 1
-    while shift < blocks:
-        w = right(power)
-        enter = enter + times(moved(enter, shift, row), w)
-        shift *= 2
-        if shift < blocks:
-            power = times(power, w)
+        if level < levels:
+            if len(leaps) < levels:
+                leap = times(leap, leaps[-1])
+                leaps.append(right(leap))
+            enter = enter + times(moved(enter, 1 << level, row), leaps[level])
+            level += 1
+    while level < levels:
+        if len(leaps) < levels:
+            leap = times(leap, leaps[-1])
+            leaps.append(right(leap))
+        enter = enter + times(moved(enter, 1 << level, row), leaps[level])
+        level += 1
     e = moved(enter, 1, row)
-    after = high(jnp.where(row == blocks - 1, enter, 0.0), ft)
-    z = loc_ref[0] + high(e, mat_ref[0]) + times(after, kept(held(1 + STEPS)))
-    level, shift = 1 + STEPS, 1
-    while shift < blocks:
-        z = z + times(moved(z, -shift, row), kept(held(level)))
-        shift *= 2
-        level += 1
-    mix = jnp.concatenate([e, moved(z, -1, row) + after], axis=1)
-    mixed = thirds(mix)
-    for j in range(STEPS):
-        x = z
-        if j > 0:
-            w = kept(beneath(pieces_of(mat_ref[j]), held(1 + STEPS - j)), 2)
-            x = loc_ref[j] + times_split(mixed, w)
-        loc_ref[j] = x
-        x_ref[pl.ds(j, blocks, stride=STEPS), :] = x
+    tail = lax.broadcasted_iota(jnp.int32, (8, n), 0) == 7
+    final = jnp.where(tail, enter[blocks - 8 :], 0.0)
+    after = times(final, kept(held(2)))
+    z = loc_ref[0] + high(e, mat_ref[0])
+    z = jnp.concatenate([z[: blocks - 8], z[blocks - 8 :] + times(final, kept(held(3)))], axis=0)
+    for level in range(levels):
+        z = z + times(moved(z, -(1 << level), row), kept(held(FIRST + STEPS - 1 + level)))
+    coming = moved(z, -1, row)
+    coming = jnp.concatenate([coming[: blocks - 8], coming[blocks - 8 :] + after], axis=0)
+    mixed = thirds(jnp.concatenate([e, coming], axis=1))
     sums = jnp.zeros((n, 2 * n), f32)
-    for j in range(STEPS):
-        x = loc_ref[j]
-        prior = moved(loc_ref[STEPS - 1], 1, row) if j == 0 else loc_ref[j - 1]
-        xa, xb, _ = thirds(x)
-        pa, pb, _ = thirds(prior)
+
+    def outer(x, prior):
+        xa, xb = x
+        pa, pb = prior
         pair = jnp.concatenate([xa, pa], axis=1)
         rest = jnp.concatenate([xb, pb], axis=1)
-        sums = sums + contracted(xa, pair) + (contracted(xb, pair) + contracted(xa, rest))
-    last = jnp.where(lax.broadcasted_iota(jnp.int32, (8, n), 0) == 7, x_ref[length - 8 :], 0.0)
+        return contracted(xa, pair) + (contracted(xb, pair) + contracted(xa, rest))
+
+    opening = prior = thirds(z)[:2]
+    x_ref[pl.ds(0, blocks, stride=STEPS), :] = z
+    for j in range(1, STEPS):
+        w = kept(beneath(pieces_of(mat_ref[j]), held(FIRST + STEPS - 1 - j)), 2)
+        x = loc_ref[j] + times_split(mixed, w)
+        x_ref[pl.ds(j, blocks, stride=STEPS), :] = x
+        here = thirds(x)[:2]
+        sums = sums + outer(here, prior)
+        prior = here
+    sums = sums + outer(opening, thirds(moved(x, 1, row))[:2])
+    last = jnp.where(tail, x_ref[length - 8 :], 0.0)
     la, lb, _ = thirds(last)
     ends = contracted(la, la) + (contracted(lb, la) + contracted(la, lb))
     total_ref[...] = sums[:, :n] + length * cov
@@ -220,7 +243,7 @@
     shown_ref[...] = x_ref[pl.ds(pl.multiple_of(place_ref[0] * count, count), count), :]
 
 
-def scanned(core, place, own, other, ready, ft, kt, cov, length, parts):
+def scanned(core, place, own, other, ready, ft, cov, length, parts):
     both, small, drift = ready
     n = ft.shape[0]
     square = jax.ShapeDtypeStruct((n, n), f32)
@@ -233,7 +256,7 @@
             jax.ShapeDtypeStruct((length // parts, n), f32),
             square, square, square,
         ),
-        in_specs=[smem] * 2 + [vmem] * 8,
+        in_specs=[smem] * 2 + [vmem] * 7,
         out_specs=[vmem] * 5,
         scratch_shapes=[
             pltpu.VMEM((STEPS, length // STEPS, n), f32),
@@ -242,7 +265,7 @@
         compiler_params=pltpu.CompilerParams(vmem_limit_bytes=44 * 1024 * 1024),
         cost_estimate=pl.CostEstimate(flops=10**10, bytes_accessed=5 * 10**6, transcendentals=0),
         name="scan",
-    )(core, place, own, other, both, small, ft, kt, cov, drift)
+    )(core, place, own, other, both, small, ft, cov, drift)
 
 
 def swept(mats, n):
@@ -321,6 +344,68 @@
     )(total, previous, lagged, cross)
 
 
+CHUNKS = 4
+
+
+def scaled_by(loadings, noise_row):
+    count, n = loadings.shape
+    noise = jnp.transpose(jnp.broadcast_to(noise_row, (n, count)))
+    return noise * loadings
+
+
+def project_kernel(start_ref, observations_ref, loadings_ref, noise_ref, out_ref, *rest):
+    window_ref, sem = rest[-2:]
+    chunk = out_ref.shape[0] // CHUNKS
+    start = pl.multiple_of(start_ref[0], out_ref.shape[0])
+
+    def copy(k):
+        rows = pl.ds(k * chunk, chunk)
+        there = pl.ds(start + k * chunk, chunk)
+        return pltpu.make_async_copy(
+            observations_ref.at[there, :], window_ref.at[rows, :], sem.at[k]
+        )
+
+    for k in range(CHUNKS):
+        copy(k).start()
+    loadings = loadings_ref[...]
+    weighted = scaled_by(loadings, noise_ref[...])
+    scaled = weighted.astype(bf16)
+    if len(rest) == 3:
+        a, b, c = thirds(loadings)
+        p, q, r = thirds(weighted)
+        pair = contracted(a, jnp.concatenate([p, q], axis=1))
+        other = contracted(b, jnp.concatenate([p, q], axis=1))
+        n = loadings.shape[1]
+        least = contracted(a, r) + contracted(c, p)
+        rest[0][...] = pair[:, :n] + (pair[:, n:] + other[:, :n] + (other[:, n:] + least))
+    for k in range(CHUNKS):
+        copy(k).wait()
+        rows = pl.ds(k * chunk, chunk)
+        out_ref[rows, :] = plain(window_ref[rows, :], scaled)
+
+
+def projected(observations, loadings, noise, start, with_info):
+    half, n = observations.shape[0] // 2, loadings.shape[1]
+    vmem = pl.BlockSpec(memory_space=pltpu.VMEM)
+    shapes = [jax.ShapeDtypeStruct((half, n), f32), jax.ShapeDtypeStruct((n, n), f32)]
+    count = 2 if with_info else 1
+    return pl.pallas_call(
+        project_kernel,
+        out_shape=tuple(shapes[:count]),
+        in_specs=[
+            pl.BlockSpec(memory_space=pltpu.SMEM), pl.BlockSpec(memory_space=pltpu.HBM), vmem, vmem
+        ],
+        out_specs=tuple([vmem] * count),
+        scratch_shapes=[
+            pltpu.VMEM((half, observations.shape[1]), bf16),
+            pltpu.SemaphoreType.DMA((CHUNKS,)),
+        ],
+        compiler_params=pltpu.CompilerParams(vmem_limit_bytes=62 * 1024 * 1024),
+        cost_estimate=pl.CostEstimate(flops=10**8, bytes_accessed=3 * 10**6, transcendentals=0),
+        name="project",
+    )(start[None].astype(jnp.int32), observations, loadings, noise[None, :])
+
+
 def turned(value, axis, steps):
     count = lax.axis_size(axis)
     return lax.ppermute(value, axis, [(i, (i + steps) % count) for i in range(count)])
@@ -329,7 +414,7 @@
 def over_z(value):
     count = lax.axis_size(Z)
     value = value + lax.ppermute(value, Z, [(i, i ^ 1) for i in range(count)])
-    arrived = [turned(value, Z, 2 * k) for k in range(1, count // 2)]
+    arrived = [turned(value, Z, k) for k in (2, count - 2, 4)]
     return sum(arrived, value)
 
 
@@ -344,16 +429,10 @@
     groups = lax.axis_size((Y, X))
     rows = half // groups
     extra = width // groups
-    weighted = noise_precision[:, None] * loadings
-    scaled = weighted.astype(bf16)
-
-    def projected(which):
-        window = lax.dynamic_slice_in_dim(observations, which * half, half, 0)
-        return jnp.dot(window, scaled, preferred_element_type=f32)
-
-    info_part = jnp.dot(loadings.T, weighted, precision=precise, preferred_element_type=f32)
-    info_part = info_part + turned(info_part, CORE, 1)
-    mine = projected(core) + turned(projected(1 - core), CORE, 1)
+    (given,) = projected(observations, loadings, noise_precision, (1 - core) * half, False)
+    taken = turned(given, CORE, 1)
+    mine, info_part = projected(observations, loadings, noise_precision, core * half, True)
+    mine = mine + taken
     pieces = jnp.concatenate(
         [mine.reshape(groups, rows, width), info_part.reshape(groups, extra, width)], axis=1
     )
@@ -365,7 +444,7 @@
     ready = readied(transition.T, filter_cov.T, smoother_gain.T, smoothed_cov, length)
     smoothed, shown, total, previous, lagged = scanned(
         core[None].astype(jnp.int32), position[None].astype(jnp.int32), own, other, ready,
-        transition.T, filter_cov.T, smoothed_cov, length, lax.axis_size(TM),
+        transition.T, smoothed_cov, length, lax.axis_size(TM),
     )
     cross = jnp.einsum(
         "ts,tk->sk", observations, smoothed.astype(bf16), preferred_element_type=f32

time: 101 us -> 98.2 us (0.972)
  Pallas kernels: 26.4 us -> 30.5 us
  matrix products: 4.48 us -> 0.92 us
  waiting for transfers between devices: 8.28 us -> 5.18 us
  local copies, waits for them, and re-layouts: 1.93 us -> 0.37 us
  other arithmetic: 0.18 us -> 1.54 us
    pallas_call x0 -> x2, Pallas kernels: none -> 8.02 us  [projected(): pl.pallas_call(project_kernel, out_shape=tuple(shapes[:count]), in_specs=...]
    pallas_call x1, Pallas kernels: 19.3 us -> 15.4 us  [scanned(): pl.pallas_call(scan_kernel, out_shape=(jax.ShapeDtypeStruct((length, n),...]
    dot_general x3 -> x0, matrix products: 3.56 us -> none  [the longest x2 3.12 us: projected(): return jnp.dot(window, scaled, preferred_element_type=f32)]
    ppermute x6 -> x5, waiting for transfers between devices: 6.58 us -> 3.48 us  [turned(): lax.ppermute(value, axis, [(i, (i + steps) % count) for i in range(count)])]
    unnamed x17 -> x15, local copies, waits for them, and re-layouts: 1.86 us -> 0.3 us
    add x0 -> x1, other arithmetic: none -> 1.36 us  [local(): mine = mine + taken]
    ppermute x6 -> x5, starting transfers between devices: 17.6 us -> 17.3 us  [turned(): lax.ppermute(value, axis, [(i, (i + steps) % count) for i in range(count)])]
  transfers between devices with their start and end apart: 7 -> 6, of which waited for: 4 -> 2; matrix products, arithmetic and copies ran while one was open for 1% -> 0% of each run, Pallas kernels for 3% -> 7%
where the time goes in v3:
time: 98.2 us; the launch traced here: 97.9 us
  blocking collectives  39.5 us (40%)
  Pallas kernels  30.5 us (31%)
  starting transfers between devices  19.1 us (19%)
  waiting for transfers between devices  5.18 us (5%)
  other arithmetic  1.54 us (2%)
    all_to_all x1, blocking collectives, local(): lax.all_to_all(pieces, (Y, X), split_axis=0, concat_axis=0, tiled=True)  22.5 us
    ppermute x5, starting transfers between devices, turned(): lax.ppermute(value, axis, [(i, (i + steps) % count) for i in range(count)])  17.3 us
    all_to_all x1, blocking collectives, local(): lax.all_to_all(copies, (Y, X), split_axis=0, concat_axis=0, tiled=True)  17 us
    pallas_call x1, Pallas kernels, scanned(): pl.pallas_call(scan_kernel, out_shape=(jax.ShapeDtypeStruct((length, n),...  15.4 us
    pallas_call x2, Pallas kernels, projected(): pl.pallas_call(project_kernel, out_shape=tuple(shapes[:count]), in_specs=...  8.02 us
    pallas_call x1, Pallas kernels, inverted(): pl.pallas_call(inverse_kernel, out_shape=(jax.ShapeDtypeStruct(cross.shap...  4.37 us
    ppermute x5, waiting for transfers between devices, turned(): lax.ppermute(value, axis, [(i, (i + steps) % count) for i in range(count)])  3.48 us
    pallas_call x1, Pallas kernels, readied(): pl.pallas_call(ready_kernel, out_shape=(jax.ShapeDtypeStruct((count, n, 2...  2.7 us
  transfers between devices with their start and end apart: 6, of which 2 were waited for; matrix products, arithmetic and copies ran while one was open for 0% of the time, Pallas kernels for 7%

profile of v3, /device:TPU:1, one launch (start us, length us, event | category | flops | bytes accessed | tf_op | source)
XLA Modules:
  0.0 97.9 jit_solution(68033862392569409)
XLA Ops:
  0.6 4.0 %project.3 = f32[2048,128]{1,0:T(8,128)} custom-call(s32[1]{0:T(128)} %bitcast.4.start_ref, bf16[4096,256]{1,0:T(8,128)(2,1)} %observations_ref.3, f32[256,128]{1,0:T(8,128)} %loadings_ref.3, f32[1,256]{1,0:T(1,128)} %bitcast.19), custom_call_target="tpu_custom_call" | custom-call | flops 100000000 | bytes 3000000 | tf_op jit(solution)/shard_map/project/pallas_call | solution.py:392
  4.7 3.3 %collective-permute-start = (f32[2048,128]{1,0:T(8,128)}, f32[2048,128]{1,0:T(8,128)S(1)}, u32[]{:S(2)}, u32[]{:S(2)}) collective-permute-start(f32[2048,128]{1,0:T(8,128)} %project.3), channel_id=1, source_target_pairs={{0,8},{8,0},{1,9},{9,1},{2,10},{10,2},{3,11},{11,3},{4,12},{12,4},... | collective-permute-start | bytes 3145736 | tf_op jit(solution)/shard_map/ppermute | solution.py:411
  8.0 4.0 %project.2 = (f32[2048,128]{1,0:T(8,128)}, f32[128,128]{1,0:T(8,128)}) custom-call(s32[1]{0:T(128)} %bitcast.2.start_ref, bf16[4096,256]{1,0:T(8,128)(2,1)} %observations_ref.3, f32[256,128]{1,0:T(8,128)} %loadings_ref.3, f32[1,256]{1,0:T(1,128)} %bitcast.20), custom_call_target="tpu_custom_call" | custom-call | flops 100000000 | bytes 3000000 | tf_op jit(solution)/shard_map/project/pallas_call | solution.py:392
  12.0 0.0 collective-permute-done
  12.0 0.0 copy-start.2
  12.0 1.4 %add.23 = f32[2048,128]{1,0:T(8,128)S(1)} add(f32[2048,128]{1,0:T(8,128)} %get-tuple-element.15, f32[2048,128]{1,0:T(8,128)S(1)} %collective-permute-done) | non-fusion elementwise | flops 262144 | bytes 3145728 | tf_op jit(solution)/shard_map/add | solution.py:435
  13.4 0.1 pad_maximum_fusion
  13.5 22.5 %all_to_all.10 = f32[16,136,128]{2,1,0:T(8,128)S(1)} all-to-all(f32[16,136,128]{2,1,0:T(8,128)S(1)} %pad_maximum_fusion), channel_id=1, replica_groups=mesh['tm_0'=4,'tm_1'=4,'tm_2'=2,'sr'=8] {'tm_0','tm_1'}, dimensions={0} | all-to-all | bytes 2228224 | tf_op jit(solution)/shard_map/all_to_all | solution.py:439
  36.0 0.1 reduce_sum.9
  36.1 1.7 %collective-permute-start.1 = (f32[136,128]{1,0:T(8,128)S(1)}, f32[136,128]{1,0:T(8,128)S(1)}, u32[]{:S(2)}, u32[]{:S(2)}) collective-permute-start(f32[136,128]{1,0:T(8,128)S(1)} %reduce_sum.9), channel_id=1, source_target_pairs={{0,1},{1,0},{2,3},{3,2},{4,5},{5,4},{6,7},{7,6},{8,9},{9,8},{10,11... | collective-permute-start | bytes 208904 | tf_op jit(solution)/shard_map/ppermute | solution.py:416
  37.8 1.7 %collective-permute-done.1 = f32[136,128]{1,0:T(8,128)S(1)} collective-permute-done((f32[136,128]{1,0:T(8,128)S(1)}, f32[136,128]{1,0:T(8,128)S(1)}, u32[]{:S(2)}, u32[]{:S(2)}) %collective-permute-start.1) | collective-permute-done | bytes 69664 | tf_op jit(solution)/shard_map/ppermute | solution.py:416
  39.5 6.8 %collective-permute-start.4 = (f32[136,128]{1,0:T(8,128)S(1)}, f32[136,128]{1,0:T(8,128)S(1)}, u32[]{:S(2)}, u32[]{:S(2)}) collective-permute-start(f32[136,128]{1,0:T(8,128)S(1)} %add.24), channel_id=1, source_target_pairs={{0,4},{1,5},{2,6},{3,7},{4,0},{5,1},{6,2},{7,3},{8,12},{9,13},{10,... | collective-permute-start | bytes 208904 | tf_op jit(solution)/shard_map/ppermute | solution.py:411
  46.3 0.0 collective-permute-start.3
  46.3 2.4 %collective-permute-start.2 = (f32[136,128]{1,0:T(8,128)S(1)}, f32[136,128]{1,0:T(8,128)S(1)}, u32[]{:S(2)}, u32[]{:S(2)}) collective-permute-start(f32[136,128]{1,0:T(8,128)S(1)} %add.24), channel_id=1, source_target_pairs={{0,2},{1,3},{2,4},{3,5},{4,6},{5,7},{6,0},{7,1},{8,10},{9,11},{10,... | collective-permute-start | bytes 208904 | tf_op jit(solution)/shard_map/ppermute | solution.py:411
  48.7 0.0 collective-permute-done.4
  48.7 3.5 %collective-permute-done.3 = f32[136,128]{1,0:T(8,128)S(1)} collective-permute-done((f32[136,128]{1,0:T(8,128)S(1)}, f32[136,128]{1,0:T(8,128)S(1)}, u32[]{:S(2)}, u32[]{:S(2)}) %collective-permute-start.3) | collective-permute-done | bytes 69664 | tf_op jit(solution)/shard_map/ppermute | solution.py:411
  52.2 0.0 collective-permute-done.2
  52.2 0.1 broadcast_in_dim.24
  52.3 0.0 copy-start.3
  52.3 0.0 copy-start.4
  52.3 0.0 copy-start.5
  52.3 0.0 copy-start
  52.3 17.0 %all_to_all.11.own_ref = f32[16,136,128]{2,1,0:T(8,128)S(1)} all-to-all(f32[16,136,128]{2,1,0:T(8,128)S(1)} %broadcast_in_dim.24), channel_id=1, replica_groups=mesh['tm_0'=4,'tm_1'=4,'tm_2'=2,'sr'=8] {'tm_0','tm_1'}, dimensions={0} | all-to-all | bytes 2228224 | tf_op jit(solution)/shard_map/all_to_all | solution.py:442
  69.3 4.8 %collective-permute-start.5 = (f32[16,136,128]{2,1,0:T(8,128)S(1)}, f32[16,136,128]{2,1,0:T(8,128)S(1)}, u32[]{:S(2)}, u32[]{:S(2)}) collective-permute-start(f32[16,136,128]{2,1,0:T(8,128)S(1)} %all_to_all.11.own_ref), channel_id=1, source_target_pairs={{0,8},{8,0},{1,9},{9,1},{2,10},{10,2},{3,11},{11,3},{4,12},{12,4},... | collective-permute-start | bytes 3342344 | tf_op jit(solution)/shard_map/ppermute | solution.py:411
  74.1 0.1 copy.10
  74.2 0.1 copy.11
  74.3 0.1 copy.12
  74.4 2.7 %ready.1 = (bf16[20,128,256]{2,1,0:T(8,128)(2,1)S(1)}, bf16[20,128,128]{2,1,0:T(8,128)(2,1)S(1)}, f32[128,128]{1,0:T(8,128)S(1)}) custom-call(f32[128,128]{1,0:T(8,128)S(1)} %bitcast.13, f32[128,128]{1,0:T(8,128)S(1)} %bitcast.15, f32[128,128]{1,0:T(8,128)S(1)} %bitcast.16, f32[128,128]{1,0:T(8,128)S(1)} %copy-done), custom_call_target="tpu_custom_call" | custom-call | flops 1000000000 | bytes 2000000 | tf_op jit(solution)/shard_map/ready/pallas_call | solution.py:126
  77.2 0.0 copy-start.1
  77.2 15.4 %scan.1 = (f32[4096,128]{1,0:T(8,128)S(1)}, f32[128,128]{1,0:T(8,128)}, f32[128,128]{1,0:T(8,128)S(1)}, f32[128,128]{1,0:T(8,128)S(1)}, f32[128,128]{1,0:T(8,128)S(1)}) custom-call(s32[1]{0:T(128)} %bitcast.core_ref, s32[1]{0:T(128)} %bitcast.1.place_ref, f32[16,136,128]{2,1,0:T(8,128)S(1)} %all_to_all.11.own_ref, ...), custom_call_target="tpu_custom_call" | custom-call | flops 10000000000 | bytes 5000000 | tf_op jit(solution)/shard_map/scan/pallas_call | solution.py:252
  92.6 0.9 convolution_bitcast_fusion.cross_ref
  93.5 4.4 %inverse.1 = (f32[256,128]{1,0:T(8,128)}, f32[128,128]{1,0:T(8,128)}) custom-call(f32[128,128]{1,0:T(8,128)S(1)} %get-tuple-element.21.total_ref, f32[128,128]{1,0:T(8,128)S(1)} %get-tuple-element.22.previous_ref, f32[128,128]{1,0:T(8,128)S(1)} %get-tuple-element.23.lagged_ref, f32[256,128]{1,0:T(8,128)S(1)} %convolution_bitcast_fusion.cross_ref), custom_call_target="tpu_custom_call" | custom-call | flops 1000000000 | bytes 600000 | tf_op jit(solution)/shard_map/inverse/pallas_call | solution.py:335
  (9 shorter events, 0.0 us)
Async XLA Ops:
  4.7 7.3 %collective-permute-start = (f32[2048,128]{1,0:T(8,128)}, f32[2048,128]{1,0:T(8,128)S(1)}, u32[]{:S(2)}, u32[]{:S(2)}) collective-permute-start(f32[2048,128]{1,0:T(8,128)} %project.3), channel_id=1, source_target_pairs={{0,8},{8,0},{1,9},{9,1},{2,10},{10,2},{3,11},{11,3},{4,12},{12,4},... | collective-permute-start | bytes 3145736 | tf_op jit(solution)/shard_map/ppermute | solution.py:411
  12.0 1.4 %copy-start.2 = (f32[128,128]{1,0:T(8,128)S(1)}, f32[128,128]{1,0:T(8,128)}, u32[]{:S(2)}) copy-start(f32[128,128]{1,0:T(8,128)} %get-tuple-element.16) | copy-start | bytes 196612
  36.1 3.4 %collective-permute-start.1 = (f32[136,128]{1,0:T(8,128)S(1)}, f32[136,128]{1,0:T(8,128)S(1)}, u32[]{:S(2)}, u32[]{:S(2)}) collective-permute-start(f32[136,128]{1,0:T(8,128)S(1)} %reduce_sum.9), channel_id=1, source_target_pairs={{0,1},{1,0},{2,3},{3,2},{4,5},{5,4},{6,7},{7,6},{8,9},{9,8},{10,11... | collective-permute-start | bytes 208904 | tf_op jit(solution)/shard_map/ppermute | solution.py:416
  39.5 9.2 %collective-permute-start.4 = (f32[136,128]{1,0:T(8,128)S(1)}, f32[136,128]{1,0:T(8,128)S(1)}, u32[]{:S(2)}, u32[]{:S(2)}) collective-permute-start(f32[136,128]{1,0:T(8,128)S(1)} %add.24), channel_id=1, source_target_pairs={{0,4},{1,5},{2,6},{3,7},{4,0},{5,1},{6,2},{7,3},{8,12},{9,13},{10,... | collective-permute-start | bytes 208904 | tf_op jit(solution)/shard_map/ppermute | solution.py:411
  46.3 5.8 %collective-permute-start.3 = (f32[136,128]{1,0:T(8,128)S(1)}, f32[136,128]{1,0:T(8,128)S(1)}, u32[]{:S(2)}, u32[]{:S(2)}) collective-permute-start(f32[136,128]{1,0:T(8,128)S(1)} %add.24), channel_id=1, source_target_pairs={{0,6},{1,7},{2,0},{3,1},{4,2},{5,3},{6,4},{7,5},{8,14},{9,15},{10,... | collective-permute-start | bytes 208904 | tf_op jit(solution)/shard_map/ppermute | solution.py:411
  46.3 5.8 %collective-permute-start.2 = (f32[136,128]{1,0:T(8,128)S(1)}, f32[136,128]{1,0:T(8,128)S(1)}, u32[]{:S(2)}, u32[]{:S(2)}) collective-permute-start(f32[136,128]{1,0:T(8,128)S(1)} %add.24), channel_id=1, source_target_pairs={{0,2},{1,3},{2,4},{3,5},{4,6},{5,7},{6,0},{7,1},{8,10},{9,11},{10,... | collective-permute-start | bytes 208904 | tf_op jit(solution)/shard_map/ppermute | solution.py:411
  52.3 21.8 %copy-start.3 = (f32[128,128]{1,0:T(8,128)S(1)}, f32[128,128]{1,0:T(8,128)}, u32[]{:S(2)}) copy-start(f32[128,128]{1,0:T(8,128)} %param.10) | copy-start | bytes 196612
  52.3 21.9 %copy-start.4 = (f32[128,128]{1,0:T(8,128)S(1)}, f32[128,128]{1,0:T(8,128)}, u32[]{:S(2)}) copy-start(f32[128,128]{1,0:T(8,128)} %param.11) | copy-start | bytes 196612
  52.3 22.0 %copy-start.5 = (f32[128,128]{1,0:T(8,128)S(1)}, f32[128,128]{1,0:T(8,128)}, u32[]{:S(2)}) copy-start(f32[128,128]{1,0:T(8,128)} %param.12) | copy-start | bytes 196612
  52.3 22.1 %copy-start = (f32[128,128]{1,0:T(8,128)S(1)}, f32[128,128]{1,0:T(8,128)}, u32[]{:S(2)}) copy-start(f32[128,128]{1,0:T(8,128)} %cov_ref.3) | copy-start | bytes 196612
  69.3 7.9 %collective-permute-start.5 = (f32[16,136,128]{2,1,0:T(8,128)S(1)}, f32[16,136,128]{2,1,0:T(8,128)S(1)}, u32[]{:S(2)}, u32[]{:S(2)}) collective-permute-start(f32[16,136,128]{2,1,0:T(8,128)S(1)} %all_to_all.11.own_ref), channel_id=1, source_target_pairs={{0,8},{8,0},{1,9},{9,1},{2,10},{10,2},{3,11},{11,3},{4,12},{12,4},... | collective-permute-start | bytes 3342344 | tf_op jit(solution)/shard_map/ppermute | solution.py:411
  77.2 15.4 %copy-start.1 = (bf16[4096,256]{1,0:T(8,128)(2,1)S(1)}, bf16[4096,256]{1,0:T(8,128)(2,1)}, u32[]{:S(2)}) copy-start(bf16[4096,256]{1,0:T(8,128)(2,1)} %observations_ref.3) | copy-start | bytes 6291460

commit v4 on v3

--- a/solution.py
+++ b/solution.py
@@ -1,6 +1,7 @@
 import jax
 import jax.numpy as jnp
 from jax import lax
+from jax.experimental.layout import Layout, with_layout_constraint
 from jax.experimental import pallas as pl
 from jax.experimental.pallas import tpu as pltpu
 from jax.sharding import Mesh
@@ -138,11 +139,36 @@
     )(ft, kt, jt, cov)
 
 
+def begin_kernel(own_ref, kt_ref, ft_ref, power_ref):
+    n = ft_ref.shape[0]
+    groups = own_ref.shape[0]
+    rows = own_ref.shape[1] - n // groups
+    info = jnp.concatenate([own_ref[g, rows:] for g in range(groups)], axis=0)
+    ft = ft_ref[...]
+    a = ft - high(high(ft, info), kt_ref[...])
+    for k, w in enumerate(powers(a, n)):
+        power_ref[k] = w
+
+
+def begun(own, kt, ft):
+    n = ft.shape[0]
+    vmem = pl.BlockSpec(memory_space=pltpu.VMEM)
+    return pl.pallas_call(
+        begin_kernel,
+        out_shape=jax.ShapeDtypeStruct((STEPS, n, n), f32),
+        in_specs=[vmem] * 3,
+        out_specs=vmem,
+        compiler_params=pltpu.CompilerParams(vmem_limit_bytes=16 * 1024 * 1024),
+        cost_estimate=pl.CostEstimate(flops=10**9, bytes_accessed=2 * 10**6, transcendentals=0),
+        name="begin",
+    )(own, kt, ft)
+
+
 def scan_kernel(
-    core_ref, place_ref, own_ref, other_ref, both_ref, small_ref, ft_ref, cov_ref, drift_ref,
+    core_ref, place_ref, own_ref, other_ref, both_ref, small_ref, power_ref, cov_ref, drift_ref,
     x_ref, shown_ref, total_ref, previous_ref, lagged_ref, loc_ref, mat_ref,
 ):
-    n = ft_ref.shape[0]
+    n = cov_ref.shape[0]
     groups = own_ref.shape[0]
     length = x_ref.shape[0]
     rows = length // (2 * groups)
@@ -150,10 +176,12 @@
     first = core_ref[0] == 0
     cov = cov_ref[...]
     held = lambda k: (both_ref[k], small_ref[k])
-    info = jnp.concatenate([own_ref[g, rows:] + other_ref[g, rows:] for g in range(groups)], axis=0)
     row = lax.broadcasted_iota(jnp.int32, (blocks, n), 0)
     levels = blocks.bit_length() - 1
-    a = ft_ref[...] - times(high(ft_ref[...], info), kept(held(0)))
+    apow = [power_ref[k] for k in range(STEPS)]
+    a = apow[0]
+    leap = apow[-1]
+    leaps = [right(leap)]
 
     def drive(j):
         def half(ref):
@@ -165,20 +193,13 @@
             [jnp.where(first, own, other), jnp.where(first, other, own)], axis=0
         )
 
-    apow, leaps = [a], []
     step = kept(beneath(pieces_of(a), held(0)), 2)
     state = times(drive(0), kept(held(0)))
     loc_ref[0] = state
     for j in range(1, STEPS):
         state = times(jnp.concatenate([state, drive(j)], axis=1), step)
         loc_ref[j] = state
-        if len(apow) < STEPS:
-            more = high(jnp.concatenate(apow, axis=0), apow[-1])
-            apow = apow + [more[i * n : (i + 1) * n] for i in range(len(apow))]
-            if len(apow) == STEPS:
-                leap = apow[-1]
-                leaps.append(right(leap))
-        elif len(leaps) < levels:
+        if len(leaps) < levels:
             leap = times(leap, leaps[-1])
             leaps.append(right(leap))
     enter = state
@@ -243,9 +264,9 @@
     shown_ref[...] = x_ref[pl.ds(pl.multiple_of(place_ref[0] * count, count), count), :]
 
 
-def scanned(core, place, own, other, ready, ft, cov, length, parts):
+def scanned(core, place, own, other, ready, power, cov, length, parts):
     both, small, drift = ready
-    n = ft.shape[0]
+    n = cov.shape[0]
     square = jax.ShapeDtypeStruct((n, n), f32)
     vmem = pl.BlockSpec(memory_space=pltpu.VMEM)
     smem = pl.BlockSpec(memory_space=pltpu.SMEM)
@@ -265,7 +286,7 @@
         compiler_params=pltpu.CompilerParams(vmem_limit_bytes=44 * 1024 * 1024),
         cost_estimate=pl.CostEstimate(flops=10**10, bytes_accessed=5 * 10**6, transcendentals=0),
         name="scan",
-    )(core, place, own, other, both, small, ft, cov, drift)
+    )(core, place, own, other, both, small, power, cov, drift)
 
 
 def swept(mats, n):
@@ -296,7 +317,7 @@
     return y[:, :n] + (y[:, n:] + plain(b, c))
 
 
-def inverse_kernel(total_ref, previous_ref, lagged_ref, cross_ref, loadings_ref, transition_ref, found_ref):
+def inverse_kernel(total_ref, previous_ref, lagged_ref, cross_ref, loadings_ref, transition_ref):
     n = total_ref.shape[0]
     eye = (
         lax.broadcasted_iota(jnp.int32, (n, n), 0) == lax.broadcasted_iota(jnp.int32, (n, n), 1)
@@ -313,20 +334,21 @@
             left[i] = three(left[i], left[i])
             near[i] = near[i] + three(near[i], left[i])
     size = jnp.zeros((1, 1), f32)
-    for i in range(2):
-        r = eye - high(mats[i], near[i])
-        found_ref[i] = near[i] + three(near[i], r)
+    for i, (taken_ref, out_ref) in enumerate(
+        ((cross_ref, loadings_ref), (lagged_ref, transition_ref))
+    ):
+        w = right(near[i])
+        r = eye - times(mats[i], w)
+        first = times(taken_ref[...], w)
+        out_ref[...] = first + three(first, r)
         square = jnp.sum(jnp.sum(r * r, axis=0, keepdims=True), axis=1, keepdims=True)
         size = jnp.maximum(size, square)
 
     @pl.when(jnp.logical_not(size[0, 0] < 1e-6))
     def _():
         one, two = swept([total_ref[...], previous_ref[...]], n)
-        found_ref[0] = one
-        found_ref[1] = two
-
-    loadings_ref[...] = high(cross_ref[...], found_ref[0])
-    transition_ref[...] = high(lagged_ref[...], found_ref[1])
+        loadings_ref[...] = high(cross_ref[...], one)
+        transition_ref[...] = high(lagged_ref[...], two)
 
 
 def inverted(total, previous, lagged, cross):
@@ -337,75 +359,12 @@
         out_shape=(jax.ShapeDtypeStruct(cross.shape, f32), square),
         in_specs=[vmem] * 4,
         out_specs=[vmem] * 2,
-        scratch_shapes=[pltpu.VMEM((2, *total.shape), f32)],
         compiler_params=pltpu.CompilerParams(vmem_limit_bytes=16 * 1024 * 1024),
         cost_estimate=pl.CostEstimate(flops=10**9, bytes_accessed=6 * 10**5, transcendentals=0),
         name="inverse",
     )(total, previous, lagged, cross)
 
 
-CHUNKS = 4
-
-
-def scaled_by(loadings, noise_row):
-    count, n = loadings.shape
-    noise = jnp.transpose(jnp.broadcast_to(noise_row, (n, count)))
-    return noise * loadings
-
-
-def project_kernel(start_ref, observations_ref, loadings_ref, noise_ref, out_ref, *rest):
-    window_ref, sem = rest[-2:]
-    chunk = out_ref.shape[0] // CHUNKS
-    start = pl.multiple_of(start_ref[0], out_ref.shape[0])
-
-    def copy(k):
-        rows = pl.ds(k * chunk, chunk)
-        there = pl.ds(start + k * chunk, chunk)
-        return pltpu.make_async_copy(
-            observations_ref.at[there, :], window_ref.at[rows, :], sem.at[k]
-        )
-
-    for k in range(CHUNKS):
-        copy(k).start()
-    loadings = loadings_ref[...]
-    weighted = scaled_by(loadings, noise_ref[...])
-    scaled = weighted.astype(bf16)
-    if len(rest) == 3:
-        a, b, c = thirds(loadings)
-        p, q, r = thirds(weighted)
-        pair = contracted(a, jnp.concatenate([p, q], axis=1))
-        other = contracted(b, jnp.concatenate([p, q], axis=1))
-        n = loadings.shape[1]
-        least = contracted(a, r) + contracted(c, p)
-        rest[0][...] = pair[:, :n] + (pair[:, n:] + other[:, :n] + (other[:, n:] + least))
-    for k in range(CHUNKS):
-        copy(k).wait()
-        rows = pl.ds(k * chunk, chunk)
-        out_ref[rows, :] = plain(window_ref[rows, :], scaled)
-
-
-def projected(observations, loadings, noise, start, with_info):
-    half, n = observations.shape[0] // 2, loadings.shape[1]
-    vmem = pl.BlockSpec(memory_space=pltpu.VMEM)
-    shapes = [jax.ShapeDtypeStruct((half, n), f32), jax.ShapeDtypeStruct((n, n), f32)]
-    count = 2 if with_info else 1
-    return pl.pallas_call(
-        project_kernel,
-        out_shape=tuple(shapes[:count]),
-        in_specs=[
-            pl.BlockSpec(memory_space=pltpu.SMEM), pl.BlockSpec(memory_space=pltpu.HBM), vmem, vmem
-        ],
-        out_specs=tuple([vmem] * count),
-        scratch_shapes=[
-            pltpu.VMEM((half, observations.shape[1]), bf16),
-            pltpu.SemaphoreType.DMA((CHUNKS,)),
-        ],
-        compiler_params=pltpu.CompilerParams(vmem_limit_bytes=62 * 1024 * 1024),
-        cost_estimate=pl.CostEstimate(flops=10**8, bytes_accessed=3 * 10**6, transcendentals=0),
-        name="project",
-    )(start[None].astype(jnp.int32), observations, loadings, noise[None, :])
-
-
 def turned(value, axis, steps):
     count = lax.axis_size(axis)
     return lax.ppermute(value, axis, [(i, (i + steps) % count) for i in range(count)])
@@ -414,7 +373,7 @@
 def over_z(value):
     count = lax.axis_size(Z)
     value = value + lax.ppermute(value, Z, [(i, i ^ 1) for i in range(count)])
-    arrived = [turned(value, Z, k) for k in (2, count - 2, 4)]
+    arrived = [turned(value, Z, 2 * k) for k in range(1, count // 2)]
     return sum(arrived, value)
 
 
@@ -429,22 +388,31 @@
     groups = lax.axis_size((Y, X))
     rows = half // groups
     extra = width // groups
-    (given,) = projected(observations, loadings, noise_precision, (1 - core) * half, False)
-    taken = turned(given, CORE, 1)
-    mine, info_part = projected(observations, loadings, noise_precision, core * half, True)
-    mine = mine + taken
+    weighted = noise_precision[:, None] * loadings
+    scaled = weighted.astype(bf16)
+
+    info_part = jnp.dot(loadings.T, weighted, precision=precise, preferred_element_type=f32)
+    info_part = info_part + turned(info_part, CORE, 1)
+    whole = jnp.dot(observations, scaled, preferred_element_type=f32)
+    whole = with_layout_constraint(whole, Layout(major_to_minor=(0, 1)))
+    given = lax.dynamic_slice_in_dim(whole, (1 - core) * half, half, 0)
+    mine = lax.dynamic_slice_in_dim(whole, core * half, half, 0)
+    given, mine = lax.optimization_barrier((given, mine))
+    mine = mine + turned(given, CORE, 1)
     pieces = jnp.concatenate(
         [mine.reshape(groups, rows, width), info_part.reshape(groups, extra, width)], axis=1
     )
     arrived = lax.all_to_all(pieces, (Y, X), split_axis=0, concat_axis=0, tiled=True)
     block = over_z(arrived.sum(axis=0))
+    ready = readied(transition.T, filter_cov.T, smoother_gain.T, smoothed_cov, length)
+    block, ready = lax.optimization_barrier((block, ready))
     copies = jnp.broadcast_to(block, (groups, *block.shape))
     own = lax.all_to_all(copies, (Y, X), split_axis=0, concat_axis=0, tiled=True)
     other = turned(own, CORE, 1)
-    ready = readied(transition.T, filter_cov.T, smoother_gain.T, smoothed_cov, length)
+    power = begun(own, filter_cov.T, transition.T)
     smoothed, shown, total, previous, lagged = scanned(
         core[None].astype(jnp.int32), position[None].astype(jnp.int32), own, other, ready,
-        transition.T, smoothed_cov, length, lax.axis_size(TM),
+        power, smoothed_cov, length, lax.axis_size(TM),
     )
     cross = jnp.einsum(
         "ts,tk->sk", observations, smoothed.astype(bf16), preferred_element_type=f32

time: 98.2 us -> 95.9 us (0.977)
  Pallas kernels: 30.5 us -> 24.4 us
  matrix products: 0.92 us -> 3.03 us
  local copies, waits for them, and re-layouts: 0.37 us -> 2.12 us
  other arithmetic: 1.54 us -> 0.34 us
    pallas_call x2 -> x1, Pallas kernels: 8.02 us -> 1.32 us  [begun(): pl.pallas_call(begin_kernel, out_shape=jax.ShapeDtypeStruct((STEPS, n, n)...]
    dot_general x0 -> x2, matrix products: none -> 2.1 us  [the longest x1 1.66 us: local(): whole = jnp.dot(observations, scaled, preferred_element_type=f32)]
    unnamed x15 -> x25, local copies, waits for them, and re-layouts: 0.3 us -> 1.9 us
    add x1, other arithmetic: 1.36 us -> 0.15 us  [local(): mine = mine + turned(given, CORE, 1)]
    ppermute x5 -> x6, waiting for transfers between devices: 3.48 us -> 4.38 us  [turned(): lax.ppermute(value, axis, [(i, (i + steps) % count) for i in range(count)])]
    ppermute x5 -> x6, starting transfers between devices: 17.3 us -> 18.2 us  [turned(): lax.ppermute(value, axis, [(i, (i + steps) % count) for i in range(count)])]
  transfers between devices with their start and end apart: 6 -> 7, of which waited for: 2 -> 5; matrix products, arithmetic and copies ran while one was open for 0% -> 1% of each run, Pallas kernels for 7% -> 4%
where the time goes in v4:
time: 95.9 us; the launch traced here: 95.6 us
  blocking collectives  39.2 us (41%)
  Pallas kernels  24.4 us (25%)
  starting transfers between devices  19.9 us (21%)
  waiting for transfers between devices  5.77 us (6%)
  matrix products  3.03 us (3%)
  local copies, waits for them, and re-layouts  2.12 us (2%)
    all_to_all x1, blocking collectives, local(): lax.all_to_all(pieces, (Y, X), split_axis=0, concat_axis=0, tiled=True)  22 us
    ppermute x6, starting transfers between devices, turned(): lax.ppermute(value, axis, [(i, (i + steps) % count) for i in range(count)])  18.2 us
    all_to_all x1, blocking collectives, local(): lax.all_to_all(copies, (Y, X), split_axis=0, concat_axis=0, tiled=True)  17.2 us
    pallas_call x1, Pallas kernels, scanned(): pl.pallas_call(scan_kernel, out_shape=(jax.ShapeDtypeStruct((length, n),...  16.3 us
    ppermute x6, waiting for transfers between devices, turned(): lax.ppermute(value, axis, [(i, (i + steps) % count) for i in range(count)])  4.38 us
    pallas_call x1, Pallas kernels, inverted(): pl.pallas_call(inverse_kernel, out_shape=(jax.ShapeDtypeStruct(cross.shap...  4.15 us
    pallas_call x1, Pallas kernels, readied(): pl.pallas_call(ready_kernel, out_shape=(jax.ShapeDtypeStruct((count, n, 2...  2.69 us
  transfers between devices with their start and end apart: 7, of which 5 were waited for; matrix products, arithmetic and copies ran while one was open for 1% of the time, Pallas kernels for 4%

profile of v4, /device:TPU:1, one launch (start us, length us, event | category | flops | bytes accessed | tf_op | source)
XLA Modules:
  0.0 95.6 jit_solution(3321823051575438996)
XLA Ops:
  0.6 0.0 copy-start
  0.7 1.6 %copy-done = bf16[4096,256]{1,0:T(8,128)(2,1)S(1)} copy-done((bf16[4096,256]{1,0:T(8,128)(2,1)S(1)}, bf16[4096,256]{1,0:T(8,128)(2,1)}, u32[]{:S(2)}) %copy-start) | copy-done | bytes 2097176
  2.2 1.7 %convolution_bitcast_fusion = f32[4096,128]{1,0:T(8,128)S(1)} fusion(bf16[4096,256]{1,0:T(8,128)(2,1)S(1)} %copy-done, f32[256,128]{1,0:T(8,128)} %param.8, f32[256]{0:T(256)} %param.9), kind=kOutput, calls=%fused_computation | convolution fusion | flops 268500992 | bytes 4326400 | tf_op jit(solution)/shard_map/dot_general | solution.py:396
  3.9 0.0 copy-start.10
  3.9 0.1 constant_dynamic-slice_fusion
  4.1 3.3 %collective-permute-start = (f32[2048,128]{1,0:T(8,128)S(1)}, f32[2048,128]{1,0:T(8,128)S(1)}, u32[]{:S(2)}, u32[]{:S(2)}) collective-permute-start(f32[2048,128]{1,0:T(8,128)S(1)} %get-tuple-element.20), channel_id=1, source_target_pairs={{0,8},{8,0},{1,9},{9,1},{2,10},{10,2},{3,11},{11,3},{4,12},{12,4},... | collective-permute-start | bytes 3145736 | tf_op jit(solution)/shard_map/ppermute | solution.py:370
  7.4 0.4 convolution_bitcast_fusion.2
  7.9 0.7 collective-permute-start.1
  8.6 1.2 %collective-permute-done.1 = f32[128,128]{1,0:T(8,128)S(1)} collective-permute-done((f32[128,128]{1,0:T(8,128)S(1)}, f32[128,128]{1,0:T(8,128)S(1)}, u32[]{:S(2)}, u32[]{:S(2)}) %collective-permute-start.1) | collective-permute-done | bytes 65568 | tf_op jit(solution)/shard_map/ppermute | solution.py:370
  9.8 0.2 add.34
  10.0 0.1 pad_maximum_fusion
  10.1 22.0 %all_to_all.10 = f32[16,136,128]{2,1,0:T(8,128)S(1)} all-to-all(f32[16,136,128]{2,1,0:T(8,128)S(1)} %pad_maximum_fusion), channel_id=1, replica_groups=mesh['tm_0'=4,'tm_1'=4,'tm_2'=2,'sr'=8] {'tm_0','tm_1'}, dimensions={0} | all-to-all | bytes 2228224 | tf_op jit(solution)/shard_map/all_to_all | solution.py:405
  32.1 0.1 reduce_sum.9
  32.1 1.7 %collective-permute-start.2 = (f32[136,128]{1,0:T(8,128)S(1)}, f32[136,128]{1,0:T(8,128)S(1)}, u32[]{:S(2)}, u32[]{:S(2)}) collective-permute-start(f32[136,128]{1,0:T(8,128)S(1)} %reduce_sum.9), channel_id=1, source_target_pairs={{0,1},{1,0},{2,3},{3,2},{4,5},{5,4},{6,7},{7,6},{8,9},{9,8},{10,11... | collective-permute-start | bytes 208904 | tf_op jit(solution)/shard_map/ppermute | solution.py:375
  33.9 0.1 copy.10
  34.0 0.1 copy.11
  34.1 0.1 copy.12
  34.2 1.4 %collective-permute-done.2 = f32[136,128]{1,0:T(8,128)S(1)} collective-permute-done((f32[136,128]{1,0:T(8,128)S(1)}, f32[136,128]{1,0:T(8,128)S(1)}, u32[]{:S(2)}, u32[]{:S(2)}) %collective-permute-start.2) | collective-permute-done | bytes 69664 | tf_op jit(solution)/shard_map/ppermute | solution.py:375
  35.6 5.9 %collective-permute-start.5 = (f32[136,128]{1,0:T(8,128)S(1)}, f32[136,128]{1,0:T(8,128)S(1)}, u32[]{:S(2)}, u32[]{:S(2)}) collective-permute-start(f32[136,128]{1,0:T(8,128)S(1)} %add.36), channel_id=1, source_target_pairs={{0,6},{1,7},{2,0},{3,1},{4,2},{5,3},{6,4},{7,5},{8,14},{9,15},{10,... | collective-permute-start | bytes 208904 | tf_op jit(solution)/shard_map/ppermute | solution.py:370
  41.5 1.0 %collective-permute-start.4 = (f32[136,128]{1,0:T(8,128)S(1)}, f32[136,128]{1,0:T(8,128)S(1)}, u32[]{:S(2)}, u32[]{:S(2)}) collective-permute-start(f32[136,128]{1,0:T(8,128)S(1)} %add.36), channel_id=1, source_target_pairs={{0,4},{1,5},{2,6},{3,7},{4,0},{5,1},{6,2},{7,3},{8,12},{9,13},{10,... | collective-permute-start | bytes 208904 | tf_op jit(solution)/shard_map/ppermute | solution.py:370
  42.5 2.3 %collective-permute-start.3 = (f32[136,128]{1,0:T(8,128)S(1)}, f32[136,128]{1,0:T(8,128)S(1)}, u32[]{:S(2)}, u32[]{:S(2)}) collective-permute-start(f32[136,128]{1,0:T(8,128)S(1)} %add.36), channel_id=1, source_target_pairs={{0,2},{1,3},{2,4},{3,5},{4,6},{5,7},{6,0},{7,1},{8,10},{9,11},{10,... | collective-permute-start | bytes 208904 | tf_op jit(solution)/shard_map/ppermute | solution.py:370
  44.8 2.7 %ready.1 = (bf16[20,128,256]{2,1,0:T(8,128)(2,1)S(1)}, bf16[20,128,128]{2,1,0:T(8,128)(2,1)S(1)}, f32[128,128]{1,0:T(8,128)S(1)}) custom-call(f32[128,128]{1,0:T(8,128)S(1)} %bitcast.17, f32[128,128]{1,0:T(8,128)S(1)} %bitcast.19, f32[128,128]{1,0:T(8,128)S(1)} %bitcast.21, f32[128,128]{1,0:T(8,128)S(1)} %copy-done.1), custom_call_target="tpu_custom_call" | custom-call | flops 1000000000 | bytes 2000000 | tf_op jit(solution)/shard_map/ready/pallas_call | solution.py:127
  47.5 1.3 %collective-permute-done.4 = f32[136,128]{1,0:T(8,128)S(1)} collective-permute-done((f32[136,128]{1,0:T(8,128)S(1)}, f32[136,128]{1,0:T(8,128)S(1)}, u32[]{:S(2)}, u32[]{:S(2)}) %collective-permute-start.4) | collective-permute-done | bytes 69664 | tf_op jit(solution)/shard_map/ppermute | solution.py:370
  48.8 0.7 collective-permute-done.3
  49.5 0.1 broadcast_in_dim.12
  49.6 17.2 %all_to_all.11.own_ref = f32[16,136,128]{2,1,0:T(8,128)S(1)} all-to-all(f32[16,136,128]{2,1,0:T(8,128)S(1)} %broadcast_in_dim.12), channel_id=1, replica_groups=mesh['tm_0'=4,'tm_1'=4,'tm_2'=2,'sr'=8] {'tm_0','tm_1'}, dimensions={0} | all-to-all | bytes 2228224 | tf_op jit(solution)/shard_map/all_to_all | solution.py:410
  66.8 4.9 %collective-permute-start.6 = (f32[16,136,128]{2,1,0:T(8,128)S(1)}, f32[16,136,128]{2,1,0:T(8,128)}, u32[]{:S(2)}, u32[]{:S(2)}) collective-permute-start(f32[16,136,128]{2,1,0:T(8,128)S(1)} %all_to_all.11.own_ref), channel_id=1, source_target_pairs={{0,8},{8,0},{1,9},{9,1},{2,10},{10,2},{3,11},{11,3},{4,12},{12,4},... | collective-permute-start | bytes 3342344 | tf_op jit(solution)/shard_map/ppermute | solution.py:370
  71.7 1.3 %begin.1.power_ref = f32[8,128,128]{2,1,0:T(8,128)S(1)} custom-call(f32[16,136,128]{2,1,0:T(8,128)S(1)} %all_to_all.11.own_ref, f32[128,128]{1,0:T(8,128)S(1)} %bitcast.20, f32[128,128]{1,0:T(8,128)S(1)} %bitcast.18), custom_call_target="tpu_custom_call" | custom-call | flops 1000000000 | bytes 2000000 | tf_op jit(solution)/shard_map/begin/pallas_call | solution.py:156
  73.1 1.2 %collective-permute-done.6.other_ref = f32[16,136,128]{2,1,0:T(8,128)} collective-permute-done((f32[16,136,128]{2,1,0:T(8,128)S(1)}, f32[16,136,128]{2,1,0:T(8,128)}, u32[]{:S(2)}, u32[]{:S(2)}) %collective-permute-start.6) | collective-permute-done | bytes 1114144 | tf_op jit(solution)/shard_map/ppermute | solution.py:370
  74.2 16.3 %scan.1 = (f32[4096,128]{1,0:T(8,128)S(1)}, f32[128,128]{1,0:T(8,128)}, f32[128,128]{1,0:T(8,128)S(1)}, f32[128,128]{1,0:T(8,128)S(1)}, f32[128,128]{1,0:T(8,128)S(1)}) custom-call(s32[1]{0:T(128)} %bitcast.core_ref, s32[1]{0:T(128)} %bitcast.1.place_ref, f32[16,136,128]{2,1,0:T(8,128)S(1)} %all_to_all.11.own_ref, ...), custom_call_target="tpu_custom_call" | custom-call | flops 10000000000 | bytes 5000000 | tf_op jit(solution)/shard_map/scan/pallas_call | solution.py:273
  90.5 0.9 convolution_bitcast_fusion.1.cross_ref
  91.5 4.1 %inverse.1 = (f32[256,128]{1,0:T(8,128)}, f32[128,128]{1,0:T(8,128)}) custom-call(f32[128,128]{1,0:T(8,128)S(1)} %get-tuple-element.29.total_ref, f32[128,128]{1,0:T(8,128)S(1)} %get-tuple-element.30.previous_ref, f32[128,128]{1,0:T(8,128)S(1)} %get-tuple-element.31.lagged_ref, f32[256,128]{1,0:T(8,128)S(1)} %convolution_bitcast_fusion.1.cross_ref), custom_call_target="tpu_custom_call" | custom-call | flops 1000000000 | bytes 600000 | tf_op jit(solution)/shard_map/inverse/pallas_call | solution.py:357
  (24 shorter events, 0.1 us)
Async XLA Ops:
  0.6 1.6 %copy-start = (bf16[4096,256]{1,0:T(8,128)(2,1)S(1)}, bf16[4096,256]{1,0:T(8,128)(2,1)}, u32[]{:S(2)}) copy-start(bf16[4096,256]{1,0:T(8,128)(2,1)} %param.7) | copy-start | bytes 6291460
  3.9 3.5 %copy-start.6 = (f32[256,128]{1,0:T(8,128)S(1)}, f32[256,128]{1,0:T(8,128)}, u32[]{:S(2)}) copy-start(f32[256,128]{1,0:T(8,128)} %param.8) | copy-start | bytes 393220
  3.9 3.5 %copy-start.10 = (f32[256]{0:T(256)S(1)}, f32[256]{0:T(256)}, u32[]{:S(2)}) copy-start(f32[256]{0:T(256)} %param.9) | copy-start | bytes 3076
  4.1 5.7 %collective-permute-start = (f32[2048,128]{1,0:T(8,128)S(1)}, f32[2048,128]{1,0:T(8,128)S(1)}, u32[]{:S(2)}, u32[]{:S(2)}) collective-permute-start(f32[2048,128]{1,0:T(8,128)S(1)} %get-tuple-element.20), channel_id=1, source_target_pairs={{0,8},{8,0},{1,9},{9,1},{2,10},{10,2},{3,11},{11,3},{4,12},{12,4},... | collective-permute-start | bytes 3145736 | tf_op jit(solution)/shard_map/ppermute | solution.py:370
  7.9 1.9 %collective-permute-start.1 = (f32[128,128]{1,0:T(8,128)S(1)}, f32[128,128]{1,0:T(8,128)S(1)}, u32[]{:S(2)}, u32[]{:S(2)}) collective-permute-start(f32[128,128]{1,0:T(8,128)S(1)} %convolution_bitcast_fusion.2), channel_id=1, source_target_pairs={{0,8},{8,0},{1,9},{9,1},{2,10},{10,2},{3,11},{11,3},{4,12},{12,4},... | collective-permute-start | bytes 196616 | tf_op jit(solution)/shard_map/ppermute | solution.py:370
  10.0 23.8 %copy-start.7 = (f32[128,128]{1,0:T(8,128)S(1)}, f32[128,128]{1,0:T(8,128)}, u32[]{:S(2)}) copy-start(f32[128,128]{1,0:T(8,128)} %param.10) | copy-start | bytes 196612
  10.1 23.9 %copy-start.8 = (f32[128,128]{1,0:T(8,128)S(1)}, f32[128,128]{1,0:T(8,128)}, u32[]{:S(2)}) copy-start(f32[128,128]{1,0:T(8,128)} %param.11) | copy-start | bytes 196612
  10.1 24.0 %copy-start.9 = (f32[128,128]{1,0:T(8,128)S(1)}, f32[128,128]{1,0:T(8,128)}, u32[]{:S(2)}) copy-start(f32[128,128]{1,0:T(8,128)} %param.12) | copy-start | bytes 196612
  10.1 34.7 %copy-start.1 = (f32[128,128]{1,0:T(8,128)S(1)}, f32[128,128]{1,0:T(8,128)}, u32[]{:S(2)}) copy-start(f32[128,128]{1,0:T(8,128)} %cov_ref.3) | copy-start | bytes 196612
  32.1 3.4 %collective-permute-start.2 = (f32[136,128]{1,0:T(8,128)S(1)}, f32[136,128]{1,0:T(8,128)S(1)}, u32[]{:S(2)}, u32[]{:S(2)}) collective-permute-start(f32[136,128]{1,0:T(8,128)S(1)} %reduce_sum.9), channel_id=1, source_target_pairs={{0,1},{1,0},{2,3},{3,2},{4,5},{5,4},{6,7},{7,6},{8,9},{9,8},{10,11... | collective-permute-start | bytes 208904 | tf_op jit(solution)/shard_map/ppermute | solution.py:375
  35.6 11.9 %collective-permute-start.5 = (f32[136,128]{1,0:T(8,128)S(1)}, f32[136,128]{1,0:T(8,128)S(1)}, u32[]{:S(2)}, u32[]{:S(2)}) collective-permute-start(f32[136,128]{1,0:T(8,128)S(1)} %add.36), channel_id=1, source_target_pairs={{0,6},{1,7},{2,0},{3,1},{4,2},{5,3},{6,4},{7,5},{8,14},{9,15},{10,... | collective-permute-start | bytes 208904 | tf_op jit(solution)/shard_map/ppermute | solution.py:370
  41.5 7.3 %collective-permute-start.4 = (f32[136,128]{1,0:T(8,128)S(1)}, f32[136,128]{1,0:T(8,128)S(1)}, u32[]{:S(2)}, u32[]{:S(2)}) collective-permute-start(f32[136,128]{1,0:T(8,128)S(1)} %add.36), channel_id=1, source_target_pairs={{0,4},{1,5},{2,6},{3,7},{4,0},{5,1},{6,2},{7,3},{8,12},{9,13},{10,... | collective-permute-start | bytes 208904 | tf_op jit(solution)/shard_map/ppermute | solution.py:370
  42.5 7.0 %collective-permute-start.3 = (f32[136,128]{1,0:T(8,128)S(1)}, f32[136,128]{1,0:T(8,128)S(1)}, u32[]{:S(2)}, u32[]{:S(2)}) collective-permute-start(f32[136,128]{1,0:T(8,128)S(1)} %add.36), channel_id=1, source_target_pairs={{0,2},{1,3},{2,4},{3,5},{4,6},{5,7},{6,0},{7,1},{8,10},{9,11},{10,... | collective-permute-start | bytes 208904 | tf_op jit(solution)/shard_map/ppermute | solution.py:370
  47.5 2.1 %copy-start.2 = (bf16[20,128,256]{2,1,0:T(8,128)(2,1)}, bf16[20,128,256]{2,1,0:T(8,128)(2,1)S(1)}, u32[]{:S(2)}) copy-start(bf16[20,128,256]{2,1,0:T(8,128)(2,1)S(1)} %get-tuple-element.25.both_ref) | copy-start | bytes 3932164
  47.5 19.3 %copy-start.4 = (bf16[20,128,128]{2,1,0:T(8,128)(2,1)}, bf16[20,128,128]{2,1,0:T(8,128)(2,1)S(1)}, u32[]{:S(2)}) copy-start(bf16[20,128,128]{2,1,0:T(8,128)(2,1)S(1)} %get-tuple-element.26.small_ref) | copy-start | bytes 1966084
  66.8 7.5 %collective-permute-start.6 = (f32[16,136,128]{2,1,0:T(8,128)S(1)}, f32[16,136,128]{2,1,0:T(8,128)}, u32[]{:S(2)}, u32[]{:S(2)}) collective-permute-start(f32[16,136,128]{2,1,0:T(8,128)S(1)} %all_to_all.11.own_ref), channel_id=1, source_target_pairs={{0,8},{8,0},{1,9},{9,1},{2,10},{10,2},{3,11},{11,3},{4,12},{12,4},... | collective-permute-start | bytes 3342344 | tf_op jit(solution)/shard_map/ppermute | solution.py:370
  71.7 2.5 %copy-start.3 = (bf16[20,128,256]{2,1,0:T(8,128)(2,1)S(1)}, bf16[20,128,256]{2,1,0:T(8,128)(2,1)}, u32[]{:S(2)}) copy-start(bf16[20,128,256]{2,1,0:T(8,128)(2,1)} %copy-done.2) | copy-start | bytes 3932164
  71.7 2.5 %copy-start.5 = (bf16[20,128,128]{2,1,0:T(8,128)(2,1)S(1)}, bf16[20,128,128]{2,1,0:T(8,128)(2,1)}, u32[]{:S(2)}) copy-start(bf16[20,128,128]{2,1,0:T(8,128)(2,1)} %copy-done.4) | copy-start | bytes 1966084

commit v5 on v4

--- a/solution.py
+++ b/solution.py
@@ -1,7 +1,6 @@
 import jax
 import jax.numpy as jnp
 from jax import lax
-from jax.experimental.layout import Layout, with_layout_constraint
 from jax.experimental import pallas as pl
 from jax.experimental.pallas import tpu as pltpu
 from jax.sharding import Mesh
@@ -13,6 +12,7 @@
 
 STEPS = 8
 SQUARINGS = 7
+LEAPS = 4
 FIRST = 4
 f32 = jnp.float32
 bf16 = jnp.bfloat16
@@ -146,7 +146,10 @@
     info = jnp.concatenate([own_ref[g, rows:] for g in range(groups)], axis=0)
     ft = ft_ref[...]
     a = ft - high(high(ft, info), kt_ref[...])
-    for k, w in enumerate(powers(a, n)):
+    found = powers(a, n)
+    for _ in range(LEAPS - 1):
+        found.append(high(found[-1], found[-1]))
+    for k, w in enumerate(found):
         power_ref[k] = w
 
 
@@ -155,7 +158,7 @@
     vmem = pl.BlockSpec(memory_space=pltpu.VMEM)
     return pl.pallas_call(
         begin_kernel,
-        out_shape=jax.ShapeDtypeStruct((STEPS, n, n), f32),
+        out_shape=jax.ShapeDtypeStruct((STEPS + LEAPS - 1, n, n), f32),
         in_specs=[vmem] * 3,
         out_specs=vmem,
         compiler_params=pltpu.CompilerParams(vmem_limit_bytes=16 * 1024 * 1024),
@@ -176,24 +179,26 @@
     first = core_ref[0] == 0
     cov = cov_ref[...]
     held = lambda k: (both_ref[k], small_ref[k])
-    row = lax.broadcasted_iota(jnp.int32, (blocks, n), 0)
+    pairs = blocks // 2
+    row = lax.broadcasted_iota(jnp.int32, (pairs, n), 0)
     levels = blocks.bit_length() - 1
-    apow = [power_ref[k] for k in range(STEPS)]
-    a = apow[0]
-    leap = apow[-1]
-    leaps = [right(leap)]
+    leap = power_ref[STEPS + LEAPS - 2]
+    leaps = [None] * (LEAPS - 1) + [right(leap)]
 
     def drive(j):
-        def half(ref):
-            parts = [ref[g, pl.ds(j, rows // STEPS, stride=STEPS), :] for g in range(groups)]
+        def half(ref, start):
+            parts = [
+                ref[g, pl.ds(start, rows // (2 * STEPS), stride=2 * STEPS), :] for g in range(groups)
+            ]
             return jnp.concatenate(parts, axis=0)
 
-        own, other = half(own_ref), half(other_ref)
-        return jnp.concatenate(
-            [jnp.where(first, own, other), jnp.where(first, other, own)], axis=0
-        )
-
-    step = kept(beneath(pieces_of(a), held(0)), 2)
+        found = []
+        for start in (j, STEPS + j):
+            own, other = half(own_ref, start), half(other_ref, start)
+            found += [jnp.where(first, own, other), jnp.where(first, other, own)]
+        return jnp.concatenate(found, axis=0)
+
+    step = kept(beneath(pieces_of(power_ref[0]), held(0)), 2)
     state = times(drive(0), kept(held(0)))
     loc_ref[0] = state
     for j in range(1, STEPS):
@@ -202,38 +207,51 @@
         if len(leaps) < levels:
             leap = times(leap, leaps[-1])
             leaps.append(right(leap))
-    enter = state
+    even, odd = state[:pairs], state[pairs:]
+    back = kept(beneath(held(FIRST), held(1)), 2)
+    both = lambda j: jnp.concatenate([loc_ref[j], power_ref[j]], axis=0)
+
+    def leap_of(level):
+        nonlocal leap
+        if level < LEAPS - 1:
+            return right(power_ref[STEPS - 1 + level])
+        if len(leaps) <= level:
+            leap = times(leap, leaps[-1])
+            leaps.append(right(leap))
+        return leaps[level]
+
+    enter = None
     level = 0
-    back = kept(beneath(held(FIRST), held(1)), 2)
-    both = lambda j: jnp.concatenate([loc_ref[j], apow[j]], axis=0)
     out = times(both(STEPS - 1), kept(held(1)))
     for j in range(STEPS - 1, -1, -1):
         if j < STEPS - 1:
             out = times(jnp.concatenate([out, both(j)], axis=1), back)
         loc_ref[j] = out[:blocks]
         mat_ref[j] = out[blocks:]
-        if level < levels:
-            if len(leaps) < levels:
-                leap = times(leap, leaps[-1])
-                leaps.append(right(leap))
-            enter = enter + times(moved(enter, 1 << level, row), leaps[level])
+        while level < (levels if j == 0 else STEPS - j):
+            if level == 0:
+                enter = times(even, leap_of(0)) + odd
+            else:
+                enter = enter + times(moved(enter, 1 << (level - 1), row), leap_of(level))
             level += 1
-    while level < levels:
-        if len(leaps) < levels:
-            leap = times(leap, leaps[-1])
-            leaps.append(right(leap))
-        enter = enter + times(moved(enter, 1 << level, row), leaps[level])
-        level += 1
-    e = moved(enter, 1, row)
+    entered = moved(enter, 1, row)
+    e = jnp.concatenate([entered, times(entered, leap_of(0)) + even], axis=0)
     tail = lax.broadcasted_iota(jnp.int32, (8, n), 0) == 7
-    final = jnp.where(tail, enter[blocks - 8 :], 0.0)
+    final = jnp.where(tail, enter[pairs - 8 :], 0.0)
     after = times(final, kept(held(2)))
     z = loc_ref[0] + high(e, mat_ref[0])
-    z = jnp.concatenate([z[: blocks - 8], z[blocks - 8 :] + times(final, kept(held(3)))], axis=0)
-    for level in range(levels):
-        z = z + times(moved(z, -(1 << level), row), kept(held(FIRST + STEPS - 1 + level)))
-    coming = moved(z, -1, row)
-    coming = jnp.concatenate([coming[: blocks - 8], coming[blocks - 8 :] + after], axis=0)
+    even = z[:pairs]
+    odd = jnp.concatenate(
+        [z[pairs : blocks - 8], z[blocks - 8 :] + times(final, kept(held(3)))], axis=0
+    )
+    one = kept(held(FIRST + STEPS - 1))
+    even = even + times(odd, one)
+    for level in range(levels - 1):
+        even = even + times(moved(even, -(1 << level), row), kept(held(FIRST + STEPS + level)))
+    ahead = moved(even, -1, row)
+    odd = odd + times(ahead, one)
+    z = jnp.concatenate([even, odd], axis=0)
+    coming = jnp.concatenate([odd, ahead[: pairs - 8], ahead[pairs - 8 :] + after], axis=0)
     mixed = thirds(jnp.concatenate([e, coming], axis=1))
     sums = jnp.zeros((n, 2 * n), f32)
 
@@ -245,15 +263,21 @@
         return contracted(xa, pair) + (contracted(xb, pair) + contracted(xa, rest))
 
     opening = prior = thirds(z)[:2]
-    x_ref[pl.ds(0, blocks, stride=STEPS), :] = z
+
+    def show(j, x):
+        x_ref[pl.ds(j, pairs, stride=2 * STEPS), :] = x[:pairs]
+        x_ref[pl.ds(STEPS + j, pairs, stride=2 * STEPS), :] = x[pairs:]
+
+    show(0, z)
     for j in range(1, STEPS):
         w = kept(beneath(pieces_of(mat_ref[j]), held(FIRST + STEPS - 1 - j)), 2)
         x = loc_ref[j] + times_split(mixed, w)
-        x_ref[pl.ds(j, blocks, stride=STEPS), :] = x
+        show(j, x)
         here = thirds(x)[:2]
         sums = sums + outer(here, prior)
         prior = here
-    sums = sums + outer(opening, thirds(moved(x, 1, row))[:2])
+    prior = jnp.concatenate([moved(x[pairs:], 1, row), x[:pairs]], axis=0)
+    sums = sums + outer(opening, thirds(prior)[:2])
     last = jnp.where(tail, x_ref[length - 8 :], 0.0)
     la, lb, _ = thirds(last)
     ends = contracted(la, la) + (contracted(lb, la) + contracted(la, lb))
@@ -393,11 +417,16 @@
 
     info_part = jnp.dot(loadings.T, weighted, precision=precise, preferred_element_type=f32)
     info_part = info_part + turned(info_part, CORE, 1)
-    whole = jnp.dot(observations, scaled, preferred_element_type=f32)
-    whole = with_layout_constraint(whole, Layout(major_to_minor=(0, 1)))
-    given = lax.dynamic_slice_in_dim(whole, (1 - core) * half, half, 0)
-    mine = lax.dynamic_slice_in_dim(whole, core * half, half, 0)
-    given, mine = lax.optimization_barrier((given, mine))
+    kept_rows, given_rows, factors = lax.optimization_barrier(
+        (
+            lax.dynamic_slice_in_dim(observations, core * half, half, 0),
+            lax.dynamic_slice_in_dim(observations, (1 - core) * half, half, 0),
+            scaled,
+        )
+    )
+    given = jnp.dot(given_rows, factors, preferred_element_type=f32)
+    mine = jnp.dot(kept_rows, factors, preferred_element_type=f32)
+    mine, info_part = lax.optimization_barrier((mine, info_part))
     mine = mine + turned(given, CORE, 1)
     pieces = jnp.concatenate(
         [mine.reshape(groups, rows, width), info_part.reshape(groups, extra, width)], axis=1

time: 95.9 us -> 93.7 us (0.977)
  Pallas kernels: 24.4 us -> 23.2 us
  other arithmetic: 0.34 us -> 1.3 us
    pallas_call x1, Pallas kernels: 16.3 us -> 14.5 us  [scanned(): pl.pallas_call(scan_kernel, out_shape=(jax.ShapeDtypeStruct((length, n),...]
    unnamed x25 -> x21, local copies, waits for them, and re-layouts: 1.9 us -> 0.31 us
    dynamic_slice x1, local copies, waits for them, and re-layouts: 0.15 us -> 1.69 us  [local(): lax.dynamic_slice_in_dim(observations, (1 - core) * half, half, 0)]
    convert_element_type x0 -> x1, other arithmetic: none -> 1 us  [local(): scaled = weighted.astype(bf16)]
  transfers between devices with their start and end apart: 7 -> 7, of which waited for: 5 -> 5; matrix products, arithmetic and copies ran while one was open for 1% -> 1% of each run, Pallas kernels for 4% -> 5%
where the time goes in v5:
time: 93.7 us; the launch traced here: 93.5 us
  blocking collectives  39.2 us (42%)
  Pallas kernels  23.2 us (25%)
  starting transfers between devices  19.6 us (21%)
  waiting for transfers between devices  4.89 us (5%)
  matrix products  2.24 us (2%)
  local copies, waits for them, and re-layouts  2.16 us (2%)
  other arithmetic  1.3 us (1%)
    all_to_all x1, blocking collectives, local(): lax.all_to_all(pieces, (Y, X), split_axis=0, concat_axis=0, tiled=True)  22 us
    ppermute x6, starting transfers between devices, turned(): lax.ppermute(value, axis, [(i, (i + steps) % count) for i in range(count)])  17.9 us
    all_to_all x1, blocking collectives, local(): lax.all_to_all(copies, (Y, X), split_axis=0, concat_axis=0, tiled=True)  17.2 us
    pallas_call x1, Pallas kernels, scanned(): pl.pallas_call(scan_kernel, out_shape=(jax.ShapeDtypeStruct((length, n),...  14.5 us
    pallas_call x1, Pallas kernels, inverted(): pl.pallas_call(inverse_kernel, out_shape=(jax.ShapeDtypeStruct(cross.shap...  4.15 us
    ppermute x6, waiting for transfers between devices, turned(): lax.ppermute(value, axis, [(i, (i + steps) % count) for i in range(count)])  3.5 us
    pallas_call x1, Pallas kernels, readied(): pl.pallas_call(ready_kernel, out_shape=(jax.ShapeDtypeStruct((count, n, 2...  2.7 us
    pallas_call x1, Pallas kernels, begun(): pl.pallas_call(begin_kernel, out_shape=jax.ShapeDtypeStruct((STEPS + LEAP...  1.91 us
  transfers between devices with their start and end apart: 7, of which 5 were waited for; matrix products, arithmetic and copies ran while one was open for 1% of the time, Pallas kernels for 5%

profile of v5, /device:TPU:1, one launch (start us, length us, event | category | flops | bytes accessed | tf_op | source)
XLA Modules:
  0.0 93.5 jit_solution(134256696150753576)
XLA Ops:
  0.6 1.0 %multiply_convert_fusion = bf16[256,128]{1,0:T(8,128)(2,1)S(1)} fusion(f32[256,128]{1,0:T(8,128)} %param.8, f32[256]{0:T(256)} %param.9), kind=kLoop, calls=%fused_computation.5 | loop fusion | flops 65536 | bytes 197632 | tf_op jit(solution)/shard_map/convert_element_type | solution.py:416
  1.6 1.7 %constant_dynamic-slice_fusion = (bf16[2048,256]{1,0:T(8,128)(2,1)S(1)}, bf16[2048,256]{1,0:T(8,128)(2,1)S(1)}) fusion(bf16[4096,256]{1,0:T(8,128)(2,1)} %param.7, s32[]{:T(128)S(6)} %select_n.7, s32[]{:T(128)S(6)} %select_n.6), kind=kLoop, calls=%fused_computation.8 | loop fusion | bytes 4194312 | tf_op jit(solution)/shard_map/dynamic_slice | solution.py:423
  3.4 0.4 fusion.4
  3.8 3.3 %collective-permute-start.1 = (f32[2048,128]{1,0:T(8,128)S(1)}, f32[2048,128]{1,0:T(8,128)S(1)}, u32[]{:S(2)}, u32[]{:S(2)}) collective-permute-start(f32[2048,128]{1,0:T(8,128)S(1)} %fusion.4), channel_id=1, source_target_pairs={{0,8},{8,0},{1,9},{9,1},{2,10},{10,2},{3,11},{11,3},{4,12},{12,4},... | collective-permute-start | bytes 3145736 | tf_op jit(solution)/shard_map/ppermute | solution.py:394
  7.1 0.5 convolution_bitcast_fusion.1
  7.6 0.5 collective-permute-start
  8.0 0.4 fusion.3
  8.5 1.0 %collective-permute-done = f32[128,128]{0,1:T(8,128)S(1)} collective-permute-done((f32[128,128]{0,1:T(8,128)S(1)}, f32[128,128]{0,1:T(8,128)S(1)}, u32[]{:S(2)}, u32[]{:S(2)}) %collective-permute-start) | collective-permute-done | bytes 65568 | tf_op jit(solution)/shard_map/ppermute | solution.py:394
  9.5 0.1 copy.15
  9.6 0.1 add.35
  9.7 0.1 pad_maximum_fusion
  9.8 22.0 %all_to_all.10 = f32[16,136,128]{2,1,0:T(8,128)S(1)} all-to-all(f32[16,136,128]{2,1,0:T(8,128)S(1)} %pad_maximum_fusion), channel_id=1, replica_groups=mesh['tm_0'=4,'tm_1'=4,'tm_2'=2,'sr'=8] {'tm_0','tm_1'}, dimensions={0} | all-to-all | bytes 2228224 | tf_op jit(solution)/shard_map/all_to_all | solution.py:434
  31.8 0.1 reduce_sum.9
  31.9 1.7 %collective-permute-start.2 = (f32[136,128]{1,0:T(8,128)S(1)}, f32[136,128]{1,0:T(8,128)S(1)}, u32[]{:S(2)}, u32[]{:S(2)}) collective-permute-start(f32[136,128]{1,0:T(8,128)S(1)} %reduce_sum.9), channel_id=1, source_target_pairs={{0,1},{1,0},{2,3},{3,2},{4,5},{5,4},{6,7},{7,6},{8,9},{9,8},{10,11... | collective-permute-start | bytes 208904 | tf_op jit(solution)/shard_map/ppermute | solution.py:399
  33.6 0.1 copy.16
  33.7 0.1 copy.17
  33.8 0.1 copy.18
  33.9 1.4 %collective-permute-done.2 = f32[136,128]{1,0:T(8,128)S(1)} collective-permute-done((f32[136,128]{1,0:T(8,128)S(1)}, f32[136,128]{1,0:T(8,128)S(1)}, u32[]{:S(2)}, u32[]{:S(2)}) %collective-permute-start.2) | collective-permute-done | bytes 69664 | tf_op jit(solution)/shard_map/ppermute | solution.py:399
  35.3 5.9 %collective-permute-start.5 = (f32[136,128]{1,0:T(8,128)S(1)}, f32[136,128]{1,0:T(8,128)S(1)}, u32[]{:S(2)}, u32[]{:S(2)}) collective-permute-start(f32[136,128]{1,0:T(8,128)S(1)} %add.36), channel_id=1, source_target_pairs={{0,6},{1,7},{2,0},{3,1},{4,2},{5,3},{6,4},{7,5},{8,14},{9,15},{10,... | collective-permute-start | bytes 208904 | tf_op jit(solution)/shard_map/ppermute | solution.py:394
  41.3 1.0 %collective-permute-start.4 = (f32[136,128]{1,0:T(8,128)S(1)}, f32[136,128]{1,0:T(8,128)S(1)}, u32[]{:S(2)}, u32[]{:S(2)}) collective-permute-start(f32[136,128]{1,0:T(8,128)S(1)} %add.36), channel_id=1, source_target_pairs={{0,4},{1,5},{2,6},{3,7},{4,0},{5,1},{6,2},{7,3},{8,12},{9,13},{10,... | collective-permute-start | bytes 208904 | tf_op jit(solution)/shard_map/ppermute | solution.py:394
  42.3 2.3 %collective-permute-start.3 = (f32[136,128]{1,0:T(8,128)S(1)}, f32[136,128]{1,0:T(8,128)S(1)}, u32[]{:S(2)}, u32[]{:S(2)}) collective-permute-start(f32[136,128]{1,0:T(8,128)S(1)} %add.36), channel_id=1, source_target_pairs={{0,2},{1,3},{2,4},{3,5},{4,6},{5,7},{6,0},{7,1},{8,10},{9,11},{10,... | collective-permute-start | bytes 208904 | tf_op jit(solution)/shard_map/ppermute | solution.py:394
  44.5 2.7 %ready.1 = (bf16[20,128,256]{2,1,0:T(8,128)(2,1)S(1)}, bf16[20,128,128]{2,1,0:T(8,128)(2,1)S(1)}, f32[128,128]{1,0:T(8,128)S(1)}) custom-call(f32[128,128]{1,0:T(8,128)S(1)} %bitcast.17, f32[128,128]{1,0:T(8,128)S(1)} %bitcast.19, f32[128,128]{1,0:T(8,128)S(1)} %bitcast.21, f32[128,128]{1,0:T(8,128)S(1)} %copy-done), custom_call_target="tpu_custom_call" | custom-call | flops 1000000000 | bytes 2000000 | tf_op jit(solution)/shard_map/ready/pallas_call | solution.py:127
  47.2 1.3 %collective-permute-done.4 = f32[136,128]{1,0:T(8,128)S(1)} collective-permute-done((f32[136,128]{1,0:T(8,128)S(1)}, f32[136,128]{1,0:T(8,128)S(1)}, u32[]{:S(2)}, u32[]{:S(2)}) %collective-permute-start.4) | collective-permute-done | bytes 69664 | tf_op jit(solution)/shard_map/ppermute | solution.py:394
  48.5 0.7 collective-permute-done.3
  49.3 0.1 broadcast_in_dim.12
  49.3 17.2 %all_to_all.11.own_ref = f32[16,136,128]{2,1,0:T(8,128)S(1)} all-to-all(f32[16,136,128]{2,1,0:T(8,128)S(1)} %broadcast_in_dim.12), channel_id=1, replica_groups=mesh['tm_0'=4,'tm_1'=4,'tm_2'=2,'sr'=8] {'tm_0','tm_1'}, dimensions={0} | all-to-all | bytes 2228224 | tf_op jit(solution)/shard_map/all_to_all | solution.py:439
  66.5 4.9 %collective-permute-start.6 = (f32[16,136,128]{2,1,0:T(8,128)S(1)}, f32[16,136,128]{2,1,0:T(8,128)S(1)}, u32[]{:S(2)}, u32[]{:S(2)}) collective-permute-start(f32[16,136,128]{2,1,0:T(8,128)S(1)} %all_to_all.11.own_ref), channel_id=1, source_target_pairs={{0,8},{8,0},{1,9},{9,1},{2,10},{10,2},{3,11},{11,3},{4,12},{12,4},... | collective-permute-start | bytes 3342344 | tf_op jit(solution)/shard_map/ppermute | solution.py:394
  71.5 1.9 %begin.1.power_ref = f32[11,128,128]{2,1,0:T(8,128)S(1)} custom-call(f32[16,136,128]{2,1,0:T(8,128)S(1)} %all_to_all.11.own_ref, f32[128,128]{1,0:T(8,128)S(1)} %bitcast.20, f32[128,128]{1,0:T(8,128)S(1)} %bitcast.18), custom_call_target="tpu_custom_call" | custom-call | flops 1000000000 | bytes 2000000 | tf_op jit(solution)/shard_map/begin/pallas_call | solution.py:159
  73.4 0.5 collective-permute-done.6.other_ref
  73.9 14.5 %scan.1 = (f32[4096,128]{1,0:T(8,128)S(1)}, f32[128,128]{1,0:T(8,128)}, f32[128,128]{1,0:T(8,128)S(1)}, f32[128,128]{1,0:T(8,128)S(1)}, f32[128,128]{1,0:T(8,128)S(1)}) custom-call(s32[1]{0:T(128)} %bitcast.core_ref, s32[1]{0:T(128)} %bitcast.1.place_ref, f32[16,136,128]{2,1,0:T(8,128)S(1)} %all_to_all.11.own_ref, ...), custom_call_target="tpu_custom_call" | custom-call | flops 10000000000 | bytes 5000000 | tf_op jit(solution)/shard_map/scan/pallas_call | solution.py:297
  88.3 1.0 %convolution_bitcast_fusion.cross_ref = f32[256,128]{1,0:T(8,128)S(1)} fusion(bf16[4096,256]{1,0:T(8,128)(2,1)S(1)} %copy-done.3, f32[4096,128]{1,0:T(8,128)S(1)} %get-tuple-element.38), kind=kOutput, calls=%fused_computation | convolution fusion | flops 268959744 | bytes 4325376 | tf_op jit(solution)/shard_map/ts,tk->sk/dot_general | solution.py:446
  89.3 4.1 %inverse.1 = (f32[256,128]{1,0:T(8,128)}, f32[128,128]{1,0:T(8,128)}) custom-call(f32[128,128]{1,0:T(8,128)S(1)} %get-tuple-element.35.total_ref, f32[128,128]{1,0:T(8,128)S(1)} %get-tuple-element.36.previous_ref, f32[128,128]{1,0:T(8,128)S(1)} %get-tuple-element.37.lagged_ref, f32[256,128]{1,0:T(8,128)S(1)} %convolution_bitcast_fusion.cross_ref), custom_call_target="tpu_custom_call" | custom-call | flops 1000000000 | bytes 600000 | tf_op jit(solution)/shard_map/inverse/pallas_call | solution.py:381
  (23 shorter events, 0.1 us)
Async XLA Ops:
  3.3 3.8 %copy-start.4 = (f32[256,128]{1,0:T(8,128)S(1)}, f32[256,128]{1,0:T(8,128)}, u32[]{:S(2)}) copy-start(f32[256,128]{1,0:T(8,128)} %param.8) | copy-start | bytes 393220
  3.3 3.8 %copy-start.8 = (f32[256]{0:T(256)S(1)}, f32[256]{0:T(256)}, u32[]{:S(2)}) copy-start(f32[256]{0:T(256)} %param.9) | copy-start | bytes 3076
  3.8 5.8 %collective-permute-start.1 = (f32[2048,128]{1,0:T(8,128)S(1)}, f32[2048,128]{1,0:T(8,128)S(1)}, u32[]{:S(2)}, u32[]{:S(2)}) collective-permute-start(f32[2048,128]{1,0:T(8,128)S(1)} %fusion.4), channel_id=1, source_target_pairs={{0,8},{8,0},{1,9},{9,1},{2,10},{10,2},{3,11},{11,3},{4,12},{12,4},... | collective-permute-start | bytes 3145736 | tf_op jit(solution)/shard_map/ppermute | solution.py:394
  7.6 1.9 %collective-permute-start = (f32[128,128]{0,1:T(8,128)S(1)}, f32[128,128]{0,1:T(8,128)S(1)}, u32[]{:S(2)}, u32[]{:S(2)}) collective-permute-start(f32[128,128]{0,1:T(8,128)S(1)} %convolution_bitcast_fusion.1), channel_id=1, source_target_pairs={{0,8},{8,0},{1,9},{9,1},{2,10},{10,2},{3,11},{11,3},{4,12},{12,4},... | collective-permute-start | bytes 196616 | tf_op jit(solution)/shard_map/ppermute | solution.py:394
  9.8 23.8 %copy-start.5 = (f32[128,128]{1,0:T(8,128)S(1)}, f32[128,128]{1,0:T(8,128)}, u32[]{:S(2)}) copy-start(f32[128,128]{1,0:T(8,128)} %param.10) | copy-start | bytes 196612
  9.8 23.9 %copy-start.6 = (f32[128,128]{1,0:T(8,128)S(1)}, f32[128,128]{1,0:T(8,128)}, u32[]{:S(2)}) copy-start(f32[128,128]{1,0:T(8,128)} %param.11) | copy-start | bytes 196612
  9.8 24.0 %copy-start.7 = (f32[128,128]{1,0:T(8,128)S(1)}, f32[128,128]{1,0:T(8,128)}, u32[]{:S(2)}) copy-start(f32[128,128]{1,0:T(8,128)} %param.12) | copy-start | bytes 196612
  31.8 12.7 %copy-start = (f32[128,128]{1,0:T(8,128)S(1)}, f32[128,128]{1,0:T(8,128)}, u32[]{:S(2)}) copy-start(f32[128,128]{1,0:T(8,128)} %cov_ref.3) | copy-start | bytes 196612
  31.9 3.4 %collective-permute-start.2 = (f32[136,128]{1,0:T(8,128)S(1)}, f32[136,128]{1,0:T(8,128)S(1)}, u32[]{:S(2)}, u32[]{:S(2)}) collective-permute-start(f32[136,128]{1,0:T(8,128)S(1)} %reduce_sum.9), channel_id=1, source_target_pairs={{0,1},{1,0},{2,3},{3,2},{4,5},{5,4},{6,7},{7,6},{8,9},{9,8},{10,11... | collective-permute-start | bytes 208904 | tf_op jit(solution)/shard_map/ppermute | solution.py:399
  35.3 11.9 %collective-permute-start.5 = (f32[136,128]{1,0:T(8,128)S(1)}, f32[136,128]{1,0:T(8,128)S(1)}, u32[]{:S(2)}, u32[]{:S(2)}) collective-permute-start(f32[136,128]{1,0:T(8,128)S(1)} %add.36), channel_id=1, source_target_pairs={{0,6},{1,7},{2,0},{3,1},{4,2},{5,3},{6,4},{7,5},{8,14},{9,15},{10,... | collective-permute-start | bytes 208904 | tf_op jit(solution)/shard_map/ppermute | solution.py:394
  41.3 7.3 %collective-permute-start.4 = (f32[136,128]{1,0:T(8,128)S(1)}, f32[136,128]{1,0:T(8,128)S(1)}, u32[]{:S(2)}, u32[]{:S(2)}) collective-permute-start(f32[136,128]{1,0:T(8,128)S(1)} %add.36), channel_id=1, source_target_pairs={{0,4},{1,5},{2,6},{3,7},{4,0},{5,1},{6,2},{7,3},{8,12},{9,13},{10,... | collective-permute-start | bytes 208904 | tf_op jit(solution)/shard_map/ppermute | solution.py:394
  42.3 7.0 %collective-permute-start.3 = (f32[136,128]{1,0:T(8,128)S(1)}, f32[136,128]{1,0:T(8,128)S(1)}, u32[]{:S(2)}, u32[]{:S(2)}) collective-permute-start(f32[136,128]{1,0:T(8,128)S(1)} %add.36), channel_id=1, source_target_pairs={{0,2},{1,3},{2,4},{3,5},{4,6},{5,7},{6,0},{7,1},{8,10},{9,11},{10,... | collective-permute-start | bytes 208904 | tf_op jit(solution)/shard_map/ppermute | solution.py:394
  47.2 19.3 %copy-start.1 = (bf16[20,128,256]{2,1,0:T(8,128)(2,1)}, bf16[20,128,256]{2,1,0:T(8,128)(2,1)S(1)}, u32[]{:S(2)}) copy-start(bf16[20,128,256]{2,1,0:T(8,128)(2,1)S(1)} %get-tuple-element.31.both_ref) | copy-start | bytes 3932164
  66.5 7.3 %collective-permute-start.6 = (f32[16,136,128]{2,1,0:T(8,128)S(1)}, f32[16,136,128]{2,1,0:T(8,128)S(1)}, u32[]{:S(2)}, u32[]{:S(2)}) collective-permute-start(f32[16,136,128]{2,1,0:T(8,128)S(1)} %all_to_all.11.own_ref), channel_id=1, source_target_pairs={{0,8},{8,0},{1,9},{9,1},{2,10},{10,2},{3,11},{11,3},{4,12},{12,4},... | collective-permute-start | bytes 3342344 | tf_op jit(solution)/shard_map/ppermute | solution.py:394
  71.5 2.4 %copy-start.2 = (bf16[20,128,256]{2,1,0:T(8,128)(2,1)S(1)}, bf16[20,128,256]{2,1,0:T(8,128)(2,1)}, u32[]{:S(2)}) copy-start(bf16[20,128,256]{2,1,0:T(8,128)(2,1)} %copy-done.1) | copy-start | bytes 3932164
  73.9 14.5 %copy-start.3 = (bf16[4096,256]{1,0:T(8,128)(2,1)S(1)}, bf16[4096,256]{1,0:T(8,128)(2,1)}, u32[]{:S(2)}) copy-start(bf16[4096,256]{1,0:T(8,128)(2,1)} %param.7) | copy-start | bytes 6291460

commit v6 on v5

--- a/solution.py
+++ b/solution.py
@@ -6,9 +6,10 @@
 from jax.sharding import Mesh
 from jax.sharding import PartitionSpec as P
 
-Y, X, CORE, Z = "tm_0", "tm_1", "tm_2", "sr"
+Y, X, CORE, ZH, ZL = "tm_0", "tm_1", "tm_2", "sr_0", "sr_1"
 TM = (Y, X, CORE)
-SR_TM = (Z, Y, X, CORE)
+SR_TM = (ZH, ZL, Y, X, CORE)
+NEAR = (Y, X, ZL)
 
 STEPS = 8
 SQUARINGS = 7
@@ -142,8 +143,8 @@
 def begin_kernel(own_ref, kt_ref, ft_ref, power_ref):
     n = ft_ref.shape[0]
     groups = own_ref.shape[0]
-    rows = own_ref.shape[1] - n // groups
-    info = jnp.concatenate([own_ref[g, rows:] for g in range(groups)], axis=0)
+    rows = own_ref.shape[1] - 2 * n // groups
+    info = jnp.concatenate([own_ref[g, rows:] for g in range(0, groups, 2)], axis=0)
     ft = ft_ref[...]
     a = ft - high(high(ft, info), kt_ref[...])
     found = powers(a, n)
@@ -188,12 +189,12 @@
     def drive(j):
         def half(ref, start):
             parts = [
-                ref[g, pl.ds(start, rows // (2 * STEPS), stride=2 * STEPS), :] for g in range(groups)
+                ref[g, pl.ds(j, rows // STEPS, stride=STEPS), :] for g in range(start, groups, 2)
             ]
             return jnp.concatenate(parts, axis=0)
 
         found = []
-        for start in (j, STEPS + j):
+        for start in range(2):
             own, other = half(own_ref, start), half(other_ref, start)
             found += [jnp.where(first, own, other), jnp.where(first, other, own)]
         return jnp.concatenate(found, axis=0)
@@ -394,11 +395,8 @@
     return lax.ppermute(value, axis, [(i, (i + steps) % count) for i in range(count)])
 
 
-def over_z(value):
-    count = lax.axis_size(Z)
-    value = value + lax.ppermute(value, Z, [(i, i ^ 1) for i in range(count)])
-    arrived = [turned(value, Z, 2 * k) for k in range(1, count // 2)]
-    return sum(arrived, value)
+def over_far(value):
+    return sum([turned(value, ZH, k) for k in range(1, lax.axis_size(ZH))], value)
 
 
 def local(
@@ -409,9 +407,9 @@
     length = observations.shape[0]
     width = transition.shape[0]
     half = length // 2
-    groups = lax.axis_size((Y, X))
+    groups = lax.axis_size(NEAR)
     rows = half // groups
-    extra = width // groups
+    extra = 2 * width // groups
     weighted = noise_precision[:, None] * loadings
     scaled = weighted.astype(bf16)
 
@@ -428,15 +426,21 @@
     mine = jnp.dot(kept_rows, factors, preferred_element_type=f32)
     mine, info_part = lax.optimization_barrier((mine, info_part))
     mine = mine + turned(given, CORE, 1)
+    mine = mine.reshape(groups // 2, rows // STEPS, 2, STEPS, width).transpose(0, 2, 1, 3, 4)
+    info_part = info_part.reshape(groups // 2, 1, extra, width)
     pieces = jnp.concatenate(
-        [mine.reshape(groups, rows, width), info_part.reshape(groups, extra, width)], axis=1
+        [
+            mine.reshape(groups, rows, width),
+            jnp.pad(info_part, ((0, 0), (0, 1), (0, 0), (0, 0))).reshape(groups, extra, width),
+        ],
+        axis=1,
     )
-    arrived = lax.all_to_all(pieces, (Y, X), split_axis=0, concat_axis=0, tiled=True)
-    block = over_z(arrived.sum(axis=0))
+    arrived = lax.all_to_all(pieces, NEAR, split_axis=0, concat_axis=0, tiled=True)
+    block = over_far(arrived.sum(axis=0))
     ready = readied(transition.T, filter_cov.T, smoother_gain.T, smoothed_cov, length)
     block, ready = lax.optimization_barrier((block, ready))
     copies = jnp.broadcast_to(block, (groups, *block.shape))
-    own = lax.all_to_all(copies, (Y, X), split_axis=0, concat_axis=0, tiled=True)
+    own = lax.all_to_all(copies, NEAR, split_axis=0, concat_axis=0, tiled=True)
     other = turned(own, CORE, 1)
     power = begun(own, filter_cov.T, transition.T)
     smoothed, shown, total, previous, lagged = scanned(
@@ -451,7 +455,8 @@
 
 
 def solution(mesh):
-    split = Mesh(mesh.devices.reshape(4, 4, 2, mesh.shape["sr"]), (Y, X, CORE, Z))
+    near = mesh.devices.reshape(4, 4, 2, mesh.shape["sr"] // 2, 2)
+    split = Mesh(near, (Y, X, CORE, ZH, ZL))
     in_specs = (P(None, SR_TM), P(SR_TM, None), P(SR_TM), P(), P(), P(), P())
     out_specs = (P(TM, None), P(SR_TM, None), P())
     return jax.shard_map(local, mesh=split, in_specs=in_specs, out_specs=out_specs, check_vma=False)

time: 93.7 us -> 94.3 us (level)
  blocking collectives: 39.2 us -> 20.4 us
  waiting for transfers between devices: 4.89 us -> 20.4 us
  starting transfers between devices: 19.6 us -> 22.3 us
  other arithmetic: 1.3 us -> 2.36 us
    all_to_all x2 -> x1, blocking collectives: 39.2 us -> 20.4 us  [local(): own = lax.all_to_all(copies, NEAR, split_axis=0, concat_axis=0, tiled=True)]
    all_to_all x0 -> x1, waiting for transfers between devices: none -> 18 us  [local(): lax.all_to_all(pieces, NEAR, split_axis=0, concat_axis=0, tiled=True)]
    all_to_all x0 -> x1, starting transfers between devices: none -> 6.8 us  [local(): lax.all_to_all(pieces, NEAR, split_axis=0, concat_axis=0, tiled=True)]
    ppermute x6, starting transfers between devices: 17.9 us -> 15.5 us  [turned(): lax.ppermute(value, axis, [(i, (i + steps) % count) for i in range(count)])]
    ppermute x1 -> x0, starting transfers between devices: 1.73 us -> none  [over_z(): value = value + lax.ppermute(value, Z, [(i, i ^ 1) for i in range(count)])]
    ppermute x1 -> x0, waiting for transfers between devices: 1.39 us -> none  [over_z(): value = value + lax.ppermute(value, Z, [(i, i ^ 1) for i in range(count)])]
    ppermute x6, waiting for transfers between devices: 3.5 us -> 2.35 us  [turned(): lax.ppermute(value, axis, [(i, (i + steps) % count) for i in range(count)])]
    concatenate x1, other arithmetic: 0.08 us -> 1.15 us  [local(): jnp.concatenate([mine.reshape(groups, rows, width), jnp.pad(info_part, ((...]
  transfers between devices with their start and end apart: 7 -> 7, of which waited for: 5 -> 4; matrix products, arithmetic and copies ran while one was open for 1% -> 1% of each run, Pallas kernels for 5% -> 5%
where the time goes in v6:
time: 94.3 us; the launch traced here: 94 us
  Pallas kernels  23.2 us (25%)
  starting transfers between devices  22.3 us (24%)
  waiting for transfers between devices  20.4 us (22%)
  blocking collectives  20.4 us (22%)
  other arithmetic  2.36 us (3%)
  local copies, waits for them, and re-layouts  2.29 us (2%)
  matrix products  2.24 us (2%)
    all_to_all x1, blocking collectives, local(): own = lax.all_to_all(copies, NEAR, split_axis=0, concat_axis=0, tiled=True)  20.4 us
    all_to_all x1, waiting for transfers between devices, local(): lax.all_to_all(pieces, NEAR, split_axis=0, concat_axis=0, tiled=True)  18 us
    ppermute x6, starting transfers between devices, turned(): lax.ppermute(value, axis, [(i, (i + steps) % count) for i in range(count)])  15.5 us
    pallas_call x1, Pallas kernels, scanned(): pl.pallas_call(scan_kernel, out_shape=(jax.ShapeDtypeStruct((length, n),...  14.4 us
    all_to_all x1, starting transfers between devices, local(): lax.all_to_all(pieces, NEAR, split_axis=0, concat_axis=0, tiled=True)  6.8 us
    pallas_call x1, Pallas kernels, inverted(): pl.pallas_call(inverse_kernel, out_shape=(jax.ShapeDtypeStruct(cross.shap...  4.15 us
    pallas_call x1, Pallas kernels, readied(): pl.pallas_call(ready_kernel, out_shape=(jax.ShapeDtypeStruct((count, n, 2...  2.69 us
    ppermute x6, waiting for transfers between devices, turned(): lax.ppermute(value, axis, [(i, (i + steps) % count) for i in range(count)])  2.35 us
  transfers between devices with their start and end apart: 7, of which 4 were waited for; matrix products, arithmetic and copies ran while one was open for 1% of the time, Pallas kernels for 5%

profile of v6, /device:TPU:1, one launch (start us, length us, event | category | flops | bytes accessed | tf_op | source)
XLA Modules:
  0.0 94.0 jit_solution(14302398955092280626)
XLA Ops:
  0.6 1.0 %multiply_convert_fusion = bf16[256,128]{1,0:T(8,128)(2,1)S(1)} fusion(f32[256,128]{1,0:T(8,128)} %param.8, f32[256]{0:T(256)} %param.9), kind=kLoop, calls=%fused_computation.5 | loop fusion | flops 65536 | bytes 197632 | tf_op jit(solution)/shard_map/convert_element_type | solution.py:414
  1.6 1.7 %constant_dynamic-slice_fusion = (bf16[2048,256]{1,0:T(8,128)(2,1)S(1)}, bf16[2048,256]{1,0:T(8,128)(2,1)S(1)}) fusion(bf16[4096,256]{1,0:T(8,128)(2,1)} %param.7, s32[]{:T(128)S(6)} %select_n.7, s32[]{:T(128)S(6)} %select_n.6), kind=kLoop, calls=%fused_computation.8 | loop fusion | bytes 4194312 | tf_op jit(solution)/shard_map/dynamic_slice | solution.py:421
  3.3 0.0 copy-start.4
  3.4 0.4 fusion.4
  3.8 3.3 %collective-permute-start.1 = (f32[2048,128]{1,0:T(8,128)S(1)}, f32[2048,128]{1,0:T(8,128)S(1)}, u32[]{:S(2)}, u32[]{:S(2)}) collective-permute-start(f32[2048,128]{1,0:T(8,128)S(1)} %fusion.4), channel_id=1, source_target_pairs={{0,8},{8,0},{1,9},{9,1},{2,10},{10,2},{3,11},{11,3},{4,12},{12,4},... | collective-permute-start | bytes 3145736 | tf_op jit(solution)/shard_map/ppermute | solution.py:395
  7.1 0.5 convolution_bitcast_fusion.1
  7.6 0.5 collective-permute-start
  8.0 0.4 fusion.3
  8.5 1.0 %collective-permute-done = f32[128,128]{0,1:T(8,128)S(1)} collective-permute-done((f32[128,128]{0,1:T(8,128)S(1)}, f32[128,128]{0,1:T(8,128)S(1)}, u32[]{:S(2)}, u32[]{:S(2)}) %collective-permute-start) | collective-permute-done | bytes 65568 | tf_op jit(solution)/shard_map/ppermute | solution.py:395
  9.5 0.1 copy.15
  9.6 0.1 add.34
  9.7 0.1 copy.14
  9.9 1.2 %pad_maximum_fusion = f32[32,72,128]{2,1,0:T(8,128)} fusion(f32[32,8,128]{2,1,0:T(8,128)S(1)} %bitcast.30, f32[32,64,128]{2,1,0:T(8,128)S(1)} %bitcast.29), kind=kLoop, calls=%fused_computation | loop fusion | flops 294912 | bytes 2359296 | tf_op jit(solution)/shard_map/concatenate | solution.py:431
  11.0 6.8 %all-to-all-start = ((f32[32,72,128]{2,1,0:T(8,128)}), f32[32,72,128]{2,1,0:T(8,128)S(1)}, u32[]{:S(2)}, u32[]{:S(2)}) async-start(f32[32,72,128]{2,1,0:T(8,128)} %pad_maximum_fusion), calls=%async_computation | async-start | bytes 2359296 | tf_op jit(solution)/shard_map/all_to_all | solution.py:438
  17.9 0.1 copy.17
  18.0 0.1 copy.18
  18.1 0.1 copy.19
  18.2 18.0 %all-to-all-done = f32[32,72,128]{2,1,0:T(8,128)S(1)} async-done(((f32[32,72,128]{2,1,0:T(8,128)}), f32[32,72,128]{2,1,0:T(8,128)S(1)}, u32[]{:S(2)}, u32[]{:S(2)}) %all-to-all-start) | async-done | bytes 1179680 | tf_op jit(solution)/shard_map/all_to_all | solution.py:438
  36.2 0.1 reduce_sum.9
  36.3 5.2 %collective-permute-start.4 = (f32[72,128]{1,0:T(8,128)S(1)}, f32[72,128]{1,0:T(8,128)S(1)}, u32[]{:S(2)}, u32[]{:S(2)}) collective-permute-start(f32[72,128]{1,0:T(8,128)S(1)} %reduce_sum.9), channel_id=1, source_target_pairs={{0,6},{2,0},{4,2},{6,4},{1,7},{3,1},{5,3},{7,5},{8,14},{10,8},{12,... | collective-permute-start | bytes 110600 | tf_op jit(solution)/shard_map/ppermute | solution.py:395
  41.5 1.2 %collective-permute-start.3 = (f32[72,128]{1,0:T(8,128)S(1)}, f32[72,128]{1,0:T(8,128)S(1)}, u32[]{:S(2)}, u32[]{:S(2)}) collective-permute-start(f32[72,128]{1,0:T(8,128)S(1)} %reduce_sum.9), channel_id=1, source_target_pairs={{0,4},{2,6},{4,0},{6,2},{1,5},{3,7},{5,1},{7,3},{8,12},{10,14},{12... | collective-permute-start | bytes 110600 | tf_op jit(solution)/shard_map/ppermute | solution.py:395
  42.6 2.1 %collective-permute-start.2 = (f32[72,128]{1,0:T(8,128)S(1)}, f32[72,128]{1,0:T(8,128)S(1)}, u32[]{:S(2)}, u32[]{:S(2)}) collective-permute-start(f32[72,128]{1,0:T(8,128)S(1)} %reduce_sum.9), channel_id=1, source_target_pairs={{0,2},{2,4},{4,6},{6,0},{1,3},{3,5},{5,7},{7,1},{8,10},{10,12},{12... | collective-permute-start | bytes 110600 | tf_op jit(solution)/shard_map/ppermute | solution.py:395
  44.7 2.7 %ready.1 = (bf16[20,128,256]{2,1,0:T(8,128)(2,1)S(1)}, bf16[20,128,128]{2,1,0:T(8,128)(2,1)S(1)}, f32[128,128]{1,0:T(8,128)S(1)}) custom-call(f32[128,128]{1,0:T(8,128)S(1)} %bitcast.23, f32[128,128]{1,0:T(8,128)S(1)} %bitcast.25, f32[128,128]{1,0:T(8,128)S(1)} %bitcast.27, f32[128,128]{1,0:T(8,128)S(1)} %copy-done), custom_call_target="tpu_custom_call" | custom-call | flops 1000000000 | bytes 2000000 | tf_op jit(solution)/shard_map/ready/pallas_call | solution.py:128
  47.5 0.7 collective-permute-done.3
  48.2 0.1 broadcast_in_dim.12
  48.3 20.4 %all_to_all.10.own_ref = f32[32,72,128]{2,1,0:T(8,128)S(1)} all-to-all(f32[32,72,128]{2,1,0:T(8,128)S(1)} %broadcast_in_dim.12), channel_id=1, replica_groups=mesh['tm_0'=4,'tm_1'=4,'tm_2'=2,'sr_0'=4,'sr_1'=2] {'tm_0','tm_1','sr_1'}, dimensions={0} | all-to-all | bytes 2359296 | tf_op jit(solution)/shard_map/all_to_all | solution.py:443
  68.7 3.2 %collective-permute-start.5 = (f32[32,72,128]{2,1,0:T(8,128)S(1)}, f32[32,72,128]{2,1,0:T(8,128)S(1)}, u32[]{:S(2)}, u32[]{:S(2)}) collective-permute-start(f32[32,72,128]{2,1,0:T(8,128)S(1)} %all_to_all.10.own_ref), channel_id=1, source_target_pairs={{0,8},{8,0},{1,9},{9,1},{2,10},{10,2},{3,11},{11,3},{4,12},{12,4},... | collective-permute-start | bytes 3538952 | tf_op jit(solution)/shard_map/ppermute | solution.py:395
  71.9 1.9 %begin.1.power_ref = f32[11,128,128]{2,1,0:T(8,128)S(1)} custom-call(f32[32,72,128]{2,1,0:T(8,128)S(1)} %all_to_all.10.own_ref, f32[128,128]{1,0:T(8,128)S(1)} %bitcast.26, f32[128,128]{1,0:T(8,128)S(1)} %bitcast.24), custom_call_target="tpu_custom_call" | custom-call | flops 1000000000 | bytes 2000000 | tf_op jit(solution)/shard_map/begin/pallas_call | solution.py:160
  73.8 0.6 collective-permute-done.5.other_ref
  74.4 14.4 %scan.1 = (f32[4096,128]{1,0:T(8,128)S(1)}, f32[128,128]{1,0:T(8,128)}, f32[128,128]{1,0:T(8,128)S(1)}, f32[128,128]{1,0:T(8,128)S(1)}, f32[128,128]{1,0:T(8,128)S(1)}) custom-call(s32[1]{0:T(128)} %bitcast.core_ref, s32[1]{0:T(128)} %bitcast.1.place_ref, f32[32,72,128]{2,1,0:T(8,128)S(1)} %all_to_all.10.own_ref, ...), custom_call_target="tpu_custom_call" | custom-call | flops 10000000000 | bytes 5000000 | tf_op jit(solution)/shard_map/scan/pallas_call | solution.py:298
  88.8 1.0 %convolution_bitcast_fusion.cross_ref = f32[256,128]{1,0:T(8,128)S(1)} fusion(bf16[4096,256]{1,0:T(8,128)(2,1)S(1)} %copy-done.3, f32[4096,128]{1,0:T(8,128)S(1)} %get-tuple-element.38), kind=kOutput, calls=%fused_computation.1 | convolution fusion | flops 268959744 | bytes 4325376 | tf_op jit(solution)/shard_map/ts,tk->sk/dot_general | solution.py:450
  89.8 4.1 %inverse.1 = (f32[256,128]{1,0:T(8,128)}, f32[128,128]{1,0:T(8,128)}) custom-call(f32[128,128]{1,0:T(8,128)S(1)} %get-tuple-element.35.total_ref, f32[128,128]{1,0:T(8,128)S(1)} %get-tuple-element.36.previous_ref, f32[128,128]{1,0:T(8,128)S(1)} %get-tuple-element.37.lagged_ref, f32[256,128]{1,0:T(8,128)S(1)} %convolution_bitcast_fusion.cross_ref), custom_call_target="tpu_custom_call" | custom-call | flops 1000000000 | bytes 600000 | tf_op jit(solution)/shard_map/inverse/pallas_call | solution.py:382
  (23 shorter events, 0.1 us)
Async XLA Ops:
  3.3 3.8 %copy-start.4 = (f32[256,128]{1,0:T(8,128)S(1)}, f32[256,128]{1,0:T(8,128)}, u32[]{:S(2)}) copy-start(f32[256,128]{1,0:T(8,128)} %param.8) | copy-start | bytes 393220
  3.3 3.8 %copy-start.8 = (f32[256]{0:T(256)S(1)}, f32[256]{0:T(256)}, u32[]{:S(2)}) copy-start(f32[256]{0:T(256)} %param.9) | copy-start | bytes 3076
  3.8 5.8 %collective-permute-start.1 = (f32[2048,128]{1,0:T(8,128)S(1)}, f32[2048,128]{1,0:T(8,128)S(1)}, u32[]{:S(2)}, u32[]{:S(2)}) collective-permute-start(f32[2048,128]{1,0:T(8,128)S(1)} %fusion.4), channel_id=1, source_target_pairs={{0,8},{8,0},{1,9},{9,1},{2,10},{10,2},{3,11},{11,3},{4,12},{12,4},... | collective-permute-start | bytes 3145736 | tf_op jit(solution)/shard_map/ppermute | solution.py:395
  7.6 1.9 %collective-permute-start = (f32[128,128]{0,1:T(8,128)S(1)}, f32[128,128]{0,1:T(8,128)S(1)}, u32[]{:S(2)}, u32[]{:S(2)}) collective-permute-start(f32[128,128]{0,1:T(8,128)S(1)} %convolution_bitcast_fusion.1), channel_id=1, source_target_pairs={{0,8},{8,0},{1,9},{9,1},{2,10},{10,2},{3,11},{11,3},{4,12},{12,4},... | collective-permute-start | bytes 196616 | tf_op jit(solution)/shard_map/ppermute | solution.py:395
  11.0 6.8 %copy-start.5 = (f32[128,128]{1,0:T(8,128)S(1)}, f32[128,128]{1,0:T(8,128)}, u32[]{:S(2)}) copy-start(f32[128,128]{1,0:T(8,128)} %param.10) | copy-start | bytes 196612
  11.0 6.9 %copy-start.6 = (f32[128,128]{1,0:T(8,128)S(1)}, f32[128,128]{1,0:T(8,128)}, u32[]{:S(2)}) copy-start(f32[128,128]{1,0:T(8,128)} %param.11) | copy-start | bytes 196612
  11.0 7.0 %copy-start.7 = (f32[128,128]{1,0:T(8,128)S(1)}, f32[128,128]{1,0:T(8,128)}, u32[]{:S(2)}) copy-start(f32[128,128]{1,0:T(8,128)} %param.12) | copy-start | bytes 196612
  11.0 25.2 %all-to-all-start = ((f32[32,72,128]{2,1,0:T(8,128)}), f32[32,72,128]{2,1,0:T(8,128)S(1)}, u32[]{:S(2)}, u32[]{:S(2)}) async-start(f32[32,72,128]{2,1,0:T(8,128)} %pad_maximum_fusion), calls=%async_computation | async-start | bytes 2359296 | tf_op jit(solution)/shard_map/all_to_all | solution.py:438
  17.9 26.9 %copy-start = (f32[128,128]{1,0:T(8,128)S(1)}, f32[128,128]{1,0:T(8,128)}, u32[]{:S(2)}) copy-start(f32[128,128]{1,0:T(8,128)} %cov_ref.3) | copy-start | bytes 196612
  36.3 11.2 %collective-permute-start.4 = (f32[72,128]{1,0:T(8,128)S(1)}, f32[72,128]{1,0:T(8,128)S(1)}, u32[]{:S(2)}, u32[]{:S(2)}) collective-permute-start(f32[72,128]{1,0:T(8,128)S(1)} %reduce_sum.9), channel_id=1, source_target_pairs={{0,6},{2,0},{4,2},{6,4},{1,7},{3,1},{5,3},{7,5},{8,14},{10,8},{12,... | collective-permute-start | bytes 110600 | tf_op jit(solution)/shard_map/ppermute | solution.py:395
  41.5 6.7 %collective-permute-start.3 = (f32[72,128]{1,0:T(8,128)S(1)}, f32[72,128]{1,0:T(8,128)S(1)}, u32[]{:S(2)}, u32[]{:S(2)}) collective-permute-start(f32[72,128]{1,0:T(8,128)S(1)} %reduce_sum.9), channel_id=1, source_target_pairs={{0,4},{2,6},{4,0},{6,2},{1,5},{3,7},{5,1},{7,3},{8,12},{10,14},{12... | collective-permute-start | bytes 110600 | tf_op jit(solution)/shard_map/ppermute | solution.py:395
  42.6 5.6 %collective-permute-start.2 = (f32[72,128]{1,0:T(8,128)S(1)}, f32[72,128]{1,0:T(8,128)S(1)}, u32[]{:S(2)}, u32[]{:S(2)}) collective-permute-start(f32[72,128]{1,0:T(8,128)S(1)} %reduce_sum.9), channel_id=1, source_target_pairs={{0,2},{2,4},{4,6},{6,0},{1,3},{3,5},{5,7},{7,1},{8,10},{10,12},{12... | collective-permute-start | bytes 110600 | tf_op jit(solution)/shard_map/ppermute | solution.py:395
  47.4 21.3 %copy-start.1 = (bf16[20,128,256]{2,1,0:T(8,128)(2,1)}, bf16[20,128,256]{2,1,0:T(8,128)(2,1)S(1)}, u32[]{:S(2)}) copy-start(bf16[20,128,256]{2,1,0:T(8,128)(2,1)S(1)} %get-tuple-element.31.both_ref) | copy-start | bytes 3932164
  68.7 5.7 %collective-permute-start.5 = (f32[32,72,128]{2,1,0:T(8,128)S(1)}, f32[32,72,128]{2,1,0:T(8,128)S(1)}, u32[]{:S(2)}, u32[]{:S(2)}) collective-permute-start(f32[32,72,128]{2,1,0:T(8,128)S(1)} %all_to_all.10.own_ref), channel_id=1, source_target_pairs={{0,8},{8,0},{1,9},{9,1},{2,10},{10,2},{3,11},{11,3},{4,12},{12,4},... | collective-permute-start | bytes 3538952 | tf_op jit(solution)/shard_map/ppermute | solution.py:395
  71.9 2.5 %copy-start.2 = (bf16[20,128,256]{2,1,0:T(8,128)(2,1)S(1)}, bf16[20,128,256]{2,1,0:T(8,128)(2,1)}, u32[]{:S(2)}) copy-start(bf16[20,128,256]{2,1,0:T(8,128)(2,1)} %copy-done.1) | copy-start | bytes 3932164
  74.4 14.4 %copy-start.3 = (bf16[4096,256]{1,0:T(8,128)(2,1)S(1)}, bf16[4096,256]{1,0:T(8,128)(2,1)}, u32[]{:S(2)}) copy-start(bf16[4096,256]{1,0:T(8,128)(2,1)} %param.7) | copy-start | bytes 6291460

commit v7 on v6

--- a/solution.py
+++ b/solution.py
@@ -1,6 +1,7 @@
 import jax
 import jax.numpy as jnp
 from jax import lax
+from jax.experimental.layout import Layout, with_layout_constraint
 from jax.experimental import pallas as pl
 from jax.experimental.pallas import tpu as pltpu
 from jax.sharding import Mesh
@@ -415,16 +416,12 @@
 
     info_part = jnp.dot(loadings.T, weighted, precision=precise, preferred_element_type=f32)
     info_part = info_part + turned(info_part, CORE, 1)
-    kept_rows, given_rows, factors = lax.optimization_barrier(
-        (
-            lax.dynamic_slice_in_dim(observations, core * half, half, 0),
-            lax.dynamic_slice_in_dim(observations, (1 - core) * half, half, 0),
-            scaled,
-        )
-    )
-    given = jnp.dot(given_rows, factors, preferred_element_type=f32)
-    mine = jnp.dot(kept_rows, factors, preferred_element_type=f32)
-    mine, info_part = lax.optimization_barrier((mine, info_part))
+    window, factors = lax.optimization_barrier((observations, scaled))
+    whole = jnp.dot(window, factors, preferred_element_type=f32)
+    whole = with_layout_constraint(whole, Layout(major_to_minor=(0, 1)))
+    given = lax.dynamic_slice_in_dim(whole, (1 - core) * half, half, 0)
+    mine = lax.dynamic_slice_in_dim(whole, core * half, half, 0)
+    given, mine = lax.optimization_barrier((given, mine))
     mine = mine + turned(given, CORE, 1)
     mine = mine.reshape(groups // 2, rows // STEPS, 2, STEPS, width).transpose(0, 2, 1, 3, 4)
     info_part = info_part.reshape(groups // 2, 1, extra, width)
@@ -436,6 +433,9 @@
         axis=1,
     )
     arrived = lax.all_to_all(pieces, NEAR, split_axis=0, concat_axis=0, tiled=True)
+    arrived, transition, filter_cov, smoother_gain, smoothed_cov = lax.optimization_barrier(
+        (arrived, transition, filter_cov, smoother_gain, smoothed_cov)
+    )
     block = over_far(arrived.sum(axis=0))
     ready = readied(transition.T, filter_cov.T, smoother_gain.T, smoothed_cov, length)
     block, ready = lax.optimization_barrier((block, ready))

time: 94.3 us -> 95.5 us (1.013)
  blocking collectives: 20.4 us -> 45.7 us
  waiting for transfers between devices: 20.4 us -> 1.9 us
  starting transfers between devices: 22.3 us -> 15.8 us
  Pallas kernels: 23.2 us -> 24.4 us
    all_to_all x0 -> x1, blocking collectives: none -> 25 us  [local(): lax.all_to_all(pieces, NEAR, split_axis=0, concat_axis=0, tiled=True)]
    all_to_all x1 -> x0, waiting for transfers between devices: 18 us -> none  [local(): lax.all_to_all(pieces, NEAR, split_axis=0, concat_axis=0, tiled=True)]
    all_to_all x1 -> x0, starting transfers between devices: 6.8 us -> none  [local(): lax.all_to_all(pieces, NEAR, split_axis=0, concat_axis=0, tiled=True)]
    dynamic_slice x1, local copies, waits for them, and re-layouts: 1.69 us -> 0.15 us  [local(): mine = lax.dynamic_slice_in_dim(whole, core * half, half, 0)]
    pallas_call x1, Pallas kernels: 14.4 us -> 15.7 us  [scanned(): pl.pallas_call(scan_kernel, out_shape=(jax.ShapeDtypeStruct((length, n),...]
    unnamed x21 -> x20, local copies, waits for them, and re-layouts: 0.31 us -> 1.47 us
    concatenate x1, other arithmetic: 1.15 us -> 0.1 us  [local(): jnp.concatenate([mine.reshape(groups, rows, width), jnp.pad(info_part, ((...]
    optimization_barrier x1 -> x3, local copies, waits for them, and re-layouts: 0.09 us -> 1.11 us  [local(): lax.optimization_barrier((arrived, transition, filter_cov, smoother_gain,...]
  transfers between devices with their start and end apart: 7 -> 6, of which waited for: 4 -> 2; matrix products, arithmetic and copies ran while one was open for 1% -> 2% of each run, Pallas kernels for 5% -> 5%
where the time goes in v7:
time: 95.5 us; the launch traced here: 95.2 us
  blocking collectives  45.7 us (48%)
  Pallas kernels  24.4 us (26%)
  starting transfers between devices  15.8 us (17%)
  local copies, waits for them, and re-layouts  2.93 us (3%)
  matrix products  2.06 us (2%)
  waiting for transfers between devices  1.9 us (2%)
  other arithmetic  1.5 us (2%)
    all_to_all x1, blocking collectives, local(): lax.all_to_all(pieces, NEAR, split_axis=0, concat_axis=0, tiled=True)  25 us
    all_to_all x1, blocking collectives, local(): own = lax.all_to_all(copies, NEAR, split_axis=0, concat_axis=0, tiled=True)  20.8 us
    ppermute x6, starting transfers between devices, turned(): lax.ppermute(value, axis, [(i, (i + steps) % count) for i in range(count)])  15.8 us
    pallas_call x1, Pallas kernels, scanned(): pl.pallas_call(scan_kernel, out_shape=(jax.ShapeDtypeStruct((length, n),...  15.7 us
    pallas_call x1, Pallas kernels, inverted(): pl.pallas_call(inverse_kernel, out_shape=(jax.ShapeDtypeStruct(cross.shap...  4.15 us
    pallas_call x1, Pallas kernels, readied(): pl.pallas_call(ready_kernel, out_shape=(jax.ShapeDtypeStruct((count, n, 2...  2.7 us
  transfers between devices with their start and end apart: 6, of which 2 were waited for; matrix products, arithmetic and copies ran while one was open for 2% of the time, Pallas kernels for 5%

profile of v7, /device:TPU:1, one launch (start us, length us, event | category | flops | bytes accessed | tf_op | source)
XLA Modules:
  0.0 95.2 jit_solution(3688186210440001042)
XLA Ops:
  0.6 0.0 copy-start
  0.7 1.1 %multiply_convert_fusion = bf16[256,128]{1,0:T(8,128)(2,1)S(1)} fusion(f32[256,128]{1,0:T(8,128)} %param.8, f32[256]{0:T(256)} %param.9), kind=kLoop, calls=%fused_computation.5 | loop fusion | flops 65536 | bytes 197632 | tf_op jit(solution)/shard_map/convert_element_type | solution.py:415
  1.8 0.5 copy-done
  2.3 0.7 fusion.3
  3.0 0.0 copy-start.9
  3.0 0.1 constant_dynamic-slice_fusion
  3.2 3.3 %collective-permute-start = (f32[2048,128]{1,0:T(8,128)S(1)}, f32[2048,128]{1,0:T(8,128)S(1)}, u32[]{:S(2)}, u32[]{:S(2)}) collective-permute-start(f32[2048,128]{1,0:T(8,128)S(1)} %get-tuple-element.29), channel_id=1, source_target_pairs={{0,8},{8,0},{1,9},{9,1},{2,10},{10,2},{3,11},{11,3},{4,12},{12,4},... | collective-permute-start | bytes 3145736 | tf_op jit(solution)/shard_map/ppermute | solution.py:396
  6.5 0.4 convolution_bitcast_fusion.1
  7.0 0.7 collective-permute-start.1
  7.7 1.2 %collective-permute-done.1 = f32[128,128]{1,0:T(8,128)S(1)} collective-permute-done((f32[128,128]{1,0:T(8,128)S(1)}, f32[128,128]{1,0:T(8,128)S(1)}, u32[]{:S(2)}, u32[]{:S(2)}) %collective-permute-start.1) | collective-permute-done | bytes 65568 | tf_op jit(solution)/shard_map/ppermute | solution.py:396
  8.9 0.2 add.33
  9.1 0.1 copy.14
  9.2 0.1 pad_maximum_fusion
  9.3 0.0 copy-start.7
  9.4 25.0 %all_to_all.10 = f32[32,72,128]{2,1,0:T(8,128)S(1)} all-to-all(f32[32,72,128]{2,1,0:T(8,128)S(1)} %pad_maximum_fusion), channel_id=1, replica_groups=mesh['tm_0'=4,'tm_1'=4,'tm_2'=2,'sr_0'=4,'sr_1'=2] {'tm_0','tm_1','sr_1'}, dimensions={0} | all-to-all | bytes 2359296 | tf_op jit(solution)/shard_map/all_to_all | solution.py:435
  34.3 0.1 reduce_sum.9
  34.4 5.2 %collective-permute-start.4 = (f32[72,128]{1,0:T(8,128)S(1)}, f32[72,128]{1,0:T(8,128)S(1)}, u32[]{:S(2)}, u32[]{:S(2)}) collective-permute-start(f32[72,128]{1,0:T(8,128)S(1)} %reduce_sum.9), channel_id=1, source_target_pairs={{0,6},{2,0},{4,2},{6,4},{1,7},{3,1},{5,3},{7,5},{8,14},{10,8},{12,... | collective-permute-start | bytes 110600 | tf_op jit(solution)/shard_map/ppermute | solution.py:396
  39.6 1.2 %collective-permute-start.3 = (f32[72,128]{1,0:T(8,128)S(1)}, f32[72,128]{1,0:T(8,128)S(1)}, u32[]{:S(2)}, u32[]{:S(2)}) collective-permute-start(f32[72,128]{1,0:T(8,128)S(1)} %reduce_sum.9), channel_id=1, source_target_pairs={{0,4},{2,6},{4,0},{6,2},{1,5},{3,7},{5,1},{7,3},{8,12},{10,14},{12... | collective-permute-start | bytes 110600 | tf_op jit(solution)/shard_map/ppermute | solution.py:396
  40.8 2.1 %collective-permute-start.2 = (f32[72,128]{1,0:T(8,128)S(1)}, f32[72,128]{1,0:T(8,128)S(1)}, u32[]{:S(2)}, u32[]{:S(2)}) collective-permute-start(f32[72,128]{1,0:T(8,128)S(1)} %reduce_sum.9), channel_id=1, source_target_pairs={{0,2},{2,4},{4,6},{6,0},{1,3},{3,5},{5,7},{7,1},{8,10},{10,12},{12... | collective-permute-start | bytes 110600 | tf_op jit(solution)/shard_map/ppermute | solution.py:396
  42.9 0.1 copy.16
  43.0 0.1 copy.17
  43.1 0.9 copy.18
  44.0 2.7 %ready.1 = (bf16[20,128,256]{2,1,0:T(8,128)(2,1)S(1)}, bf16[20,128,128]{2,1,0:T(8,128)(2,1)S(1)}, f32[128,128]{1,0:T(8,128)S(1)}) custom-call(f32[128,128]{1,0:T(8,128)S(1)} %bitcast.22, f32[128,128]{1,0:T(8,128)S(1)} %bitcast.24, f32[128,128]{1,0:T(8,128)S(1)} %bitcast.26, f32[128,128]{1,0:T(8,128)S(1)} %copy-done.1), custom_call_target="tpu_custom_call" | custom-call | flops 1000000000 | bytes 2000000 | tf_op jit(solution)/shard_map/ready/pallas_call | solution.py:129
  46.8 0.1 broadcast_in_dim.12
  46.9 0.9 copy-done.2
  47.8 20.8 %all_to_all.11.own_ref = f32[32,72,128]{2,1,0:T(8,128)S(1)} all-to-all(f32[32,72,128]{2,1,0:T(8,128)S(1)} %broadcast_in_dim.12), channel_id=1, replica_groups=mesh['tm_0'=4,'tm_1'=4,'tm_2'=2,'sr_0'=4,'sr_1'=2] {'tm_0','tm_1','sr_1'}, dimensions={0} | all-to-all | bytes 2359296 | tf_op jit(solution)/shard_map/all_to_all | solution.py:443
  68.6 3.2 %collective-permute-start.5 = (f32[32,72,128]{2,1,0:T(8,128)S(1)}, f32[32,72,128]{2,1,0:T(8,128)}, u32[]{:S(2)}, u32[]{:S(2)}) collective-permute-start(f32[32,72,128]{2,1,0:T(8,128)S(1)} %all_to_all.11.own_ref), channel_id=1, source_target_pairs={{0,8},{8,0},{1,9},{9,1},{2,10},{10,2},{3,11},{11,3},{4,12},{12,4},... | collective-permute-start | bytes 3538952 | tf_op jit(solution)/shard_map/ppermute | solution.py:396
  71.8 1.9 %begin.1.power_ref = f32[11,128,128]{2,1,0:T(8,128)S(1)} custom-call(f32[32,72,128]{2,1,0:T(8,128)S(1)} %all_to_all.11.own_ref, f32[128,128]{1,0:T(8,128)S(1)} %bitcast.25, f32[128,128]{1,0:T(8,128)S(1)} %bitcast.23), custom_call_target="tpu_custom_call" | custom-call | flops 1000000000 | bytes 2000000 | tf_op jit(solution)/shard_map/begin/pallas_call | solution.py:161
  73.7 0.7 collective-permute-done.5.other_ref
  74.4 15.7 %scan.1 = (f32[4096,128]{1,0:T(8,128)S(1)}, f32[128,128]{1,0:T(8,128)}, f32[128,128]{1,0:T(8,128)S(1)}, f32[128,128]{1,0:T(8,128)S(1)}, f32[128,128]{1,0:T(8,128)S(1)}) custom-call(s32[1]{0:T(128)} %bitcast.core_ref, s32[1]{0:T(128)} %bitcast.1.place_ref, f32[32,72,128]{2,1,0:T(8,128)S(1)} %all_to_all.11.own_ref, ...), custom_call_target="tpu_custom_call" | custom-call | flops 10000000000 | bytes 5000000 | tf_op jit(solution)/shard_map/scan/pallas_call | solution.py:299
  90.1 0.9 convolution_bitcast_fusion.cross_ref
  91.0 4.1 %inverse.1 = (f32[256,128]{1,0:T(8,128)}, f32[128,128]{1,0:T(8,128)}) custom-call(f32[128,128]{1,0:T(8,128)S(1)} %get-tuple-element.43.total_ref, f32[128,128]{1,0:T(8,128)S(1)} %get-tuple-element.44.previous_ref, f32[128,128]{1,0:T(8,128)S(1)} %get-tuple-element.45.lagged_ref, f32[256,128]{1,0:T(8,128)S(1)} %convolution_bitcast_fusion.cross_ref), custom_call_target="tpu_custom_call" | custom-call | flops 1000000000 | bytes 600000 | tf_op jit(solution)/shard_map/inverse/pallas_call | solution.py:383
  (22 shorter events, 0.1 us)
Async XLA Ops:
  0.6 1.7 %copy-start = (bf16[4096,256]{1,0:T(8,128)(2,1)S(1)}, bf16[4096,256]{1,0:T(8,128)(2,1)}, u32[]{:S(2)}) copy-start(bf16[4096,256]{1,0:T(8,128)(2,1)} %param.7) | copy-start | bytes 6291460
  3.0 3.5 %copy-start.6 = (f32[256,128]{1,0:T(8,128)S(1)}, f32[256,128]{1,0:T(8,128)}, u32[]{:S(2)}) copy-start(f32[256,128]{1,0:T(8,128)} %param.8) | copy-start | bytes 393220
  3.0 3.5 %copy-start.9 = (f32[256]{0:T(256)S(1)}, f32[256]{0:T(256)}, u32[]{:S(2)}) copy-start(f32[256]{0:T(256)} %param.9) | copy-start | bytes 3076
  3.2 5.7 %collective-permute-start = (f32[2048,128]{1,0:T(8,128)S(1)}, f32[2048,128]{1,0:T(8,128)S(1)}, u32[]{:S(2)}, u32[]{:S(2)}) collective-permute-start(f32[2048,128]{1,0:T(8,128)S(1)} %get-tuple-element.29), channel_id=1, source_target_pairs={{0,8},{8,0},{1,9},{9,1},{2,10},{10,2},{3,11},{11,3},{4,12},{12,4},... | collective-permute-start | bytes 3145736 | tf_op jit(solution)/shard_map/ppermute | solution.py:396
  7.0 1.9 %collective-permute-start.1 = (f32[128,128]{1,0:T(8,128)S(1)}, f32[128,128]{1,0:T(8,128)S(1)}, u32[]{:S(2)}, u32[]{:S(2)}) collective-permute-start(f32[128,128]{1,0:T(8,128)S(1)} %convolution_bitcast_fusion.1), channel_id=1, source_target_pairs={{0,8},{8,0},{1,9},{9,1},{2,10},{10,2},{3,11},{11,3},{4,12},{12,4},... | collective-permute-start | bytes 196616 | tf_op jit(solution)/shard_map/ppermute | solution.py:396
  9.3 33.5 %copy-start.7 = (f32[128,128]{1,0:T(8,128)S(1)}, f32[128,128]{1,0:T(8,128)}, u32[]{:S(2)}) copy-start(f32[128,128]{1,0:T(8,128)} %param.10) | copy-start | bytes 196612
  9.3 33.6 %copy-start.8 = (f32[128,128]{1,0:T(8,128)S(1)}, f32[128,128]{1,0:T(8,128)}, u32[]{:S(2)}) copy-start(f32[128,128]{1,0:T(8,128)} %param.11) | copy-start | bytes 196612
  9.3 34.6 %copy-start.1 = (f32[128,128]{1,0:T(8,128)S(1)}, f32[128,128]{1,0:T(8,128)}, u32[]{:S(2)}) copy-start(f32[128,128]{1,0:T(8,128)} %cov_ref.1) | copy-start | bytes 196612
  34.4 12.3 %collective-permute-start.4 = (f32[72,128]{1,0:T(8,128)S(1)}, f32[72,128]{1,0:T(8,128)S(1)}, u32[]{:S(2)}, u32[]{:S(2)}) collective-permute-start(f32[72,128]{1,0:T(8,128)S(1)} %reduce_sum.9), channel_id=1, source_target_pairs={{0,6},{2,0},{4,2},{6,4},{1,7},{3,1},{5,3},{7,5},{8,14},{10,8},{12,... | collective-permute-start | bytes 110600 | tf_op jit(solution)/shard_map/ppermute | solution.py:396
  39.6 7.2 %collective-permute-start.3 = (f32[72,128]{1,0:T(8,128)S(1)}, f32[72,128]{1,0:T(8,128)S(1)}, u32[]{:S(2)}, u32[]{:S(2)}) collective-permute-start(f32[72,128]{1,0:T(8,128)S(1)} %reduce_sum.9), channel_id=1, source_target_pairs={{0,4},{2,6},{4,0},{6,2},{1,5},{3,7},{5,1},{7,3},{8,12},{10,14},{12... | collective-permute-start | bytes 110600 | tf_op jit(solution)/shard_map/ppermute | solution.py:396
  40.8 6.0 %collective-permute-start.2 = (f32[72,128]{1,0:T(8,128)S(1)}, f32[72,128]{1,0:T(8,128)S(1)}, u32[]{:S(2)}, u32[]{:S(2)}) collective-permute-start(f32[72,128]{1,0:T(8,128)S(1)} %reduce_sum.9), channel_id=1, source_target_pairs={{0,2},{2,4},{4,6},{6,0},{1,3},{3,5},{5,7},{7,1},{8,10},{10,12},{12... | collective-permute-start | bytes 110600 | tf_op jit(solution)/shard_map/ppermute | solution.py:396
  46.7 1.1 %copy-start.2 = (bf16[20,128,256]{2,1,0:T(8,128)(2,1)}, bf16[20,128,256]{2,1,0:T(8,128)(2,1)S(1)}, u32[]{:S(2)}) copy-start(bf16[20,128,256]{2,1,0:T(8,128)(2,1)S(1)} %get-tuple-element.39.both_ref) | copy-start | bytes 3932164
  46.7 21.8 %copy-start.4 = (bf16[20,128,128]{2,1,0:T(8,128)(2,1)}, bf16[20,128,128]{2,1,0:T(8,128)(2,1)S(1)}, u32[]{:S(2)}) copy-start(bf16[20,128,128]{2,1,0:T(8,128)(2,1)S(1)} %get-tuple-element.40.small_ref) | copy-start | bytes 1966084
  68.6 5.9 %collective-permute-start.5 = (f32[32,72,128]{2,1,0:T(8,128)S(1)}, f32[32,72,128]{2,1,0:T(8,128)}, u32[]{:S(2)}, u32[]{:S(2)}) collective-permute-start(f32[32,72,128]{2,1,0:T(8,128)S(1)} %all_to_all.11.own_ref), channel_id=1, source_target_pairs={{0,8},{8,0},{1,9},{9,1},{2,10},{10,2},{3,11},{11,3},{4,12},{12,4},... | collective-permute-start | bytes 3538952 | tf_op jit(solution)/shard_map/ppermute | solution.py:396
  71.8 2.6 %copy-start.3 = (bf16[20,128,256]{2,1,0:T(8,128)(2,1)S(1)}, bf16[20,128,256]{2,1,0:T(8,128)(2,1)}, u32[]{:S(2)}) copy-start(bf16[20,128,256]{2,1,0:T(8,128)(2,1)} %copy-done.2) | copy-start | bytes 3932164
  71.8 2.6 %copy-start.5 = (bf16[20,128,128]{2,1,0:T(8,128)(2,1)S(1)}, bf16[20,128,128]{2,1,0:T(8,128)(2,1)}, u32[]{:S(2)}) copy-start(bf16[20,128,128]{2,1,0:T(8,128)(2,1)} %copy-done.4) | copy-start | bytes 1966084

commit v8 on v5

--- a/solution.py
+++ b/solution.py
@@ -412,19 +412,19 @@
     groups = lax.axis_size((Y, X))
     rows = half // groups
     extra = width // groups
-    weighted = noise_precision[:, None] * loadings
-    scaled = weighted.astype(bf16)
-
-    info_part = jnp.dot(loadings.T, weighted, precision=precise, preferred_element_type=f32)
-    info_part = info_part + turned(info_part, CORE, 1)
-    kept_rows, given_rows, factors = lax.optimization_barrier(
+    kept_rows, given_rows, loadings, noise_precision = lax.optimization_barrier(
         (
             lax.dynamic_slice_in_dim(observations, core * half, half, 0),
             lax.dynamic_slice_in_dim(observations, (1 - core) * half, half, 0),
-            scaled,
+            loadings,
+            noise_precision,
         )
     )
+    weighted = noise_precision[:, None] * loadings
+    factors = lax.optimization_barrier(weighted.astype(bf16))
     given = jnp.dot(given_rows, factors, preferred_element_type=f32)
+    info_part = jnp.dot(loadings.T, weighted, precision=precise, preferred_element_type=f32)
+    info_part = info_part + turned(info_part, CORE, 1)
     mine = jnp.dot(kept_rows, factors, preferred_element_type=f32)
     mine, info_part = lax.optimization_barrier((mine, info_part))
     mine = mine + turned(given, CORE, 1)

time: 93.7 us -> 92.7 us (0.989)
  no operation moved by 1% of the time
where the time goes in v8:
time: 92.7 us; the launch traced here: 92.5 us
  blocking collectives  39.2 us (42%)
  Pallas kernels  23.2 us (25%)
  starting transfers between devices  19.3 us (21%)
  waiting for transfers between devices  5.27 us (6%)
  matrix products  2.24 us (2%)
  local copies, waits for them, and re-layouts  2.1 us (2%)
    all_to_all x1, blocking collectives, local(): lax.all_to_all(pieces, (Y, X), split_axis=0, concat_axis=0, tiled=True)  22 us
    ppermute x6, starting transfers between devices, turned(): lax.ppermute(value, axis, [(i, (i + steps) % count) for i in range(count)])  17.5 us
    all_to_all x1, blocking collectives, local(): lax.all_to_all(copies, (Y, X), split_axis=0, concat_axis=0, tiled=True)  17.2 us
    pallas_call x1, Pallas kernels, scanned(): pl.pallas_call(scan_kernel, out_shape=(jax.ShapeDtypeStruct((length, n),...  14.5 us
    pallas_call x1, Pallas kernels, inverted(): pl.pallas_call(inverse_kernel, out_shape=(jax.ShapeDtypeStruct(cross.shap...  4.15 us
    ppermute x6, waiting for transfers between devices, turned(): lax.ppermute(value, axis, [(i, (i + steps) % count) for i in range(count)])  3.88 us
    pallas_call x1, Pallas kernels, readied(): pl.pallas_call(ready_kernel, out_shape=(jax.ShapeDtypeStruct((count, n, 2...  2.69 us
    pallas_call x1, Pallas kernels, begun(): pl.pallas_call(begin_kernel, out_shape=jax.ShapeDtypeStruct((STEPS + LEAP...  1.9 us
  transfers between devices with their start and end apart: 7, of which 5 were waited for; matrix products, arithmetic and copies ran while one was open for 1% of the time, Pallas kernels for 5%

profile of v8, /device:TPU:1, one launch (start us, length us, event | category | flops | bytes accessed | tf_op | source)
XLA Modules:
  0.0 92.5 jit_solution(11017332070806361224)
XLA Ops:
  0.7 1.7 %constant_dynamic-slice_fusion = (bf16[2048,256]{1,0:T(8,128)(2,1)S(1)}, bf16[2048,256]{1,0:T(8,128)(2,1)S(1)}) fusion(bf16[4096,256]{1,0:T(8,128)(2,1)} %param.7, s32[]{:T(128)S(6)} %select_n.7, s32[]{:T(128)S(6)} %select_n.6), kind=kLoop, calls=%fused_computation.8 | loop fusion | bytes 4194312 | tf_op jit(solution)/shard_map/dynamic_slice | solution.py:418
  2.4 0.1 multiply_convert_fusion
  2.5 0.4 fusion.5
  2.9 3.3 %collective-permute-start.1 = (f32[2048,128]{1,0:T(8,128)S(1)}, f32[2048,128]{1,0:T(8,128)S(1)}, u32[]{:S(2)}, u32[]{:S(2)}) collective-permute-start(f32[2048,128]{1,0:T(8,128)S(1)} %fusion.5), channel_id=1, source_target_pairs={{0,8},{8,0},{1,9},{9,1},{2,10},{10,2},{3,11},{11,3},{4,12},{12,4},... | collective-permute-start | bytes 3145736 | tf_op jit(solution)/shard_map/ppermute | solution.py:394
  6.3 0.4 fusion.1
  6.7 0.1 collective-permute-start
  6.8 0.4 fusion.4
  7.2 1.4 %collective-permute-done = f32[128,128]{1,0:T(8,128)S(1)} collective-permute-done((f32[128,128]{1,0:T(8,128)S(1)}, f32[128,128]{1,0:T(8,128)S(1)}, u32[]{:S(2)}, u32[]{:S(2)}) %collective-permute-start) | collective-permute-done | bytes 65568 | tf_op jit(solution)/shard_map/ppermute | solution.py:394
  8.7 0.1 add.35
  8.8 0.1 pad_maximum_fusion
  8.9 0.0 copy-start.5
  8.9 22.0 %all_to_all.10 = f32[16,136,128]{2,1,0:T(8,128)S(1)} all-to-all(f32[16,136,128]{2,1,0:T(8,128)S(1)} %pad_maximum_fusion), channel_id=1, replica_groups=mesh['tm_0'=4,'tm_1'=4,'tm_2'=2,'sr'=8] {'tm_0','tm_1'}, dimensions={0} | all-to-all | bytes 2228224 | tf_op jit(solution)/shard_map/all_to_all | solution.py:434
  30.9 0.1 reduce_sum.9
  31.0 1.7 %collective-permute-start.2 = (f32[136,128]{1,0:T(8,128)S(1)}, f32[136,128]{1,0:T(8,128)S(1)}, u32[]{:S(2)}, u32[]{:S(2)}) collective-permute-start(f32[136,128]{1,0:T(8,128)S(1)} %reduce_sum.9), channel_id=1, source_target_pairs={{0,1},{1,0},{2,3},{3,2},{4,5},{5,4},{6,7},{7,6},{8,9},{9,8},{10,11... | collective-permute-start | bytes 208904 | tf_op jit(solution)/shard_map/ppermute | solution.py:399
  32.7 0.1 copy.10
  32.8 0.1 copy.11
  32.9 0.1 copy.12
  33.0 1.4 %collective-permute-done.2 = f32[136,128]{1,0:T(8,128)S(1)} collective-permute-done((f32[136,128]{1,0:T(8,128)S(1)}, f32[136,128]{1,0:T(8,128)S(1)}, u32[]{:S(2)}, u32[]{:S(2)}) %collective-permute-start.2) | collective-permute-done | bytes 69664 | tf_op jit(solution)/shard_map/ppermute | solution.py:399
  34.4 5.9 %collective-permute-start.5 = (f32[136,128]{1,0:T(8,128)S(1)}, f32[136,128]{1,0:T(8,128)S(1)}, u32[]{:S(2)}, u32[]{:S(2)}) collective-permute-start(f32[136,128]{1,0:T(8,128)S(1)} %add.36), channel_id=1, source_target_pairs={{0,6},{1,7},{2,0},{3,1},{4,2},{5,3},{6,4},{7,5},{8,14},{9,15},{10,... | collective-permute-start | bytes 208904 | tf_op jit(solution)/shard_map/ppermute | solution.py:394
  40.3 1.0 %collective-permute-start.4 = (f32[136,128]{1,0:T(8,128)S(1)}, f32[136,128]{1,0:T(8,128)S(1)}, u32[]{:S(2)}, u32[]{:S(2)}) collective-permute-start(f32[136,128]{1,0:T(8,128)S(1)} %add.36), channel_id=1, source_target_pairs={{0,4},{1,5},{2,6},{3,7},{4,0},{5,1},{6,2},{7,3},{8,12},{9,13},{10,... | collective-permute-start | bytes 208904 | tf_op jit(solution)/shard_map/ppermute | solution.py:394
  41.3 2.3 %collective-permute-start.3 = (f32[136,128]{1,0:T(8,128)S(1)}, f32[136,128]{1,0:T(8,128)S(1)}, u32[]{:S(2)}, u32[]{:S(2)}) collective-permute-start(f32[136,128]{1,0:T(8,128)S(1)} %add.36), channel_id=1, source_target_pairs={{0,2},{1,3},{2,4},{3,5},{4,6},{5,7},{6,0},{7,1},{8,10},{9,11},{10,... | collective-permute-start | bytes 208904 | tf_op jit(solution)/shard_map/ppermute | solution.py:394
  43.6 2.7 %ready.1 = (bf16[20,128,256]{2,1,0:T(8,128)(2,1)S(1)}, bf16[20,128,128]{2,1,0:T(8,128)(2,1)S(1)}, f32[128,128]{1,0:T(8,128)S(1)}) custom-call(f32[128,128]{1,0:T(8,128)S(1)} %bitcast.15, f32[128,128]{1,0:T(8,128)S(1)} %bitcast.17, f32[128,128]{1,0:T(8,128)S(1)} %bitcast.19, f32[128,128]{1,0:T(8,128)S(1)} %copy-done), custom_call_target="tpu_custom_call" | custom-call | flops 1000000000 | bytes 2000000 | tf_op jit(solution)/shard_map/ready/pallas_call | solution.py:127
  46.3 1.3 %collective-permute-done.4 = f32[136,128]{1,0:T(8,128)S(1)} collective-permute-done((f32[136,128]{1,0:T(8,128)S(1)}, f32[136,128]{1,0:T(8,128)S(1)}, u32[]{:S(2)}, u32[]{:S(2)}) %collective-permute-start.4) | collective-permute-done | bytes 69664 | tf_op jit(solution)/shard_map/ppermute | solution.py:394
  47.6 0.7 collective-permute-done.3
  48.3 0.1 broadcast_in_dim.12
  48.4 17.2 %all_to_all.11.own_ref = f32[16,136,128]{2,1,0:T(8,128)S(1)} all-to-all(f32[16,136,128]{2,1,0:T(8,128)S(1)} %broadcast_in_dim.12), channel_id=1, replica_groups=mesh['tm_0'=4,'tm_1'=4,'tm_2'=2,'sr'=8] {'tm_0','tm_1'}, dimensions={0} | all-to-all | bytes 2228224 | tf_op jit(solution)/shard_map/all_to_all | solution.py:439
  65.6 4.9 %collective-permute-start.6 = (f32[16,136,128]{2,1,0:T(8,128)S(1)}, f32[16,136,128]{2,1,0:T(8,128)S(1)}, u32[]{:S(2)}, u32[]{:S(2)}) collective-permute-start(f32[16,136,128]{2,1,0:T(8,128)S(1)} %all_to_all.11.own_ref), channel_id=1, source_target_pairs={{0,8},{8,0},{1,9},{9,1},{2,10},{10,2},{3,11},{11,3},{4,12},{12,4},... | collective-permute-start | bytes 3342344 | tf_op jit(solution)/shard_map/ppermute | solution.py:394
  70.5 1.9 %begin.1.power_ref = f32[11,128,128]{2,1,0:T(8,128)S(1)} custom-call(f32[16,136,128]{2,1,0:T(8,128)S(1)} %all_to_all.11.own_ref, f32[128,128]{1,0:T(8,128)S(1)} %bitcast.18, f32[128,128]{1,0:T(8,128)S(1)} %bitcast.16), custom_call_target="tpu_custom_call" | custom-call | flops 1000000000 | bytes 2000000 | tf_op jit(solution)/shard_map/begin/pallas_call | solution.py:159
  72.4 0.5 collective-permute-done.6.other_ref
  72.9 14.5 %scan.1 = (f32[4096,128]{1,0:T(8,128)S(1)}, f32[128,128]{1,0:T(8,128)}, f32[128,128]{1,0:T(8,128)S(1)}, f32[128,128]{1,0:T(8,128)S(1)}, f32[128,128]{1,0:T(8,128)S(1)}) custom-call(s32[1]{0:T(128)} %bitcast.core_ref, s32[1]{0:T(128)} %bitcast.1.place_ref, f32[16,136,128]{2,1,0:T(8,128)S(1)} %all_to_all.11.own_ref, ...), custom_call_target="tpu_custom_call" | custom-call | flops 10000000000 | bytes 5000000 | tf_op jit(solution)/shard_map/scan/pallas_call | solution.py:297
  87.4 1.0 %convolution_bitcast_fusion.cross_ref = f32[256,128]{1,0:T(8,128)S(1)} fusion(bf16[4096,256]{1,0:T(8,128)(2,1)S(1)} %copy-done.3, f32[4096,128]{1,0:T(8,128)S(1)} %get-tuple-element.40), kind=kOutput, calls=%fused_computation | convolution fusion | flops 268959744 | bytes 4325376 | tf_op jit(solution)/shard_map/ts,tk->sk/dot_general | solution.py:446
  88.4 4.1 %inverse.1 = (f32[256,128]{1,0:T(8,128)}, f32[128,128]{1,0:T(8,128)}) custom-call(f32[128,128]{1,0:T(8,128)S(1)} %get-tuple-element.37.total_ref, f32[128,128]{1,0:T(8,128)S(1)} %get-tuple-element.38.previous_ref, f32[128,128]{1,0:T(8,128)S(1)} %get-tuple-element.39.lagged_ref, f32[256,128]{1,0:T(8,128)S(1)} %convolution_bitcast_fusion.cross_ref), custom_call_target="tpu_custom_call" | custom-call | flops 1000000000 | bytes 600000 | tf_op jit(solution)/shard_map/inverse/pallas_call | solution.py:381
  (22 shorter events, 0.1 us)
Async XLA Ops:
  0.6 1.7 %copy-start.4 = (f32[256,128]{1,0:T(8,128)S(1)}, f32[256,128]{1,0:T(8,128)}, u32[]{:S(2)}) copy-start(f32[256,128]{1,0:T(8,128)} %param.8) | copy-start | bytes 393220
  0.6 1.7 %copy-start.8 = (f32[256]{0:T(256)S(1)}, f32[256]{0:T(256)}, u32[]{:S(2)}) copy-start(f32[256]{0:T(256)} %param.9) | copy-start | bytes 3076
  2.9 5.7 %collective-permute-start.1 = (f32[2048,128]{1,0:T(8,128)S(1)}, f32[2048,128]{1,0:T(8,128)S(1)}, u32[]{:S(2)}, u32[]{:S(2)}) collective-permute-start(f32[2048,128]{1,0:T(8,128)S(1)} %fusion.5), channel_id=1, source_target_pairs={{0,8},{8,0},{1,9},{9,1},{2,10},{10,2},{3,11},{11,3},{4,12},{12,4},... | collective-permute-start | bytes 3145736 | tf_op jit(solution)/shard_map/ppermute | solution.py:394
  6.7 1.9 %collective-permute-start = (f32[128,128]{1,0:T(8,128)S(1)}, f32[128,128]{1,0:T(8,128)S(1)}, u32[]{:S(2)}, u32[]{:S(2)}) collective-permute-start(f32[128,128]{1,0:T(8,128)S(1)} %fusion.1), channel_id=1, source_target_pairs={{0,8},{8,0},{1,9},{9,1},{2,10},{10,2},{3,11},{11,3},{4,12},{12,4},... | collective-permute-start | bytes 196616 | tf_op jit(solution)/shard_map/ppermute | solution.py:394
  8.9 23.8 %copy-start.5 = (f32[128,128]{1,0:T(8,128)S(1)}, f32[128,128]{1,0:T(8,128)}, u32[]{:S(2)}) copy-start(f32[128,128]{1,0:T(8,128)} %param.10) | copy-start | bytes 196612
  8.9 23.9 %copy-start.6 = (f32[128,128]{1,0:T(8,128)S(1)}, f32[128,128]{1,0:T(8,128)}, u32[]{:S(2)}) copy-start(f32[128,128]{1,0:T(8,128)} %param.11) | copy-start | bytes 196612
  8.9 24.0 %copy-start.7 = (f32[128,128]{1,0:T(8,128)S(1)}, f32[128,128]{1,0:T(8,128)}, u32[]{:S(2)}) copy-start(f32[128,128]{1,0:T(8,128)} %param.12) | copy-start | bytes 196612
  30.9 12.7 %copy-start = (f32[128,128]{1,0:T(8,128)S(1)}, f32[128,128]{1,0:T(8,128)}, u32[]{:S(2)}) copy-start(f32[128,128]{1,0:T(8,128)} %cov_ref.3) | copy-start | bytes 196612
  31.0 3.4 %collective-permute-start.2 = (f32[136,128]{1,0:T(8,128)S(1)}, f32[136,128]{1,0:T(8,128)S(1)}, u32[]{:S(2)}, u32[]{:S(2)}) collective-permute-start(f32[136,128]{1,0:T(8,128)S(1)} %reduce_sum.9), channel_id=1, source_target_pairs={{0,1},{1,0},{2,3},{3,2},{4,5},{5,4},{6,7},{7,6},{8,9},{9,8},{10,11... | collective-permute-start | bytes 208904 | tf_op jit(solution)/shard_map/ppermute | solution.py:399
  34.4 11.9 %collective-permute-start.5 = (f32[136,128]{1,0:T(8,128)S(1)}, f32[136,128]{1,0:T(8,128)S(1)}, u32[]{:S(2)}, u32[]{:S(2)}) collective-permute-start(f32[136,128]{1,0:T(8,128)S(1)} %add.36), channel_id=1, source_target_pairs={{0,6},{1,7},{2,0},{3,1},{4,2},{5,3},{6,4},{7,5},{8,14},{9,15},{10,... | collective-permute-start | bytes 208904 | tf_op jit(solution)/shard_map/ppermute | solution.py:394
  40.3 7.3 %collective-permute-start.4 = (f32[136,128]{1,0:T(8,128)S(1)}, f32[136,128]{1,0:T(8,128)S(1)}, u32[]{:S(2)}, u32[]{:S(2)}) collective-permute-start(f32[136,128]{1,0:T(8,128)S(1)} %add.36), channel_id=1, source_target_pairs={{0,4},{1,5},{2,6},{3,7},{4,0},{5,1},{6,2},{7,3},{8,12},{9,13},{10,... | collective-permute-start | bytes 208904 | tf_op jit(solution)/shard_map/ppermute | solution.py:394
  41.3 7.0 %collective-permute-start.3 = (f32[136,128]{1,0:T(8,128)S(1)}, f32[136,128]{1,0:T(8,128)S(1)}, u32[]{:S(2)}, u32[]{:S(2)}) collective-permute-start(f32[136,128]{1,0:T(8,128)S(1)} %add.36), channel_id=1, source_target_pairs={{0,2},{1,3},{2,4},{3,5},{4,6},{5,7},{6,0},{7,1},{8,10},{9,11},{10,... | collective-permute-start | bytes 208904 | tf_op jit(solution)/shard_map/ppermute | solution.py:394
  46.3 19.3 %copy-start.1 = (bf16[20,128,256]{2,1,0:T(8,128)(2,1)}, bf16[20,128,256]{2,1,0:T(8,128)(2,1)S(1)}, u32[]{:S(2)}) copy-start(bf16[20,128,256]{2,1,0:T(8,128)(2,1)S(1)} %get-tuple-element.33.both_ref) | copy-start | bytes 3932164
  65.6 7.3 %collective-permute-start.6 = (f32[16,136,128]{2,1,0:T(8,128)S(1)}, f32[16,136,128]{2,1,0:T(8,128)S(1)}, u32[]{:S(2)}, u32[]{:S(2)}) collective-permute-start(f32[16,136,128]{2,1,0:T(8,128)S(1)} %all_to_all.11.own_ref), channel_id=1, source_target_pairs={{0,8},{8,0},{1,9},{9,1},{2,10},{10,2},{3,11},{11,3},{4,12},{12,4},... | collective-permute-start | bytes 3342344 | tf_op jit(solution)/shard_map/ppermute | solution.py:394
  70.5 2.4 %copy-start.2 = (bf16[20,128,256]{2,1,0:T(8,128)(2,1)S(1)}, bf16[20,128,256]{2,1,0:T(8,128)(2,1)}, u32[]{:S(2)}) copy-start(bf16[20,128,256]{2,1,0:T(8,128)(2,1)} %copy-done.1) | copy-start | bytes 3932164
  72.9 14.5 %copy-start.3 = (bf16[4096,256]{1,0:T(8,128)(2,1)S(1)}, bf16[4096,256]{1,0:T(8,128)(2,1)}, u32[]{:S(2)}) copy-start(bf16[4096,256]{1,0:T(8,128)(2,1)} %param.7) | copy-start | bytes 6291460

commit v9 on v8

--- a/solution.py
+++ b/solution.py
@@ -12,7 +12,7 @@
 
 STEPS = 8
 SQUARINGS = 7
-LEAPS = 4
+LEAPS = 8
 FIRST = 4
 f32 = jnp.float32
 bf16 = jnp.bfloat16

time: 92.7 us -> 92.6 us (level)
  transfers between devices with their start and end apart: 7 -> 7, of which waited for: 5 -> 4; matrix products, arithmetic and copies ran while one was open for 1% -> 1% of each run, Pallas kernels for 5% -> 6%
where the time goes in v9:
time: 92.6 us; the launch traced here: 92.4 us
  blocking collectives  39.2 us (42%)
  Pallas kernels  23.5 us (25%)
  starting transfers between devices  19.3 us (21%)
  waiting for transfers between devices  4.8 us (5%)
  matrix products  2.24 us (2%)
  local copies, waits for them, and re-layouts  2.1 us (2%)
    all_to_all x1, blocking collectives, local(): lax.all_to_all(pieces, (Y, X), split_axis=0, concat_axis=0, tiled=True)  22 us
    ppermute x6, starting transfers between devices, turned(): lax.ppermute(value, axis, [(i, (i + steps) % count) for i in range(count)])  17.5 us
    all_to_all x1, blocking collectives, local(): lax.all_to_all(copies, (Y, X), split_axis=0, concat_axis=0, tiled=True)  17.2 us
    pallas_call x1, Pallas kernels, scanned(): pl.pallas_call(scan_kernel, out_shape=(jax.ShapeDtypeStruct((length, n),...  13.9 us
    pallas_call x1, Pallas kernels, inverted(): pl.pallas_call(inverse_kernel, out_shape=(jax.ShapeDtypeStruct(cross.shap...  4.15 us
    ppermute x6, waiting for transfers between devices, turned(): lax.ppermute(value, axis, [(i, (i + steps) % count) for i in range(count)])  3.41 us
    pallas_call x1, Pallas kernels, begun(): pl.pallas_call(begin_kernel, out_shape=jax.ShapeDtypeStruct((STEPS + LEAP...  2.71 us
    pallas_call x1, Pallas kernels, readied(): pl.pallas_call(ready_kernel, out_shape=(jax.ShapeDtypeStruct((count, n, 2...  2.69 us
  transfers between devices with their start and end apart: 7, of which 4 were waited for; matrix products, arithmetic and copies ran while one was open for 1% of the time, Pallas kernels for 6%

profile of v9, /device:TPU:1, one launch (start us, length us, event | category | flops | bytes accessed | tf_op | source)
XLA Modules:
  0.0 92.4 jit_solution(8904745320604196199)
XLA Ops:
  0.7 1.7 %constant_dynamic-slice_fusion = (bf16[2048,256]{1,0:T(8,128)(2,1)S(1)}, bf16[2048,256]{1,0:T(8,128)(2,1)S(1)}) fusion(bf16[4096,256]{1,0:T(8,128)(2,1)} %param.7, s32[]{:T(128)S(6)} %select_n.7, s32[]{:T(128)S(6)} %select_n.6), kind=kLoop, calls=%fused_computation.8 | loop fusion | bytes 4194312 | tf_op jit(solution)/shard_map/dynamic_slice | solution.py:418
  2.4 0.1 multiply_convert_fusion
  2.5 0.4 fusion.5
  2.9 3.3 %collective-permute-start.1 = (f32[2048,128]{1,0:T(8,128)S(1)}, f32[2048,128]{1,0:T(8,128)S(1)}, u32[]{:S(2)}, u32[]{:S(2)}) collective-permute-start(f32[2048,128]{1,0:T(8,128)S(1)} %fusion.5), channel_id=1, source_target_pairs={{0,8},{8,0},{1,9},{9,1},{2,10},{10,2},{3,11},{11,3},{4,12},{12,4},... | collective-permute-start | bytes 3145736 | tf_op jit(solution)/shard_map/ppermute | solution.py:394
  6.3 0.4 fusion.1
  6.7 0.1 collective-permute-start
  6.8 0.4 fusion.4
  7.2 1.4 %collective-permute-done = f32[128,128]{1,0:T(8,128)S(1)} collective-permute-done((f32[128,128]{1,0:T(8,128)S(1)}, f32[128,128]{1,0:T(8,128)S(1)}, u32[]{:S(2)}, u32[]{:S(2)}) %collective-permute-start) | collective-permute-done | bytes 65568 | tf_op jit(solution)/shard_map/ppermute | solution.py:394
  8.7 0.1 add.35
  8.8 0.1 pad_maximum_fusion
  8.9 0.0 copy-start.6
  8.9 0.0 copy-start.7
  8.9 22.0 %all_to_all.10 = f32[16,136,128]{2,1,0:T(8,128)S(1)} all-to-all(f32[16,136,128]{2,1,0:T(8,128)S(1)} %pad_maximum_fusion), channel_id=1, replica_groups=mesh['tm_0'=4,'tm_1'=4,'tm_2'=2,'sr'=8] {'tm_0','tm_1'}, dimensions={0} | all-to-all | bytes 2228224 | tf_op jit(solution)/shard_map/all_to_all | solution.py:434
  30.9 0.1 reduce_sum.9
  31.0 1.7 %collective-permute-start.2 = (f32[136,128]{1,0:T(8,128)S(1)}, f32[136,128]{1,0:T(8,128)S(1)}, u32[]{:S(2)}, u32[]{:S(2)}) collective-permute-start(f32[136,128]{1,0:T(8,128)S(1)} %reduce_sum.9), channel_id=1, source_target_pairs={{0,1},{1,0},{2,3},{3,2},{4,5},{5,4},{6,7},{7,6},{8,9},{9,8},{10,11... | collective-permute-start | bytes 208904 | tf_op jit(solution)/shard_map/ppermute | solution.py:399
  32.7 0.1 copy.10
  32.8 0.1 copy.11
  32.9 0.1 copy.12
  33.0 1.4 %collective-permute-done.2 = f32[136,128]{1,0:T(8,128)S(1)} collective-permute-done((f32[136,128]{1,0:T(8,128)S(1)}, f32[136,128]{1,0:T(8,128)S(1)}, u32[]{:S(2)}, u32[]{:S(2)}) %collective-permute-start.2) | collective-permute-done | bytes 69664 | tf_op jit(solution)/shard_map/ppermute | solution.py:399
  34.4 5.9 %collective-permute-start.5 = (f32[136,128]{1,0:T(8,128)S(1)}, f32[136,128]{1,0:T(8,128)S(1)}, u32[]{:S(2)}, u32[]{:S(2)}) collective-permute-start(f32[136,128]{1,0:T(8,128)S(1)} %add.36), channel_id=1, source_target_pairs={{0,6},{1,7},{2,0},{3,1},{4,2},{5,3},{6,4},{7,5},{8,14},{9,15},{10,... | collective-permute-start | bytes 208904 | tf_op jit(solution)/shard_map/ppermute | solution.py:394
  40.3 1.0 %collective-permute-start.4 = (f32[136,128]{1,0:T(8,128)S(1)}, f32[136,128]{1,0:T(8,128)S(1)}, u32[]{:S(2)}, u32[]{:S(2)}) collective-permute-start(f32[136,128]{1,0:T(8,128)S(1)} %add.36), channel_id=1, source_target_pairs={{0,4},{1,5},{2,6},{3,7},{4,0},{5,1},{6,2},{7,3},{8,12},{9,13},{10,... | collective-permute-start | bytes 208904 | tf_op jit(solution)/shard_map/ppermute | solution.py:394
  41.3 2.3 %collective-permute-start.3 = (f32[136,128]{1,0:T(8,128)S(1)}, f32[136,128]{1,0:T(8,128)S(1)}, u32[]{:S(2)}, u32[]{:S(2)}) collective-permute-start(f32[136,128]{1,0:T(8,128)S(1)} %add.36), channel_id=1, source_target_pairs={{0,2},{1,3},{2,4},{3,5},{4,6},{5,7},{6,0},{7,1},{8,10},{9,11},{10,... | collective-permute-start | bytes 208904 | tf_op jit(solution)/shard_map/ppermute | solution.py:394
  43.6 2.7 %ready.1 = (bf16[20,128,256]{2,1,0:T(8,128)(2,1)S(1)}, bf16[20,128,128]{2,1,0:T(8,128)(2,1)S(1)}, f32[128,128]{1,0:T(8,128)S(1)}) custom-call(f32[128,128]{1,0:T(8,128)S(1)} %bitcast.15, f32[128,128]{1,0:T(8,128)S(1)} %bitcast.17, f32[128,128]{1,0:T(8,128)S(1)} %bitcast.19, f32[128,128]{1,0:T(8,128)S(1)} %copy-done), custom_call_target="tpu_custom_call" | custom-call | flops 1000000000 | bytes 2000000 | tf_op jit(solution)/shard_map/ready/pallas_call | solution.py:127
  46.3 1.3 %collective-permute-done.4 = f32[136,128]{1,0:T(8,128)S(1)} collective-permute-done((f32[136,128]{1,0:T(8,128)S(1)}, f32[136,128]{1,0:T(8,128)S(1)}, u32[]{:S(2)}, u32[]{:S(2)}) %collective-permute-start.4) | collective-permute-done | bytes 69664 | tf_op jit(solution)/shard_map/ppermute | solution.py:394
  47.6 0.7 collective-permute-done.3
  48.3 0.1 broadcast_in_dim.12
  48.4 17.2 %all_to_all.11.own_ref = f32[16,136,128]{2,1,0:T(8,128)S(1)} all-to-all(f32[16,136,128]{2,1,0:T(8,128)S(1)} %broadcast_in_dim.12), channel_id=1, replica_groups=mesh['tm_0'=4,'tm_1'=4,'tm_2'=2,'sr'=8] {'tm_0','tm_1'}, dimensions={0} | all-to-all | bytes 2228224 | tf_op jit(solution)/shard_map/all_to_all | solution.py:439
  65.6 4.9 %collective-permute-start.6 = (f32[16,136,128]{2,1,0:T(8,128)S(1)}, f32[16,136,128]{2,1,0:T(8,128)S(1)}, u32[]{:S(2)}, u32[]{:S(2)}) collective-permute-start(f32[16,136,128]{2,1,0:T(8,128)S(1)} %all_to_all.11.own_ref), channel_id=1, source_target_pairs={{0,8},{8,0},{1,9},{9,1},{2,10},{10,2},{3,11},{11,3},{4,12},{12,4},... | collective-permute-start | bytes 3342344 | tf_op jit(solution)/shard_map/ppermute | solution.py:394
  70.5 2.7 %begin.1.power_ref = f32[15,128,128]{2,1,0:T(8,128)S(1)} custom-call(f32[16,136,128]{2,1,0:T(8,128)S(1)} %all_to_all.11.own_ref, f32[128,128]{1,0:T(8,128)S(1)} %bitcast.18, f32[128,128]{1,0:T(8,128)S(1)} %bitcast.16), custom_call_target="tpu_custom_call" | custom-call | flops 1000000000 | bytes 2000000 | tf_op jit(solution)/shard_map/begin/pallas_call | solution.py:159
  73.3 13.9 %scan.1 = (f32[4096,128]{1,0:T(8,128)S(1)}, f32[128,128]{1,0:T(8,128)}, f32[128,128]{1,0:T(8,128)S(1)}, f32[128,128]{1,0:T(8,128)S(1)}, f32[128,128]{1,0:T(8,128)S(1)}) custom-call(s32[1]{0:T(128)} %bitcast.core_ref, s32[1]{0:T(128)} %bitcast.1.place_ref, f32[16,136,128]{2,1,0:T(8,128)S(1)} %all_to_all.11.own_ref, ...), custom_call_target="tpu_custom_call" | custom-call | flops 10000000000 | bytes 5000000 | tf_op jit(solution)/shard_map/scan/pallas_call | solution.py:297
  87.3 1.0 %convolution_bitcast_fusion.cross_ref = f32[256,128]{1,0:T(8,128)S(1)} fusion(bf16[4096,256]{1,0:T(8,128)(2,1)S(1)} %copy-done.3, f32[4096,128]{1,0:T(8,128)S(1)} %get-tuple-element.40), kind=kOutput, calls=%fused_computation | convolution fusion | flops 268959744 | bytes 4325376 | tf_op jit(solution)/shard_map/ts,tk->sk/dot_general | solution.py:446
  88.2 4.1 %inverse.1 = (f32[256,128]{1,0:T(8,128)}, f32[128,128]{1,0:T(8,128)}) custom-call(f32[128,128]{1,0:T(8,128)S(1)} %get-tuple-element.37.total_ref, f32[128,128]{1,0:T(8,128)S(1)} %get-tuple-element.38.previous_ref, f32[128,128]{1,0:T(8,128)S(1)} %get-tuple-element.39.lagged_ref, f32[256,128]{1,0:T(8,128)S(1)} %convolution_bitcast_fusion.cross_ref), custom_call_target="tpu_custom_call" | custom-call | flops 1000000000 | bytes 600000 | tf_op jit(solution)/shard_map/inverse/pallas_call | solution.py:381
  (22 shorter events, 0.1 us)
Async XLA Ops:
  0.6 1.7 %copy-start.4 = (f32[256,128]{1,0:T(8,128)S(1)}, f32[256,128]{1,0:T(8,128)}, u32[]{:S(2)}) copy-start(f32[256,128]{1,0:T(8,128)} %param.8) | copy-start | bytes 393220
  0.6 1.7 %copy-start.8 = (f32[256]{0:T(256)S(1)}, f32[256]{0:T(256)}, u32[]{:S(2)}) copy-start(f32[256]{0:T(256)} %param.9) | copy-start | bytes 3076
  2.9 5.7 %collective-permute-start.1 = (f32[2048,128]{1,0:T(8,128)S(1)}, f32[2048,128]{1,0:T(8,128)S(1)}, u32[]{:S(2)}, u32[]{:S(2)}) collective-permute-start(f32[2048,128]{1,0:T(8,128)S(1)} %fusion.5), channel_id=1, source_target_pairs={{0,8},{8,0},{1,9},{9,1},{2,10},{10,2},{3,11},{11,3},{4,12},{12,4},... | collective-permute-start | bytes 3145736 | tf_op jit(solution)/shard_map/ppermute | solution.py:394
  6.7 1.9 %collective-permute-start = (f32[128,128]{1,0:T(8,128)S(1)}, f32[128,128]{1,0:T(8,128)S(1)}, u32[]{:S(2)}, u32[]{:S(2)}) collective-permute-start(f32[128,128]{1,0:T(8,128)S(1)} %fusion.1), channel_id=1, source_target_pairs={{0,8},{8,0},{1,9},{9,1},{2,10},{10,2},{3,11},{11,3},{4,12},{12,4},... | collective-permute-start | bytes 196616 | tf_op jit(solution)/shard_map/ppermute | solution.py:394
  8.9 23.8 %copy-start.5 = (f32[128,128]{1,0:T(8,128)S(1)}, f32[128,128]{1,0:T(8,128)}, u32[]{:S(2)}) copy-start(f32[128,128]{1,0:T(8,128)} %param.10) | copy-start | bytes 196612
  8.9 23.9 %copy-start.6 = (f32[128,128]{1,0:T(8,128)S(1)}, f32[128,128]{1,0:T(8,128)}, u32[]{:S(2)}) copy-start(f32[128,128]{1,0:T(8,128)} %param.11) | copy-start | bytes 196612
  8.9 24.0 %copy-start.7 = (f32[128,128]{1,0:T(8,128)S(1)}, f32[128,128]{1,0:T(8,128)}, u32[]{:S(2)}) copy-start(f32[128,128]{1,0:T(8,128)} %param.12) | copy-start | bytes 196612
  30.9 12.7 %copy-start = (f32[128,128]{1,0:T(8,128)S(1)}, f32[128,128]{1,0:T(8,128)}, u32[]{:S(2)}) copy-start(f32[128,128]{1,0:T(8,128)} %cov_ref.3) | copy-start | bytes 196612
  31.0 3.4 %collective-permute-start.2 = (f32[136,128]{1,0:T(8,128)S(1)}, f32[136,128]{1,0:T(8,128)S(1)}, u32[]{:S(2)}, u32[]{:S(2)}) collective-permute-start(f32[136,128]{1,0:T(8,128)S(1)} %reduce_sum.9), channel_id=1, source_target_pairs={{0,1},{1,0},{2,3},{3,2},{4,5},{5,4},{6,7},{7,6},{8,9},{9,8},{10,11... | collective-permute-start | bytes 208904 | tf_op jit(solution)/shard_map/ppermute | solution.py:399
  34.4 11.9 %collective-permute-start.5 = (f32[136,128]{1,0:T(8,128)S(1)}, f32[136,128]{1,0:T(8,128)S(1)}, u32[]{:S(2)}, u32[]{:S(2)}) collective-permute-start(f32[136,128]{1,0:T(8,128)S(1)} %add.36), channel_id=1, source_target_pairs={{0,6},{1,7},{2,0},{3,1},{4,2},{5,3},{6,4},{7,5},{8,14},{9,15},{10,... | collective-permute-start | bytes 208904 | tf_op jit(solution)/shard_map/ppermute | solution.py:394
  40.3 7.3 %collective-permute-start.4 = (f32[136,128]{1,0:T(8,128)S(1)}, f32[136,128]{1,0:T(8,128)S(1)}, u32[]{:S(2)}, u32[]{:S(2)}) collective-permute-start(f32[136,128]{1,0:T(8,128)S(1)} %add.36), channel_id=1, source_target_pairs={{0,4},{1,5},{2,6},{3,7},{4,0},{5,1},{6,2},{7,3},{8,12},{9,13},{10,... | collective-permute-start | bytes 208904 | tf_op jit(solution)/shard_map/ppermute | solution.py:394
  41.3 7.0 %collective-permute-start.3 = (f32[136,128]{1,0:T(8,128)S(1)}, f32[136,128]{1,0:T(8,128)S(1)}, u32[]{:S(2)}, u32[]{:S(2)}) collective-permute-start(f32[136,128]{1,0:T(8,128)S(1)} %add.36), channel_id=1, source_target_pairs={{0,2},{1,3},{2,4},{3,5},{4,6},{5,7},{6,0},{7,1},{8,10},{9,11},{10,... | collective-permute-start | bytes 208904 | tf_op jit(solution)/shard_map/ppermute | solution.py:394
  46.3 19.3 %copy-start.1 = (bf16[20,128,256]{2,1,0:T(8,128)(2,1)}, bf16[20,128,256]{2,1,0:T(8,128)(2,1)S(1)}, u32[]{:S(2)}) copy-start(bf16[20,128,256]{2,1,0:T(8,128)(2,1)S(1)} %get-tuple-element.33.both_ref) | copy-start | bytes 3932164
  65.6 7.7 %collective-permute-start.6 = (f32[16,136,128]{2,1,0:T(8,128)S(1)}, f32[16,136,128]{2,1,0:T(8,128)S(1)}, u32[]{:S(2)}, u32[]{:S(2)}) collective-permute-start(f32[16,136,128]{2,1,0:T(8,128)S(1)} %all_to_all.11.own_ref), channel_id=1, source_target_pairs={{0,8},{8,0},{1,9},{9,1},{2,10},{10,2},{3,11},{11,3},{4,12},{12,4},... | collective-permute-start | bytes 3342344 | tf_op jit(solution)/shard_map/ppermute | solution.py:394
  70.5 2.7 %copy-start.2 = (bf16[20,128,256]{2,1,0:T(8,128)(2,1)S(1)}, bf16[20,128,256]{2,1,0:T(8,128)(2,1)}, u32[]{:S(2)}) copy-start(bf16[20,128,256]{2,1,0:T(8,128)(2,1)} %copy-done.1) | copy-start | bytes 3932164
  73.3 14.0 %copy-start.3 = (bf16[4096,256]{1,0:T(8,128)(2,1)S(1)}, bf16[4096,256]{1,0:T(8,128)(2,1)}, u32[]{:S(2)}) copy-start(bf16[4096,256]{1,0:T(8,128)(2,1)} %param.7) | copy-start | bytes 6291460
